TPU v7x, 128 devices: a whole 4x4x4 slice. The times are simulated.
128 devices in a mesh: gx: 4 (over x), gy: 4 (over y), gz: 8 (over z, core).
Axes of the slice: x: 4, y: 4, z: 4, core: 2. Of those that a mesh axis runs over, the one named last changes fastest.
Arguments:
- scalar_field: float32 [64, 384, 2048], P('gx', 'gy', 'gz'), may hold values from -6 to 6
- velocity: bfloat16 [3, 64, 384, 2048], P(None, 'gx', 'gy', 'gz'), may hold values from -12 to 12
Outputs:
- updated: float32 [64, 384, 2048], P('gx', 'gy', 'gz')
All inputs are finite; a program needn't handle non-finite values.
Results may differ from a plain program's by a relative error of at most 0.0003.
Values sent between devices are 32-bit elements; how exact they have to be, the bound alone decides.
No kernel may reach another device: no remote copies, remote signals or barrier semaphores. Data moves between devices by JAX's collectives and lax.ppermute only.
A program may use at most 128 MiB of HBM per device.

v0:
```python
import functools

import jax
import jax.numpy as jnp
import numpy as np
from jax import lax
from jax.experimental import pallas as pl
from jax.experimental.pallas import tpu as pltpu
from jax.sharding import PartitionSpec as P

DT = 0.002
NU_BASE = 0.3
SGS_COEF = 0.01
FILTER_STRENGTH = 0.3
GLL_POINTS = [
    -1.0,
    -0.8717401485096066,
    -0.5917001814331423,
    -0.2092992179024789,
    0.2092992179024789,
    0.5917001814331423,
    0.8717401485096066,
    1.0,
]
BF = jnp.bfloat16
F32 = jnp.float32
VM = pl.BlockSpec(memory_space=pltpu.VMEM)


def legendre_all(point):
    values_list = [1.0, point]
    for order in range(1, 7):
        values_list.append(
            ((2 * order + 1) * point * values_list[order] - order * values_list[order - 1])
            / (order + 1)
        )
    return values_list


def gll_tables():
    degree = 7
    table = [legendre_all(p) for p in GLL_POINTS]
    top = [table[i][degree] for i in range(8)]
    weights = [2.0 / (degree * (degree + 1) * top[i] * top[i]) for i in range(8)]
    derivative = [[0.0] * 8 for i in range(8)]
    for i in range(8):
        for j in range(8):
            if i != j:
                derivative[i][j] = top[i] / (top[j] * (GLL_POINTS[i] - GLL_POINTS[j]))
    derivative[0][0] = -degree * (degree + 1) / 4.0
    derivative[7][7] = degree * (degree + 1) / 4.0
    damping = [1.0] * 8
    for k in (6, 7):
        damping[k] = 1.0 - FILTER_STRENGTH * ((k - 5) / 2.0) ** 2
    gammas = [2.0 / (2 * k + 1) for k in range(7)] + [2.0 / degree]
    filter_mat = [[0.0] * 8 for i in range(8)]
    for i in range(8):
        for j in range(8):
            total = 0.0
            for k in range(8):
                total += table[i][k] * damping[k] * weights[j] * table[j][k] / gammas[k]
            filter_mat[i][j] = total
    return np.array(derivative), np.array(weights), np.array(filter_mat)


D, WT, FM = gll_tables()
DR = -DT * (D.T * WT[None, :]) / WT[:, None]


def block(mat, length):
    return np.kron(np.eye(length // 8), mat)


def average(length):
    mat = np.eye(length)
    for k in range(8, length, 8):
        mat[k - 1 : k + 1, k - 1 : k + 1] = 0.5
    mat[0, 0] = mat[-1, -1] = 0.5
    return mat


class Line:
    def __init__(self, length):
        avg = average(length)
        filt = block(FM, length)
        self.avg = avg
        self.grad = avg @ block(D, length)
        self.res = block(DR, length)
        self.filt = avg @ filt
        self.both = avg @ filt @ avg
        self.both[0, 0] += 0.25 * FM[7, 7]
        self.both[-1, -1] += 0.25 * FM[0, 0]
        self.face = filt @ avg
        first, last = np.eye(length)[0], np.eye(length)[-1]
        self.halo = np.stack([self.filt[:, 0] * 0.5, 0.5 * first, self.filt[:, -1] * 0.5, 0.5 * last])


def halves(mat):
    mat = np.asarray(mat, np.float64)
    high = mat.astype(jnp.bfloat16)
    low = (mat - high.astype(np.float64)).astype(jnp.bfloat16)
    return high, low


def on_right(mat):
    high, low = halves(mat)
    return jnp.asarray(np.concatenate([high, high, low], axis=0))


def on_left(mat):
    high, low = halves(mat)
    return jnp.asarray(np.concatenate([high, high, low], axis=1))


def exact_right(mat):
    mat = np.asarray(mat).astype(jnp.bfloat16)
    return jnp.asarray(np.concatenate([mat, mat], axis=0))


def exact_left(mat):
    mat = np.asarray(mat).astype(jnp.bfloat16)
    return jnp.asarray(np.concatenate([mat, mat], axis=1))


def split(val):
    high = val.astype(BF)
    return high, (val - high.astype(F32)).astype(BF)


def mm(a, b):
    return jnp.dot(a, b, preferred_element_type=F32)


def right(pair, mat):
    return mm(jnp.concatenate([pair[0], pair[1], pair[0]], axis=1), mat)


def right_exact(pair, mat):
    return mm(jnp.concatenate(pair, axis=1), mat)


def left(mat, pair):
    return mm(mat, jnp.concatenate([pair[0], pair[1], pair[0]], axis=0))


def left_exact(mat, pair):
    return mm(mat, jnp.concatenate(pair, axis=0))


def call(kernel, outs, *args, scratch=(), flops=0, nbytes=0, name=None, hbm=(), hbm_out=False, smem=()):
    single = not isinstance(outs, list)
    shapes = [jax.ShapeDtypeStruct(o, F32) for o in ([outs] if single else outs)]
    kinds = {i: pl.BlockSpec(memory_space=pl.ANY) for i in hbm}
    kinds.update({i: pl.BlockSpec(memory_space=pltpu.SMEM) for i in smem})
    res = pl.pallas_call(
        kernel,
        out_shape=shapes,
        in_specs=[kinds.get(i, VM) for i in range(len(args))],
        out_specs=[pl.BlockSpec(memory_space=pl.ANY) if hbm_out else VM] * len(shapes),
        scratch_shapes=list(scratch),
        compiler_params=pltpu.CompilerParams(vmem_limit_bytes=20 << 20),
        cost_estimate=pl.CostEstimate(flops=flops, bytes_accessed=nbytes, transcendentals=0),
        name=name,
    )(*args)
    return res[0] if single else res


NXL, NYL, NZL = 16, 96, 256
ROWS = NXL * NYL
TILES = NYL // 8


LX, LY, LZ = Line(NXL), Line(NYL), Line(NZL)


def face_x_kernel(u_hbm, u_ref, lo_ref, hi_ref, sems):
    copies = []
    for c in range(4):
        rows = slice(c * 24, c * 24 + 24)
        for s in range(2):
            xs = slice(8 * s, 8 * s + 8)
            copies.append(
                pltpu.make_async_copy(u_hbm.at[xs, rows, :], u_ref.at[xs, rows, :], sems.at[2 * c + s])
            )
    for copy in copies:
        copy.start()
    for c in range(4):
        copies[2 * c].wait()
        copies[2 * c + 1].wait()
        for t in range(3):
            rows = slice(c * 24 + t * 8, c * 24 + t * 8 + 8)
            nodes = [u_ref[k, rows, :] for k in range(NXL)]
            lo_ref[0, rows, :] = 0.5 * nodes[0]
            lo_ref[1, rows, :] = sum(float(0.5 * D[0, j]) * nodes[j] for j in range(8))
            hi_ref[0, rows, :] = 0.5 * nodes[15]
            hi_ref[1, rows, :] = sum(float(0.5 * D[7, j]) * nodes[8 + j] for j in range(8))


def even_odd(mat, nodes, sign):
    even = [nodes[j] + nodes[7 - j] for j in range(4)]
    odd = [nodes[j] - nodes[7 - j] for j in range(4)]
    out = [None] * 8
    for i in range(4):
        a = sum(float(0.5 * (mat[i, j] + mat[i, 7 - j])) * even[j] for j in range(4))
        b = sum(float(0.5 * (mat[i, j] - mat[i, 7 - j])) * odd[j] for j in range(4))
        out[i] = a + b
        out[7 - i] = (a - b) if sign > 0 else (b - a)
    return out


def average_x(vals):
    vals = list(vals)
    mid = 0.5 * (vals[7] + vals[8])
    vals[7] = vals[8] = mid
    vals[0] = 0.5 * vals[0]
    vals[15] = 0.5 * vals[15]
    return vals


def lane_iota(rows):
    return lax.broadcasted_iota(jnp.int32, (rows, 128), 1)


def pack_columns(fields, x, lane):
    total = None
    for q, field in enumerate(fields):
        ends = jnp.where(lane == 127, field[:, 128:256], field[:, 0:128])
        pos = 2 * (16 * q + x)
        rolled = pltpu.roll(ends, (pos - 127) % 128, 1)
        piece = jnp.where((lane == pos) | (lane == pos + 1), rolled, 0.0)
        total = piece if total is None else total + piece
    return total


def received(par_ref, near_ref, far_ref):
    first = par_ref[0, 0] == 0
    near, far = near_ref[...], far_ref[...]
    return jnp.where(first, far, near), jnp.where(first, near, far)


def halo_columns(par_ref, near_ref, far_ref):
    low, high = received(par_ref, near_ref, far_ref)
    return jnp.where((lane_iota(NYL) % 2) == 0, low, pltpu.roll(high, 126, 1))


def local_z_kernel(u_ref, sz_ref, dz_ref, fz_ref, z1, z2, z3, z4, cols):
    lane = lane_iota(16)
    for t in range(NYL // 16):
        rows = slice(t * 16, t * 16 + 16)
        nodes = [u_ref[k, rows, :] for k in range(NXL)]
        grads = even_odd(D, nodes[:8], -1) + even_odd(D, nodes[8:], -1)
        flat = lambda vals: jnp.concatenate(vals, axis=0)
        p = split(flat(average_x(nodes)))
        g = split(flat(average_x(grads)))
        outs = [
            right_exact(p, sz_ref[...]),
            right(p, dz_ref[...]),
            right_exact(g, sz_ref[...]),
            right(split(flat(nodes)), fz_ref[...]),
        ]
        acc = None
        for k in range(NXL):
            vals = [o[16 * k : 16 * k + 16] for o in outs]
            for ref, val in zip((z1, z2, z3, z4), vals):
                ref[k, rows, :] = val
            piece = pack_columns(vals, k, lane)
            acc = piece if acc is None else acc + piece
        cols[rows, :] = acc


def face_z_kernel(lo_ref, hi_ref, cols_ref, sz_ref, dz_ref, dlt, cols):
    p = split(jnp.concatenate([lo_ref[0], hi_ref[0]], axis=0))
    g = split(jnp.concatenate([lo_ref[1], hi_ref[1]], axis=0))
    outs = [right_exact(p, sz_ref[...]), right(p, dz_ref[...]), right_exact(g, sz_ref[...])]
    lane = lane_iota(NYL)
    acc = cols_ref[...]
    for s, x in ((0, 0), (1, NXL - 1)):
        vals = [o[s * NYL : (s + 1) * NYL] for o in outs]
        for q in range(3):
            dlt[s, q] = vals[q]
        acc = acc + pack_columns(vals, x, lane)
    cols[...] = acc


def local_y_kernel(z1, z2, z3, dlt, sy_ref, dy_ref, sx_, sy_, sz_):
    for x in range(NXL):
        vals = [z1[x], z2[x], z3[x]]
        if x in (0, NXL - 1):
            vals = [v + dlt[0 if x == 0 else 1, q] for q, v in enumerate(vals)]
        sy_[x] = left(dy_ref[...], split(vals[0]))
        sz_[x] = left_exact(sy_ref[...], split(vals[1]))
        sx_[x] = left_exact(sy_ref[...], split(vals[2]))


def row_sum(vals, coefs):
    row = lax.broadcasted_iota(jnp.int32, vals.shape, 0)
    weight = jnp.zeros(vals.shape, F32)
    for k, c in enumerate(coefs):
        weight = jnp.where(row == k, float(c), weight)
    return jnp.sum(vals * weight, axis=0, keepdims=True)


def eddy(sx, sy, sz):
    mag = 1.0 + sx * sx + sy * sy + sz * sz
    return NU_BASE + SGS_COEF * (mag * lax.rsqrt(mag))


def residue_kernel(
    par, near, far, sx_, sy_, sz_, z4, u_ref, v_ref, avg_ref, dy_ref, ry_ref, rz_ref,
    r_ref, out_lo, out_hi, hcols, fx, fyh, fyl,
):
    lane = lane_iota(NYL)
    halo = halo_columns(par, near, far)
    pair = split(halo)
    grad = left(dy_ref[...], pair)
    avg = left_exact(avg_ref[...], pair)
    which = ((lane + 1) % 128) // 32
    hcols[...] = jnp.where(which == 0, grad, jnp.where(which == 3, halo, avg))
    lane16 = lane_iota(16)
    row16 = lax.broadcasted_iota(jnp.int32, (16, NZL), 0)

    def inject(val, rows, q, x):
        rolled = pltpu.roll(hcols[rows, :], (-2 * (16 * q + x)) % 128, 1)
        return jnp.concatenate(
            [
                val[:, 0:128] + jnp.where(lane16 == 0, rolled, 0.0),
                val[:, 128:256] + jnp.where(lane16 == 127, rolled, 0.0),
            ],
            axis=1,
        )

    last = NYL // 16 - 1
    for t in range(last + 1):
        rows = slice(t * 16, t * 16 + 16)
        fz = []
        for x in range(NXL):
            sy = inject(sy_[x, rows, :], rows, 0, x)
            sz = inject(sz_[x, rows, :], rows, 1, x)
            sx = inject(sx_[x, rows, :], rows, 2, x)
            nu = eddy(sx, sy, sz)
            if t in (0, last):
                face, edge, out = (0, 0, out_lo) if t == 0 else (15, -1, out_hi)
                coefs = 0.5 * FM[0] if t == 0 else np.concatenate([np.zeros(8), 0.5 * FM[7]])
                nu = jnp.where(row16 == face, 0.0, nu)
                one = slice(x, x + 1)
                for q, s in enumerate((sx, sy, sz)):
                    out[q, one, :] = s[face : face + 1, :]
                out[5, one, :] = row_sum(inject(z4[x, rows, :], rows, 3, x), coefs)
            uval = u_ref[x, rows, :]
            fx[x, rows, :] = nu * sx - v_ref[0, x, rows, :].astype(F32) * uval
            a, b = split(nu * sy - v_ref[1, x, rows, :].astype(F32) * uval)
            fyh[x, rows, :] = a
            fyl[x, rows, :] = b
            fz.append(nu * sz - v_ref[2, x, rows, :].astype(F32) * uval)
        nodes = [fx[k, rows, :] for k in range(NXL)]
        rx = jnp.concatenate(even_odd(DR, nodes[:8], -1) + even_odd(DR, nodes[8:], -1), axis=0)
        val = rx + right(split(jnp.concatenate(fz, axis=0)), rz_ref[...])
        for x in range(NXL):
            fx[x, rows, :] = val[16 * x : 16 * x + 16]
    face = LY.face
    for x in range(NXL):
        r_ref[x] = fx[x] + left(ry_ref[...], (fyh[x], fyl[x]))
        one = slice(x, x + 1)
        out_lo[3, one, :] = r_ref[x, 0:1, :]
        out_hi[3, one, :] = r_ref[x, NYL - 1 : NYL, :]
        out_lo[4, one, :] = row_sum(r_ref[x, 0:16, :], face[0, 0:16])
        out_hi[4, one, :] = row_sum(r_ref[x, NYL - 16 : NYL, :], face[-1, NYL - 16 :])


def place(pay, x, lane):
    keep = ((lane % 32) // 2) == x
    return jnp.where(keep, pltpu.roll(pay, 2 * x, 1) if x else pay, 0.0)


def filter_kernel(r_ref, z4, hcols, ty_ref, fy_ref, pay_ref, tz_ref, r2, vu, cols):
    lane = lane_iota(NYL)
    acc = None
    for x in range(NXL):
        pair = split(left(ty_ref[...], split(r_ref[x])))
        r2[x] = right(pair, tz_ref[...])
        piece = place(right(pair, pay_ref[...]), x, lane)
        acc = piece if acc is None else acc + piece
        rolled = pltpu.roll(hcols[...], (-2 * (48 + x)) % 128, 1)
        field = z4[x]
        vu[x, :, 0:128] = left(fy_ref[...], split(field[:, 0:128] + jnp.where(lane == 0, rolled, 0.0)))
        vu[x, :, 128:256] = left(fy_ref[...], split(field[:, 128:256] + jnp.where(lane == 127, rolled, 0.0)))
    cols[...] = acc


def y_spread():
    low_t = LY.both[:, 0] + LY.halo[0] + LY.face[-1, -1] * LY.halo[1]
    low_g = (
        LY.both @ LY.res[:, 0] + DR[7, 7] * LY.halo[0] + (LY.face[-1] @ LY.res[:, -1]) * LY.halo[1]
    )
    high_t = LY.both[:, -1] + LY.halo[2] + LY.face[0, 0] * LY.halo[3]
    high_g = (
        LY.both @ LY.res[:, -1] + DR[0, 0] * LY.halo[2] + (LY.face[0] @ LY.res[:, 0]) * LY.halo[3]
    )
    return np.stack(
        [low_t, low_g, LY.halo[0], LY.halo[1], high_t, high_g, LY.halo[2], LY.halo[3]], axis=1
    )


SPREAD = y_spread()


def face_z2_kernel(
    cols_ref, own_lo, own_hi, lo_ref, hi_ref, rx_ref, rz_ref, pay_ref, ay_ref, cols, rows_ref
):
    sides = ((own_lo, lo_ref), (own_hi, hi_ref))
    flux = []
    for own, ref in sides:
        s = [own[q] + ref[q] for q in range(3)]
        nu = eddy(*s)
        flux.append([nu * v for v in s])
    along_x = left(rx_ref[...], split(jnp.concatenate([flux[0][0], flux[1][0]], axis=1)))
    along_z = right(split(jnp.concatenate([flux[0][2], flux[1][2]], axis=0)), rz_ref[...])
    vals = []
    for s, (own, ref) in enumerate(sides):
        tau = along_x[:, s * NZL : (s + 1) * NZL] + along_z[s * NXL : (s + 1) * NXL]
        vals += [tau, flux[s][1], ref[3], ref[4]]
    for k, val in enumerate(vals):
        rows_ref[k] = val
    pay = right(split(jnp.concatenate(vals, axis=0)), pay_ref[...])
    lane16 = lane_iota(NXL)
    row16 = lax.broadcasted_iota(jnp.int32, (NXL, 128), 0)
    keep = ((lane16 % 32) // 2) == row16
    acc = cols_ref[...]
    for k in range(8):
        val = pay[16 * k : 16 * k + 16]
        moved = val
        for bit in (1, 2, 4, 8):
            moved = jnp.where((row16 & bit) != 0, pltpu.roll(moved, 2 * bit, 1), moved)
        vec = jnp.sum(jnp.where(keep, moved, 0.0), axis=0, keepdims=True)
        acc = acc + ay_ref[:, k : k + 1] * vec
    cols[...] = acc


def spread_kernel(r2, vu, rows_ref, lo_ref, hi_ref, ay_ref, tz_ref, out, vout, pay_lo, pay_hi, zr):
    zr[...] = right(split(rows_ref[...].reshape(8 * NXL, NZL)), tz_ref[...]).reshape(8, NXL, NZL)
    row8 = lax.broadcasted_iota(jnp.int32, (8, NZL), 0)
    for t in range(TILES):
        rows = slice(t * 8, t * 8 + 8)
        r, w = [], []
        for x in range(NXL):
            one = slice(x, x + 1)
            val, wal = r2[x, rows, :], vu[x, rows, :]
            if t in (0, 1, 2, TILES - 3, TILES - 2, TILES - 1):
                for k in range(4):
                    k = k if t < 3 else k + 4
                    if np.any(SPREAD[rows, k]):
                        val = val + ay_ref[rows, k : k + 1] * zr[k, one, :]
                out[x, rows, :] = val
            else:
                out[x, rows, :] = val
            if t == 0:
                wal = wal + jnp.where(row8 == 0, lo_ref[5, one, :], 0.0)
            if t == TILES - 1:
                wal = wal + jnp.where(row8 == 7, hi_ref[5, one, :], 0.0)
            vout[x, rows, :] = wal
            r.append(val)
            w.append(wal)
        a = [s + v for s, v in zip(average_x(r), w)]
        pay_lo[0, rows, :] = r[0]
        pay_hi[0, rows, :] = r[15]
        pay_lo[1, rows, :] = sum(float(FM[0, j]) * a[j] for j in range(8))
        pay_hi[1, rows, :] = sum(float(FM[7, j]) * a[8 + j] for j in range(8))


def z_spread():
    add = np.zeros((128, NZL))
    add[0], add[32], add[1], add[33] = LZ.halo
    return add


def z_to_x():
    out = np.zeros((128, 4 * NZL))
    low = np.zeros(16)
    low[:] = LX.face[0]
    high = LX.face[-1]
    for x in range(NXL):
        for q in range(2):
            for side in range(2):
                lane = 2 * (16 * q + x) + side
                vec = LZ.halo[2 * side + q]
                if x == 0:
                    out[lane, 0:NZL] = vec
                if x == NXL - 1:
                    out[lane, 2 * NZL : 3 * NZL] = vec
                out[lane, NZL : 2 * NZL] = low[x] * vec
                out[lane, 3 * NZL :] = high[x] * vec
    return out


def face_x2_kernel(par, near, far, lo_ref, hi_ref, mat_ref, pay_lo, pay_hi, hs):
    low, high = received(par, near, far)
    halo = jnp.where((lane_iota(NYL) % 2) == 0, low, high)
    hs[...] = halo
    add = right(split(halo), mat_ref[...])
    pay_lo[0] = lo_ref[0] + add[:, 0:NZL]
    pay_lo[1] = lo_ref[1] + add[:, NZL : 2 * NZL]
    pay_hi[0] = hi_ref[0] + add[:, 2 * NZL : 3 * NZL]
    pay_hi[1] = hi_ref[1] + add[:, 3 * NZL :]


def local_x_kernel(r2, vu, hs, add_ref, out):
    for t in range(NYL // 16):
        rows = slice(t * 16, t * 16 + 16)
        col = hs[rows, :]
        rolled = [pltpu.roll(col, (-2 * x) % 128, 1) if x else col for x in range(NXL)]
        add = right(split(jnp.concatenate(rolled, axis=0)), add_ref[...])
        r = [r2[x, rows, :] + add[16 * x : 16 * x + 16] for x in range(NXL)]
        a = [s + vu[k, rows, :] for k, s in enumerate(average_x(r))]
        f = average_x(even_odd(FM, a[:8], 1) + even_odd(FM, a[8:], 1))
        f[0] = f[0] + float(0.25 * FM[7, 7]) * r[0]
        f[15] = f[15] + float(0.25 * FM[0, 0]) * r[15]
        for k in range(NXL):
            out[k, rows, :] = f[k]


def final_kernel(val_ref, lo_ref, hi_ref, out_hbm, buf, sems):
    copies = []
    for c in range(4):
        for t in range(3):
            rows = slice(c * 24 + t * 8, c * 24 + t * 8 + 8)
            halo = [lo_ref[0, rows, :], lo_ref[1, rows, :], hi_ref[0, rows, :], hi_ref[1, rows, :]]
            for k in range(NXL):
                val = val_ref[k, rows, :]
                for j in range(4):
                    if LX.halo[j][k] != 0.0:
                        val = val + float(LX.halo[j][k]) * halo[j]
                buf[k, rows, :] = val
        rows = slice(c * 24, c * 24 + 24)
        copies.append(pltpu.make_async_copy(buf.at[:, rows, :], out_hbm.at[:, rows, :], sems.at[c]))
        copies[-1].start()
    for copy in copies:
        copy.wait()


def shift(val, axis, step):
    count = lax.axis_size(axis)
    return lax.ppermute(val, axis, [(i, (i + step) % count) for i in range(count)])


def exchange(lo, hi, axis):
    return shift(hi, axis, 1), shift(lo, axis, -1)


def swap(val, axis, start):
    count = lax.axis_size(axis)
    pairs = [(k % count, (k + 1) % count) for k in range(start, count + start, 2)]
    return lax.ppermute(val, axis, pairs + [(b, a) for a, b in pairs])


def on_device(u, velocity):
    full = (NXL, NYL, NZL)
    face_x = (2, NYL, NZL)
    face_y = (6, NXL, NZL)
    colshape = (NYL, 128)
    par = (lax.axis_index("gz") % 2).astype(jnp.int32).reshape(1, 1)

    sz, dz, fz = exact_right(LZ.avg.T), on_right(LZ.grad.T), on_right(LZ.filt.T)
    sy, dy, fy = exact_left(LY.avg), on_left(LY.grad), on_left(LY.filt)
    ry, rz, rx = on_left(LY.res), on_right(LZ.res.T), on_left(LX.res)
    pay = np.zeros((NZL, 128))
    pay[NZL - 1, 0] = pay[0, 1] = 1.0
    pay[:, 32], pay[:, 33] = LZ.face[-1], LZ.face[0]
    pay = on_right(pay)
    ay = jnp.asarray(SPREAD.astype(np.float32))
    ty, tz = on_left(LY.both), on_right(LZ.both.T)

    u, lo, hi = call(
        face_x_kernel, [full, face_x, face_x], u, hbm=(0,),
        scratch=[pltpu.SemaphoreType.DMA((8,))], name="face_x",
    )
    xlo, xhi = exchange(lo, hi, "gx")
    z1, z2, z3, z4, cols = call(
        local_z_kernel, [full] * 4 + [colshape], u, sz, dz, fz,
        flops=3 * 10**9, nbytes=8 * 10**6, name="local_z",
    )
    dlt, cols = call(face_z_kernel, [(2, 3, NYL, NZL), colshape], xlo, xhi, cols, sz, dz, name="face_z")
    near, far = swap(cols, "gz", 0), swap(cols, "gz", 1)
    sx_, sy_, sz_ = call(
        local_y_kernel, [full] * 3, z1, z2, z3, dlt, sy, dy,
        flops=10**9, nbytes=9 * 10**6, name="local_y",
    )
    r, lo, hi, hcols = call(
        residue_kernel, [full, face_y, face_y, colshape],
        par, near, far, sx_, sy_, sz_, z4, u, velocity, sy, dy, ry, rz, smem=(0,),
        scratch=[pltpu.VMEM(full, F32)] + [pltpu.VMEM(full, BF)] * 2,
        flops=2 * 10**9, nbytes=12 * 10**6, name="residue",
    )
    ylo, yhi = exchange(lo, hi, "gy")
    r2, vu, cols = call(
        filter_kernel, [full, full, colshape], r, z4, hcols, ty, fy, pay, tz,
        flops=2 * 10**9, nbytes=9 * 10**6, name="filter",
    )
    cols, rows = call(
        face_z2_kernel, [colshape, (8, NXL, NZL)], cols, lo, hi, ylo, yhi, rx, rz, pay, ay, name="face_z2"
    )
    near, far = swap(cols, "gz", 0), swap(cols, "gz", 1)
    r2, vu, lo, hi = call(
        spread_kernel, [full, full, face_x, face_x], r2, vu, rows, ylo, yhi, ay, tz,
        scratch=[pltpu.VMEM((8, NXL, NZL), F32)], flops=10**9, nbytes=6 * 10**6, name="spread",
    )
    lo, hi, hs = call(
        face_x2_kernel, [face_x, face_x, colshape], par, near, far, lo, hi, on_right(z_to_x()),
        smem=(0,), name="face_x2",
    )
    xlo, xhi = exchange(lo, hi, "gx")
    val = call(
        local_x_kernel, full, r2, vu, hs, on_right(z_spread()),
        flops=10**9, nbytes=6 * 10**6, name="local_x",
    )
    return call(
        final_kernel, full, val, xlo, xhi, hbm_out=True,
        scratch=[pltpu.VMEM(full, F32), pltpu.SemaphoreType.DMA((4,))], name="final",
    )


def solution(mesh):
    return jax.shard_map(
        on_device,
        mesh=mesh,
        in_specs=(P("gx", "gy", "gz"), P(None, "gx", "gy", "gz")),
        out_specs=P("gx", "gy", "gz"),
        check_vma=False,
    )
```

profile of v0, /device:TPU:6, one launch (start us, length us, event | category | flops | bytes accessed | tf_op | source)
XLA Modules:
  0.0 42.2 jit_solution(8735619507300456206)
XLA Ops:
  0.0 1.4 %copy-done.2 = f32[16,96,256]{2,1,0:T(8,128)S(1)} copy-done((f32[16,96,256]{2,1,0:T(8,128)S(1)}, f32[16,96,256]{2,1,0:T(8,128)}, u32[]{:S(2)}) %copy-start.2) | copy-done | bytes 1572888
  1.4 0.5 %face_x.1 = (f32[16,96,256]{2,1,0:T(8,128)S(1)}, f32[2,96,256]{2,1,0:T(8,128)S(1)}, f32[2,96,256]{2,1,0:T(8,128)S(1)}) custom-call(f32[16,96,256]{2,1,0:T(8,128)S(1)} %copy-done.2), custom_call_target="tpu_custom_call" | custom-call | tf_op jit(solution)/shard_map/face_x/pallas_call | solution.py:155
  1.9 0.5 %collective-permute-start = (f32[2,96,256]{2,1,0:T(8,128)S(1)}, f32[2,96,256]{2,1,0:T(8,128)S(1)}, u32[]{:S(2)}, u32[]{:S(2)}) collective-permute-start(f32[2,96,256]{2,1,0:T(8,128)S(1)} %get-tuple-element.34), channel_id=1, source_target_pairs={{0,32},{32,64},{64,96},{96,0},{1,33},{33,65},{65,97},{97,1},{2,34}... | collective-permute-start | bytes 589832 | tf_op jit(solution)/shard_map/ppermute | solution.py:542
  2.4 1.6 %collective-permute-start.1 = (f32[2,96,256]{2,1,0:T(8,128)S(1)}, f32[2,96,256]{2,1,0:T(8,128)S(1)}, u32[]{:S(2)}, u32[]{:S(2)}) collective-permute-start(f32[2,96,256]{2,1,0:T(8,128)S(1)} %get-tuple-element.35), channel_id=1, source_target_pairs={{0,96},{32,0},{64,32},{96,64},{1,97},{33,1},{65,33},{97,65},{2,98}... | collective-permute-start | bytes 589832 | tf_op jit(solution)/shard_map/ppermute | solution.py:542
  4.0 2.4 %local_z.1 = (f32[16,96,256]{2,1,0:T(8,128)S(1)}, f32[16,96,256]{2,1,0:T(8,128)S(1)}, f32[16,96,256]{2,1,0:T(8,128)S(1)}, f32[16,96,256]{2,1,0:T(8,128)S(1)}, f32[96,128]{1,0:T(8,128)S(1)}) custom-call(f32[16,96,256]{2,1,0:T(8,128)S(1)} %get-tuple-element.36.u_ref, bf16[512,256]{1,0:T(8,128)(2,1)S(1)} %copy-done.7, bf16[768,256]{1,0:T(8,128)(2,1)S(1)} %copy-done.4, ...), custom_call_target="tpu_custom_call" | custom-call | flops 3000000000 | bytes 8000000 | tf_op jit(solution)/shard_map/local_z/pallas_call | solution.py:155
  6.5 2.1 %collective-permute-done.lo_ref = f32[2,96,256]{2,1,0:T(8,128)S(1)} collective-permute-done((f32[2,96,256]{2,1,0:T(8,128)S(1)}, f32[2,96,256]{2,1,0:T(8,128)S(1)}, u32[]{:S(2)}, u32[]{:S(2)}) %collective-permute-start) | collective-permute-done | bytes 196640 | tf_op jit(solution)/shard_map/ppermute | solution.py:542
  8.6 1.3 %collective-permute-done.1.hi_ref = f32[2,96,256]{2,1,0:T(8,128)S(1)} collective-permute-done((f32[2,96,256]{2,1,0:T(8,128)S(1)}, f32[2,96,256]{2,1,0:T(8,128)S(1)}, u32[]{:S(2)}, u32[]{:S(2)}) %collective-permute-start.1) | collective-permute-done | bytes 196640 | tf_op jit(solution)/shard_map/ppermute | solution.py:542
  9.9 0.4 face_z.1
  10.3 2.5 %collective-permute-start.3 = (f32[96,128]{1,0:T(8,128)S(1)}, f32[96,128]{1,0:T(8,128)S(1)}, u32[]{:S(2)}, u32[]{:S(2)}) collective-permute-start(f32[96,128]{1,0:T(8,128)S(1)} %get-tuple-element.38), channel_id=1, source_target_pairs={{1,2},{3,4},{5,6},{7,0},{2,1},{4,3},{6,5},{0,7},{9,10},{11,12},{13... | collective-permute-start | bytes 147464 | tf_op jit(solution)/shard_map/ppermute | solution.py:552
  12.9 1.1 %local_y.1 = (f32[16,96,256]{2,1,0:T(8,128)S(1)}, f32[16,96,256]{2,1,0:T(8,128)S(1)}, f32[16,96,256]{2,1,0:T(8,128)S(1)}) custom-call(f32[16,96,256]{2,1,0:T(8,128)S(1)} %get-tuple-element.39.z1, f32[16,96,256]{2,1,0:T(8,128)S(1)} %get-tuple-element.40.z2, f32[16,96,256]{2,1,0:T(8,128)S(1)} %get-tuple-element.41.z3, ...), custom_call_target="tpu_custom_call" | custom-call | flops 1000000000 | bytes 9000000 | tf_op jit(solution)/shard_map/local_y/pallas_call | solution.py:155
  14.0 1.1 %collective-permute-done.3.far = f32[96,128]{1,0:T(8,128)S(1)} collective-permute-done((f32[96,128]{1,0:T(8,128)S(1)}, f32[96,128]{1,0:T(8,128)S(1)}, u32[]{:S(2)}, u32[]{:S(2)}) %collective-permute-start.3) | collective-permute-done | bytes 49184 | tf_op jit(solution)/shard_map/ppermute | solution.py:552
  15.2 3.5 %residue.1 = (f32[16,96,256]{2,1,0:T(8,128)S(1)}, f32[6,16,256]{2,1,0:T(8,128)S(1)}, f32[6,16,256]{2,1,0:T(8,128)S(1)}, f32[96,128]{1,0:T(8,128)S(1)}) custom-call(s32[1,1]{1,0:T(1,128)} %bitcast.par, f32[96,128]{1,0:T(8,128)S(1)} %collective-permute-done.2.near, f32[96,128]{1,0:T(8,128)S(1)} %collective-permute-done.3.far, ...), custom_call_target="tpu_custom_call" | custom-call | flops 2000000000 | bytes 12000000 | tf_op jit(solution)/shard_map/residue/pallas_call | solution.py:155
  18.7 3.2 %collective-permute-start.5 = (f32[6,16,256]{2,1,0:T(8,128)S(1)}, f32[6,16,256]{2,1,0:T(8,128)S(1)}, u32[]{:S(2)}, u32[]{:S(2)}) collective-permute-start(f32[6,16,256]{2,1,0:T(8,128)S(1)} %get-tuple-element.52.own_lo), channel_id=1, source_target_pairs={{0,24},{8,0},{16,8},{24,16},{1,25},{9,1},{17,9},{25,17},{2,26},{10... | collective-permute-start | bytes 294920 | tf_op jit(solution)/shard_map/ppermute | solution.py:542
  21.9 5.3 %filter.1 = (f32[16,96,256]{2,1,0:T(8,128)S(1)}, f32[16,96,256]{2,1,0:T(8,128)S(1)}, f32[96,128]{1,0:T(8,128)S(1)}) custom-call(f32[16,96,256]{2,1,0:T(8,128)S(1)} %get-tuple-element.47.r_ref, f32[16,96,256]{2,1,0:T(8,128)S(1)} %get-tuple-element.46.z4, f32[96,128]{1,0:T(8,128)S(1)} %get-tuple-element.48.hcols, bf16[96,288]{1,0:T(8,128)(2,1)S(1)} %copy-done.15, ...), custom_call_target="tpu_custom_call" | custom-call | flops 2000000000 | bytes 9000000 | tf_op jit(solution)/shard_map/filter/pallas_call | solution.py:155
  27.3 0.4 %collective-permute-done.4.lo_ref = f32[6,16,256]{2,1,0:T(8,128)S(1)} collective-permute-done((f32[6,16,256]{2,1,0:T(8,128)S(1)}, f32[6,16,256]{2,1,0:T(8,128)S(1)}, u32[]{:S(2)}, u32[]{:S(2)}) %collective-permute-start.4) | collective-permute-done | bytes 98336 | tf_op jit(solution)/shard_map/ppermute | solution.py:542
  27.7 0.8 %face_z2.1 = (f32[96,128]{1,0:T(8,128)S(1)}, f32[8,16,256]{2,1,0:T(8,128)S(1)}) custom-call(f32[96,128]{1,0:T(8,128)S(1)} %get-tuple-element.51.cols_ref, f32[6,16,256]{2,1,0:T(8,128)S(1)} %get-tuple-element.52.own_lo, f32[6,16,256]{2,1,0:T(8,128)S(1)} %get-tuple-element.53.own_hi, f32[6,16,256]{2,1,0:T(8,128)S(1)} %collective-permute-done.4.lo_ref, ...), custom_call_target="tpu_custom_call" | custom-call | tf_op jit(solution)/shard_map/face_z2/pallas_call | solution.py:155
  28.5 1.7 %collective-permute-start.7 = (f32[96,128]{1,0:T(8,128)S(1)}, f32[96,128]{1,0:T(8,128)S(1)}, u32[]{:S(2)}, u32[]{:S(2)}) collective-permute-start(f32[96,128]{1,0:T(8,128)S(1)} %get-tuple-element.57), channel_id=1, source_target_pairs={{1,2},{3,4},{5,6},{7,0},{2,1},{4,3},{6,5},{0,7},{9,10},{11,12},{13... | collective-permute-start | bytes 147464 | tf_op jit(solution)/shard_map/ppermute | solution.py:552
  30.2 0.7 %spread.1 = (f32[16,96,256]{2,1,0:T(8,128)S(1)}, f32[16,96,256]{2,1,0:T(8,128)S(1)}, f32[2,96,256]{2,1,0:T(8,128)S(1)}, f32[2,96,256]{2,1,0:T(8,128)S(1)}) custom-call(f32[16,96,256]{2,1,0:T(8,128)S(1)} %get-tuple-element.49.r2, f32[16,96,256]{2,1,0:T(8,128)S(1)} %get-tuple-element.50.vu, f32[8,16,256]{2,1,0:T(8,128)S(1)} %get-tuple-element.54.rows_ref, ...), custom_call_target="tpu_custom_call" | custom-call | flops 1000000000 | bytes 6000000 | tf_op jit(solution)/shard_map/spread/pallas_call | solution.py:155
  30.9 2.4 %collective-permute-done.7.far = f32[96,128]{1,0:T(8,128)S(1)} collective-permute-done((f32[96,128]{1,0:T(8,128)S(1)}, f32[96,128]{1,0:T(8,128)S(1)}, u32[]{:S(2)}, u32[]{:S(2)}) %collective-permute-start.7) | collective-permute-done | bytes 49184 | tf_op jit(solution)/shard_map/ppermute | solution.py:552
  33.9 1.7 %collective-permute-start.9 = (f32[2,96,256]{2,1,0:T(8,128)S(1)}, f32[2,96,256]{2,1,0:T(8,128)S(1)}, u32[]{:S(2)}, u32[]{:S(2)}) collective-permute-start(f32[2,96,256]{2,1,0:T(8,128)S(1)} %get-tuple-element.62), channel_id=1, source_target_pairs={{0,96},{32,0},{64,32},{96,64},{1,97},{33,1},{65,33},{97,65},{2,98}... | collective-permute-start | bytes 589832 | tf_op jit(solution)/shard_map/ppermute | solution.py:542
  35.7 1.1 %local_x.1.val_ref = f32[16,96,256]{2,1,0:T(8,128)S(1)} custom-call(f32[16,96,256]{2,1,0:T(8,128)S(1)} %get-tuple-element.55.r2, f32[16,96,256]{2,1,0:T(8,128)S(1)} %get-tuple-element.56.vu, f32[96,128]{1,0:T(8,128)S(1)} %get-tuple-element.60.hs, bf16[384,256]{1,0:T(8,128)(2,1)S(1)} %copy-done.10), custom_call_target="tpu_custom_call" | custom-call | flops 1000000000 | bytes 6000000 | tf_op jit(solution)/shard_map/local_x/pallas_call | solution.py:155
  36.8 2.5 %collective-permute-done.8.lo_ref = f32[2,96,256]{2,1,0:T(8,128)S(1)} collective-permute-done((f32[2,96,256]{2,1,0:T(8,128)S(1)}, f32[2,96,256]{2,1,0:T(8,128)S(1)}, u32[]{:S(2)}, u32[]{:S(2)}) %collective-permute-start.8) | collective-permute-done | bytes 196640 | tf_op jit(solution)/shard_map/ppermute | solution.py:542
  39.3 1.5 %collective-permute-done.9.hi_ref = f32[2,96,256]{2,1,0:T(8,128)S(1)} collective-permute-done((f32[2,96,256]{2,1,0:T(8,128)S(1)}, f32[2,96,256]{2,1,0:T(8,128)S(1)}, u32[]{:S(2)}, u32[]{:S(2)}) %collective-permute-start.9) | collective-permute-done | bytes 196640 | tf_op jit(solution)/shard_map/ppermute | solution.py:542
  40.8 1.2 %final.1 = f32[16,96,256]{2,1,0:T(8,128)} custom-call(f32[16,96,256]{2,1,0:T(8,128)S(1)} %local_x.1.val_ref, f32[2,96,256]{2,1,0:T(8,128)S(1)} %collective-permute-done.8.lo_ref, f32[2,96,256]{2,1,0:T(8,128)S(1)} %collective-permute-done.9.hi_ref), custom_call_target="tpu_custom_call" | custom-call | tf_op jit(solution)/shard_map/final/pallas_call | solution.py:155
  (41 shorter events, 0.7 us)
Async XLA Ops:
  1.4 2.6 %copy-start.4 = (bf16[768,256]{1,0:T(8,128)(2,1)S(1)}, bf16[768,256]{1,0:T(8,128)(2,1)}, u32[]{:S(2)}) copy-start(bf16[768,256]{1,0:T(8,128)(2,1)} %constant.48.clone.dz_ref) | copy-start | bytes 1179652
  1.4 2.6 %copy-start.7 = (bf16[512,256]{1,0:T(8,128)(2,1)S(1)}, bf16[512,256]{1,0:T(8,128)(2,1)}, u32[]{:S(2)}) copy-start(bf16[512,256]{1,0:T(8,128)(2,1)} %constant.47.clone.sz_ref) | copy-start | bytes 786436
  1.4 2.6 %copy-start.14 = (bf16[768,256]{1,0:T(8,128)(2,1)S(1)}, bf16[768,256]{1,0:T(8,128)(2,1)}, u32[]{:S(2)}) copy-start(bf16[768,256]{1,0:T(8,128)(2,1)} %constant.49.clone.fz_ref) | copy-start | bytes 1179652
  1.9 6.7 %collective-permute-start = (f32[2,96,256]{2,1,0:T(8,128)S(1)}, f32[2,96,256]{2,1,0:T(8,128)S(1)}, u32[]{:S(2)}, u32[]{:S(2)}) collective-permute-start(f32[2,96,256]{2,1,0:T(8,128)S(1)} %get-tuple-element.34), channel_id=1, source_target_pairs={{0,32},{32,64},{64,96},{96,0},{1,33},{33,65},{65,97},{97,1},{2,34}... | collective-permute-start | bytes 589832 | tf_op jit(solution)/shard_map/ppermute | solution.py:542
  2.4 7.5 %collective-permute-start.1 = (f32[2,96,256]{2,1,0:T(8,128)S(1)}, f32[2,96,256]{2,1,0:T(8,128)S(1)}, u32[]{:S(2)}, u32[]{:S(2)}) collective-permute-start(f32[2,96,256]{2,1,0:T(8,128)S(1)} %get-tuple-element.35), channel_id=1, source_target_pairs={{0,96},{32,0},{64,32},{96,64},{1,97},{33,1},{65,33},{97,65},{2,98}... | collective-permute-start | bytes 589832 | tf_op jit(solution)/shard_map/ppermute | solution.py:542
  4.0 8.8 %copy-start.6 = (bf16[96,288]{1,0:T(8,128)(2,1)S(1)}, bf16[96,288]{1,0:T(8,128)(2,1)}, u32[]{:S(2)}) copy-start(bf16[96,288]{1,0:T(8,128)(2,1)} %constant.51.clone.dy_ref) | copy-start | bytes 165892
  4.0 8.8 %copy-start.8 = (bf16[96,192]{1,0:T(8,128)(2,1)S(1)}, bf16[96,192]{1,0:T(8,128)(2,1)}, u32[]{:S(2)}) copy-start(bf16[96,192]{1,0:T(8,128)(2,1)} %constant.50.clone.sy_ref.avg_ref) | copy-start | bytes 110596
  10.3 4.8 %collective-permute-start.3 = (f32[96,128]{1,0:T(8,128)S(1)}, f32[96,128]{1,0:T(8,128)S(1)}, u32[]{:S(2)}, u32[]{:S(2)}) collective-permute-start(f32[96,128]{1,0:T(8,128)S(1)} %get-tuple-element.38), channel_id=1, source_target_pairs={{1,2},{3,4},{5,6},{7,0},{2,1},{4,3},{6,5},{0,7},{9,10},{11,12},{13... | collective-permute-start | bytes 147464 | tf_op jit(solution)/shard_map/ppermute | solution.py:552
  12.8 2.3 %collective-permute-start.2 = (f32[96,128]{1,0:T(8,128)S(1)}, f32[96,128]{1,0:T(8,128)S(1)}, u32[]{:S(2)}, u32[]{:S(2)}) collective-permute-start(f32[96,128]{1,0:T(8,128)S(1)} %get-tuple-element.38), channel_id=1, source_target_pairs={{0,1},{2,3},{4,5},{6,7},{1,0},{3,2},{5,4},{7,6},{8,9},{10,11},{12,... | collective-permute-start | bytes 147464 | tf_op jit(solution)/shard_map/ppermute | solution.py:552
  12.8 2.3 %copy-start = (bf16[3,16,96,256]{3,2,1,0:T(8,128)(2,1)S(1)}, bf16[3,16,96,256]{3,2,1,0:T(8,128)(2,1)}, u32[]{:S(2)}) copy-start(bf16[3,16,96,256]{3,2,1,0:T(8,128)(2,1)} %v_ref.1) | copy-start | bytes 7077892
  15.2 6.7 %copy-start.5 = (bf16[768,256]{1,0:T(8,128)(2,1)S(1)}, bf16[768,256]{1,0:T(8,128)(2,1)}, u32[]{:S(2)}) copy-start(bf16[768,256]{1,0:T(8,128)(2,1)} %constant.59.clone.tz_ref) | copy-start | bytes 1179652
  15.2 6.7 %copy-start.11 = (bf16[768,128]{1,0:T(8,128)(2,1)S(1)}, bf16[768,128]{1,0:T(8,128)(2,1)}, u32[]{:S(2)}) copy-start(bf16[768,128]{1,0:T(8,128)(2,1)} %constant.56.clone.pay_ref) | copy-start | bytes 589828
  15.2 6.7 %copy-start.15 = (bf16[96,288]{1,0:T(8,128)(2,1)S(1)}, bf16[96,288]{1,0:T(8,128)(2,1)}, u32[]{:S(2)}) copy-start(bf16[96,288]{1,0:T(8,128)(2,1)} %constant.58.clone.ty_ref) | copy-start | bytes 165892
  15.2 6.7 %copy-start.16 = (bf16[96,288]{1,0:T(8,128)(2,1)S(1)}, bf16[96,288]{1,0:T(8,128)(2,1)}, u32[]{:S(2)}) copy-start(bf16[96,288]{1,0:T(8,128)(2,1)} %constant.52.clone.fy_ref) | copy-start | bytes 165892
  18.7 8.6 %collective-permute-start.5 = (f32[6,16,256]{2,1,0:T(8,128)S(1)}, f32[6,16,256]{2,1,0:T(8,128)S(1)}, u32[]{:S(2)}, u32[]{:S(2)}) collective-permute-start(f32[6,16,256]{2,1,0:T(8,128)S(1)} %get-tuple-element.52.own_lo), channel_id=1, source_target_pairs={{0,24},{8,0},{16,8},{24,16},{1,25},{9,1},{17,9},{25,17},{2,26},{10... | collective-permute-start | bytes 294920 | tf_op jit(solution)/shard_map/ppermute | solution.py:542
  21.9 5.8 %collective-permute-start.4 = (f32[6,16,256]{2,1,0:T(8,128)S(1)}, f32[6,16,256]{2,1,0:T(8,128)S(1)}, u32[]{:S(2)}, u32[]{:S(2)}) collective-permute-start(f32[6,16,256]{2,1,0:T(8,128)S(1)} %get-tuple-element.53.own_hi), channel_id=1, source_target_pairs={{0,8},{8,16},{16,24},{24,0},{1,9},{9,17},{17,25},{25,1},{2,10},{10... | collective-permute-start | bytes 294920 | tf_op jit(solution)/shard_map/ppermute | solution.py:542
  21.9 5.8 %copy-start.9 = (f32[96,8]{1,0:T(8,128)S(1)}, f32[96,8]{1,0:T(8,128)}, u32[]{:S(2)}) copy-start(f32[96,8]{1,0:T(8,128)} %constant.57.clone.ay_ref) | copy-start | bytes 9220
  21.9 5.8 %copy-start.13 = (bf16[16,48]{1,0:T(8,128)(2,1)S(1)}, bf16[16,48]{1,0:T(8,128)(2,1)}, u32[]{:S(2)}) copy-start(bf16[16,48]{1,0:T(8,128)(2,1)} %constant.55.clone.rx_ref) | copy-start | bytes 4612
  28.5 4.8 %collective-permute-start.7 = (f32[96,128]{1,0:T(8,128)S(1)}, f32[96,128]{1,0:T(8,128)S(1)}, u32[]{:S(2)}, u32[]{:S(2)}) collective-permute-start(f32[96,128]{1,0:T(8,128)S(1)} %get-tuple-element.57), channel_id=1, source_target_pairs={{1,2},{3,4},{5,6},{7,0},{2,1},{4,3},{6,5},{0,7},{9,10},{11,12},{13... | collective-permute-start | bytes 147464 | tf_op jit(solution)/shard_map/ppermute | solution.py:552
  30.2 3.1 %collective-permute-start.6 = (f32[96,128]{1,0:T(8,128)S(1)}, f32[96,128]{1,0:T(8,128)S(1)}, u32[]{:S(2)}, u32[]{:S(2)}) collective-permute-start(f32[96,128]{1,0:T(8,128)S(1)} %get-tuple-element.57), channel_id=1, source_target_pairs={{0,1},{2,3},{4,5},{6,7},{1,0},{3,2},{5,4},{7,6},{8,9},{10,11},{12,... | collective-permute-start | bytes 147464 | tf_op jit(solution)/shard_map/ppermute | solution.py:552
  30.2 3.1 %copy-start.3 = (bf16[384,1024]{1,0:T(8,128)(2,1)S(1)}, bf16[384,1024]{1,0:T(8,128)(2,1)}, u32[]{:S(2)}) copy-start(bf16[384,1024]{1,0:T(8,128)(2,1)} %constant.60.clone.mat_ref) | copy-start | bytes 2359300
  30.2 5.5 %copy-start.10 = (bf16[384,256]{1,0:T(8,128)(2,1)S(1)}, bf16[384,256]{1,0:T(8,128)(2,1)}, u32[]{:S(2)}) copy-start(bf16[384,256]{1,0:T(8,128)(2,1)} %constant.61.clone.add_ref) | copy-start | bytes 589828
  33.6 5.7 %collective-permute-start.8 = (f32[2,96,256]{2,1,0:T(8,128)S(1)}, f32[2,96,256]{2,1,0:T(8,128)S(1)}, u32[]{:S(2)}, u32[]{:S(2)}) collective-permute-start(f32[2,96,256]{2,1,0:T(8,128)S(1)} %get-tuple-element.61), channel_id=1, source_target_pairs={{0,32},{32,64},{64,96},{96,0},{1,33},{33,65},{65,97},{97,1},{2,34}... | collective-permute-start | bytes 589832 | tf_op jit(solution)/shard_map/ppermute | solution.py:542
  33.9 6.9 %collective-permute-start.9 = (f32[2,96,256]{2,1,0:T(8,128)S(1)}, f32[2,96,256]{2,1,0:T(8,128)S(1)}, u32[]{:S(2)}, u32[]{:S(2)}) collective-permute-start(f32[2,96,256]{2,1,0:T(8,128)S(1)} %get-tuple-element.62), channel_id=1, source_target_pairs={{0,96},{32,0},{64,32},{96,64},{1,97},{33,1},{65,33},{97,65},{2,98}... | collective-permute-start | bytes 589832 | tf_op jit(solution)/shard_map/ppermute | solution.py:542
  (3 other events, 6.0 us)
where the time goes:
time: 42.3 us; the launch traced here: 42.2 us
  Pallas kernels  17.4 us (41%)
  starting transfers between devices  11.6 us (27%)
  waiting for transfers between devices  11.4 us (27%)
  local copies, waits for them, and re-layouts  1.5 us (4%)
    pallas_call x11, Pallas kernels, call(): pl.pallas_call(kernel, out_shape=shapes, in_specs=[kinds.get(i, VM) for i...  17.4 us
    ppermute x6, waiting for transfers between devices, shift(): lax.ppermute(val, axis, [(i, (i + step) % count) for i in range(count)])  7.89 us
    ppermute x6, starting transfers between devices, shift(): lax.ppermute(val, axis, [(i, (i + step) % count) for i in range(count)])  7.4 us
    ppermute x4, starting transfers between devices, swap(): return lax.ppermute(val, axis, pairs + [(b, a) for a, b in pairs])  4.17 us
    ppermute x4, waiting for transfers between devices, swap(): return lax.ppermute(val, axis, pairs + [(b, a) for a, b in pairs])  3.51 us
    unnamed x34, local copies, waits for them, and re-layouts  1.5 us
  transfers between devices with their start and end apart: 10, of which 7 were waited for; matrix products, arithmetic and copies ran while one was open for 0% of the time, Pallas kernels for 25%

commit v1 on v0

--- a/solution.py
+++ b/solution.py
@@ -147,18 +147,19 @@
     return mm(mat, jnp.concatenate(pair, axis=0))
 
 
-def call(kernel, outs, *args, scratch=(), flops=0, nbytes=0, name=None, hbm=(), hbm_out=False, smem=()):
+def call(kernel, outs, *args, scratch=(), flops=0, nbytes=0, name=None, hbm=(), hbm_out=False, smem=(), limit=6 << 20):
     single = not isinstance(outs, list)
-    shapes = [jax.ShapeDtypeStruct(o, F32) for o in ([outs] if single else outs)]
-    kinds = {i: pl.BlockSpec(memory_space=pl.ANY) for i in hbm}
+    place_at = pltpu.HBM if hbm_out else pltpu.VMEM
+    shapes = [place_at(tuple(o), F32) for o in ([outs] if single else outs)]
+    kinds = {i: pl.BlockSpec(memory_space=pltpu.HBM) for i in hbm}
     kinds.update({i: pl.BlockSpec(memory_space=pltpu.SMEM) for i in smem})
     res = pl.pallas_call(
         kernel,
         out_shape=shapes,
         in_specs=[kinds.get(i, VM) for i in range(len(args))],
-        out_specs=[pl.BlockSpec(memory_space=pl.ANY) if hbm_out else VM] * len(shapes),
+        out_specs=[pl.BlockSpec(memory_space=pltpu.HBM) if hbm_out else VM] * len(shapes),
         scratch_shapes=list(scratch),
-        compiler_params=pltpu.CompilerParams(vmem_limit_bytes=20 << 20),
+        compiler_params=pltpu.CompilerParams(vmem_limit_bytes=limit),
         cost_estimate=pl.CostEstimate(flops=flops, bytes_accessed=nbytes, transcendentals=0),
         name=name,
     )(*args)
@@ -173,27 +174,18 @@
 LX, LY, LZ = Line(NXL), Line(NYL), Line(NZL)
 
 
-def face_x_kernel(u_hbm, u_ref, lo_ref, hi_ref, sems):
-    copies = []
-    for c in range(4):
-        rows = slice(c * 24, c * 24 + 24)
-        for s in range(2):
-            xs = slice(8 * s, 8 * s + 8)
-            copies.append(
-                pltpu.make_async_copy(u_hbm.at[xs, rows, :], u_ref.at[xs, rows, :], sems.at[2 * c + s])
-            )
-    for copy in copies:
-        copy.start()
-    for c in range(4):
-        copies[2 * c].wait()
-        copies[2 * c + 1].wait()
-        for t in range(3):
-            rows = slice(c * 24 + t * 8, c * 24 + t * 8 + 8)
-            nodes = [u_ref[k, rows, :] for k in range(NXL)]
-            lo_ref[0, rows, :] = 0.5 * nodes[0]
-            lo_ref[1, rows, :] = sum(float(0.5 * D[0, j]) * nodes[j] for j in range(8))
-            hi_ref[0, rows, :] = 0.5 * nodes[15]
-            hi_ref[1, rows, :] = sum(float(0.5 * D[7, j]) * nodes[8 + j] for j in range(8))
+def face_hi_kernel(u_ref, hi_ref):
+    for t in range(TILES):
+        rows = slice(t * 8, t * 8 + 8)
+        hi_ref[0, rows, :] = 0.5 * u_ref[7, rows, :]
+        hi_ref[1, rows, :] = sum(float(0.5 * D[7, j]) * u_ref[j, rows, :] for j in range(8))
+
+
+def face_lo_kernel(u_ref, lo_ref):
+    for t in range(TILES):
+        rows = slice(t * 8, t * 8 + 8)
+        lo_ref[0, rows, :] = 0.5 * u_ref[0, rows, :]
+        lo_ref[1, rows, :] = sum(float(0.5 * D[0, j]) * u_ref[j, rows, :] for j in range(8))
 
 
 def even_odd(mat, nodes, sign):
@@ -232,22 +224,22 @@
     return total
 
 
-def received(par_ref, near_ref, far_ref):
-    first = par_ref[0, 0] == 0
+def received(near_ref, far_ref):
+    first = lax.rem(lax.axis_index("gz"), 2) == 0
     near, far = near_ref[...], far_ref[...]
     return jnp.where(first, far, near), jnp.where(first, near, far)
 
 
-def halo_columns(par_ref, near_ref, far_ref):
-    low, high = received(par_ref, near_ref, far_ref)
-    return jnp.where((lane_iota(NYL) % 2) == 0, low, pltpu.roll(high, 126, 1))
-
-
-def local_z_kernel(u_ref, sz_ref, dz_ref, fz_ref, z1, z2, z3, z4, cols):
+def halo_columns(near_ref, far_ref):
+    low, high = received(near_ref, far_ref)
+    return jnp.where((lane_iota(NYL) % 2) == 0, pltpu.roll(high, 127, 1), pltpu.roll(low, 1, 1))
+
+
+def local_z_kernel(ulo_ref, uhi_ref, sz_ref, dz_ref, fz_ref, z1, z2, z3, z4, cols):
     lane = lane_iota(16)
     for t in range(NYL // 16):
         rows = slice(t * 16, t * 16 + 16)
-        nodes = [u_ref[k, rows, :] for k in range(NXL)]
+        nodes = [ref[k, rows, :] for ref in (ulo_ref, uhi_ref) for k in range(8)]
         grads = even_odd(D, nodes[:8], -1) + even_odd(D, nodes[8:], -1)
         flat = lambda vals: jnp.concatenate(vals, axis=0)
         p = split(flat(average_x(nodes)))
@@ -282,14 +274,18 @@
     cols[...] = acc
 
 
-def local_y_kernel(z1, z2, z3, dlt, sy_ref, dy_ref, sx_, sy_, sz_):
+def local_y_kernel(z1, z2, z3, sy_ref, dy_ref, sx_, sy_, sz_):
+    for x in range(1, NXL - 1):
+        sy_[x - 1] = left(dy_ref[...], split(z1[x]))
+        sz_[x - 1] = left_exact(sy_ref[...], split(z2[x]))
+        sx_[x - 1] = left_exact(sy_ref[...], split(z3[x]))
+
+
+def product_kernel(ulo_ref, uhi_ref, v_ref, after_ref, h_ref):
     for x in range(NXL):
-        vals = [z1[x], z2[x], z3[x]]
-        if x in (0, NXL - 1):
-            vals = [v + dlt[0 if x == 0 else 1, q] for q, v in enumerate(vals)]
-        sy_[x] = left(dy_ref[...], split(vals[0]))
-        sz_[x] = left_exact(sy_ref[...], split(vals[1]))
-        sx_[x] = left_exact(sy_ref[...], split(vals[2]))
+        u = ulo_ref[x] if x < 8 else uhi_ref[x - 8]
+        for d in range(3):
+            h_ref[d, x] = v_ref[d, x].astype(F32) * u
 
 
 def row_sum(vals, coefs):
@@ -306,52 +302,45 @@
 
 
 def residue_kernel(
-    par, near, far, sx_, sy_, sz_, z4, u_ref, v_ref, avg_ref, dy_ref, ry_ref, rz_ref,
-    r_ref, out_lo, out_hi, hcols, fx, fyh, fyl,
+    sx_, sy_, sz_, z1, z2, z3, z4, dlt, h_ref, avg_ref, dy_ref, ry_ref, rz_ref,
+    r_ref, out_lo, out_hi, fx, fyh, fyl, edge,
 ):
-    lane = lane_iota(NYL)
-    halo = halo_columns(par, near, far)
-    pair = split(halo)
-    grad = left(dy_ref[...], pair)
-    avg = left_exact(avg_ref[...], pair)
-    which = ((lane + 1) % 128) // 32
-    hcols[...] = jnp.where(which == 0, grad, jnp.where(which == 3, halo, avg))
-    lane16 = lane_iota(16)
+    for s, x in ((0, 0), (1, NXL - 1)):
+        edge[s, 1] = left(dy_ref[...], split(z1[x] + dlt[s, 0]))
+        edge[s, 2] = left_exact(avg_ref[...], split(z2[x] + dlt[s, 1]))
+        edge[s, 0] = left_exact(avg_ref[...], split(z3[x] + dlt[s, 2]))
     row16 = lax.broadcasted_iota(jnp.int32, (16, NZL), 0)
-
-    def inject(val, rows, q, x):
-        rolled = pltpu.roll(hcols[rows, :], (-2 * (16 * q + x)) % 128, 1)
-        return jnp.concatenate(
-            [
-                val[:, 0:128] + jnp.where(lane16 == 0, rolled, 0.0),
-                val[:, 128:256] + jnp.where(lane16 == 127, rolled, 0.0),
-            ],
-            axis=1,
-        )
-
+    lane16 = lax.broadcasted_iota(jnp.int32, (16, NZL), 1)
+    inner = (lane16 != 0) & (lane16 != NZL - 1)
     last = NYL // 16 - 1
     for t in range(last + 1):
         rows = slice(t * 16, t * 16 + 16)
+        mask = inner
+        if t == 0:
+            mask = mask & (row16 != 0)
+        if t == last:
+            mask = mask & (row16 != 15)
+        mask = mask.astype(F32)
         fz = []
         for x in range(NXL):
-            sy = inject(sy_[x, rows, :], rows, 0, x)
-            sz = inject(sz_[x, rows, :], rows, 1, x)
-            sx = inject(sx_[x, rows, :], rows, 2, x)
-            nu = eddy(sx, sy, sz)
+            if x in (0, NXL - 1):
+                sx, sy, sz = [edge[0 if x == 0 else 1, q, rows, :] for q in range(3)]
+            else:
+                sx, sy, sz = [ref[x - 1, rows, :] for ref in (sx_, sy_, sz_)]
+            nu = eddy(sx, sy, sz) * mask
             if t in (0, last):
-                face, edge, out = (0, 0, out_lo) if t == 0 else (15, -1, out_hi)
+                face, out = (0, out_lo) if t == 0 else (15, out_hi)
                 coefs = 0.5 * FM[0] if t == 0 else np.concatenate([np.zeros(8), 0.5 * FM[7]])
-                nu = jnp.where(row16 == face, 0.0, nu)
                 one = slice(x, x + 1)
-                for q, s in enumerate((sx, sy, sz)):
-                    out[q, one, :] = s[face : face + 1, :]
-                out[5, one, :] = row_sum(inject(z4[x, rows, :], rows, 3, x), coefs)
-            uval = u_ref[x, rows, :]
-            fx[x, rows, :] = nu * sx - v_ref[0, x, rows, :].astype(F32) * uval
-            a, b = split(nu * sy - v_ref[1, x, rows, :].astype(F32) * uval)
+                for q, val in enumerate((sx, sy, sz)):
+                    row = val[face : face + 1, :]
+                    out[q, one, :] = jnp.where(inner[0:1, :], row, 0.0)
+                out[5, one, :] = row_sum(z4[x, rows, :], coefs)
+            fx[x, rows, :] = nu * sx - h_ref[0, x, rows, :]
+            a, b = split(nu * sy - h_ref[1, x, rows, :])
             fyh[x, rows, :] = a
             fyl[x, rows, :] = b
-            fz.append(nu * sz - v_ref[2, x, rows, :].astype(F32) * uval)
+            fz.append(nu * sz - h_ref[2, x, rows, :])
         nodes = [fx[k, rows, :] for k in range(NXL)]
         rx = jnp.concatenate(even_odd(DR, nodes[:8], -1) + even_odd(DR, nodes[8:], -1), axis=0)
         val = rx + right(split(jnp.concatenate(fz, axis=0)), rz_ref[...])
@@ -367,24 +356,95 @@
         out_hi[4, one, :] = row_sum(r_ref[x, NYL - 16 : NYL, :], face[-1, NYL - 16 :])
 
 
+def z_columns_x():
+    mat = np.zeros((128, 128))
+    for side in range(2):
+        mat[side:32:2, side:32:2] = LX.res.T
+    return mat
+
+
+def z_face_vectors():
+    mat = np.zeros((128, NZL))
+    for x in range(NXL):
+        for side, node in ((0, NZL - 1), (1, 0)):
+            mat[2 * x + side, node] = 1.0
+            mat[32 + 2 * x + side] = LZ.res[:, node]
+    return mat
+
+
+def y_rows():
+    rows = np.zeros((8, NYL))
+    rows[0], rows[1] = LY.face[0], LY.face[-1]
+    rows[2, 0:8], rows[3, NYL - 8 :] = 0.5 * FM[0], 0.5 * FM[7]
+    return rows
+
+
+def face_y_kernel(
+    near, far, cols, lo_ref, hi_ref, avg_ref, dy_ref, ry_ref, rx_ref, zv_ref, yr_ref,
+    out_lo, out_hi, cval, halo_ref,
+):
+    lane = lane_iota(NYL)
+    halo = halo_columns(near, far)
+    halo_ref[...] = halo
+    pair = split(cols[...] + halo)
+    sy = left(dy_ref[...], pair)
+    avg = left_exact(avg_ref[...], pair)
+    sz, sx = pltpu.roll(avg, 96, 1), pltpu.roll(avg, 64, 1)
+    row = lax.broadcasted_iota(jnp.int32, (NYL, 128), 0)
+    keep = (lane < 32) & (row != 0) & (row != NYL - 1)
+    nu = jnp.where(keep, eddy(sx, sy, sz), 0.0)
+    tau = right(split(nu * sx), rx_ref[...]) + left(ry_ref[...], split(nu * sy))
+    val = tau + pltpu.roll(nu * sz, 32, 1)
+    cval[...] = val
+    rows = left(yr_ref[...], split(jnp.concatenate([val, pltpu.roll(halo, 32, 1)], axis=1)))
+    lane16 = lane_iota(NXL)
+    row16 = lax.broadcasted_iota(jnp.int32, (NXL, 128), 0)
+    diag = ((lane16 % 32) // 2) == row16
+    short, long = diag & (lane16 < 32), diag & (lane16 < 64)
+    parts_ = []
+    for s, r in ((0, 0), (1, NYL - 1)):
+        one = slice(r, r + 1)
+        for vec, keep in (
+            (sx[one], short), (sy[one], short), (sz[one], short), (val[one], long),
+            (rows[s : s + 1, 0:128], long), (rows[2 + s : 3 + s, 128:256], short),
+        ):
+            parts_.append(jnp.where(keep, jnp.broadcast_to(vec, (NXL, 128)), 0.0))
+    add = right(split(jnp.concatenate(parts_, axis=0)), zv_ref[...])
+    for q in range(6):
+        out_lo[q] = lo_ref[q] + add[16 * q : 16 * q + 16]
+        out_hi[q] = hi_ref[q] + add[96 + 16 * q : 112 + 16 * q]
+
+
 def place(pay, x, lane):
     keep = ((lane % 32) // 2) == x
     return jnp.where(keep, pltpu.roll(pay, 2 * x, 1) if x else pay, 0.0)
 
 
-def filter_kernel(r_ref, z4, hcols, ty_ref, fy_ref, pay_ref, tz_ref, r2, vu, cols):
+def filter_kernel(r_ref, cval, ty_ref, pay_ref, zc_ref, r1, cols, cout):
     lane = lane_iota(NYL)
     acc = None
+    for c in range(4):
+        for x in range(4 * c, 4 * c + 4):
+            r1[x] = left(ty_ref[...], split(r_ref[x]))
+        val = r1[4 * c : 4 * c + 4].reshape(4 * NYL, NZL)
+        out = right(split(val), pay_ref[...])
+        for k in range(4):
+            piece = place(out[k * NYL : (k + 1) * NYL], 4 * c + k, lane)
+            acc = piece if acc is None else acc + piece
+    val = left(ty_ref[...], split(cval[...]))
+    cout[...] = val
+    cols[...] = acc + right(split(val), zc_ref[...])
+
+
+def z_columns_z():
+    mat = np.zeros((128, 128))
     for x in range(NXL):
-        pair = split(left(ty_ref[...], split(r_ref[x])))
-        r2[x] = right(pair, tz_ref[...])
-        piece = place(right(pair, pay_ref[...]), x, lane)
-        acc = piece if acc is None else acc + piece
-        rolled = pltpu.roll(hcols[...], (-2 * (48 + x)) % 128, 1)
-        field = z4[x]
-        vu[x, :, 0:128] = left(fy_ref[...], split(field[:, 0:128] + jnp.where(lane == 0, rolled, 0.0)))
-        vu[x, :, 128:256] = left(fy_ref[...], split(field[:, 128:256] + jnp.where(lane == 127, rolled, 0.0)))
-    cols[...] = acc
+        for side, node in ((0, NZL - 1), (1, 0)):
+            at = 2 * x + side
+            mat[at, at], mat[32 + at, at] = 1.0, LZ.res[node, node]
+            mat[at, 32 + at] = LZ.face[node, node]
+            mat[32 + at, 32 + at] = LZ.face[node] @ LZ.res[:, node]
+    return mat
 
 
 def y_spread():
@@ -407,16 +467,16 @@
 def face_z2_kernel(
     cols_ref, own_lo, own_hi, lo_ref, hi_ref, rx_ref, rz_ref, pay_ref, ay_ref, cols, rows_ref
 ):
-    sides = ((own_lo, lo_ref), (own_hi, hi_ref))
+    both = ((own_lo, lo_ref), (own_hi, hi_ref))
     flux = []
-    for own, ref in sides:
+    for own, ref in both:
         s = [own[q] + ref[q] for q in range(3)]
         nu = eddy(*s)
         flux.append([nu * v for v in s])
     along_x = left(rx_ref[...], split(jnp.concatenate([flux[0][0], flux[1][0]], axis=1)))
     along_z = right(split(jnp.concatenate([flux[0][2], flux[1][2]], axis=0)), rz_ref[...])
     vals = []
-    for s, (own, ref) in enumerate(sides):
+    for s, (own, ref) in enumerate(both):
         tau = along_x[:, s * NZL : (s + 1) * NZL] + along_z[s * NXL : (s + 1) * NXL]
         vals += [tau, flux[s][1], ref[3], ref[4]]
     for k, val in enumerate(vals):
@@ -425,64 +485,86 @@
     lane16 = lane_iota(NXL)
     row16 = lax.broadcasted_iota(jnp.int32, (NXL, 128), 0)
     keep = ((lane16 % 32) // 2) == row16
-    acc = cols_ref[...]
+    vecs = []
     for k in range(8):
         val = pay[16 * k : 16 * k + 16]
         moved = val
         for bit in (1, 2, 4, 8):
             moved = jnp.where((row16 & bit) != 0, pltpu.roll(moved, 2 * bit, 1), moved)
         vec = jnp.sum(jnp.where(keep, moved, 0.0), axis=0, keepdims=True)
-        acc = acc + ay_ref[:, k : k + 1] * vec
-    cols[...] = acc
-
-
-def spread_kernel(r2, vu, rows_ref, lo_ref, hi_ref, ay_ref, tz_ref, out, vout, pay_lo, pay_hi, zr):
+        vecs.append(vec)
+    for rows, ks in ((slice(0, 24), range(4)), (slice(NYL - 24, NYL), range(4, 8))):
+        acc = cols_ref[rows, :]
+        for k in ks:
+            acc = acc + ay_ref[rows, k : k + 1] * vecs[k]
+        cols[rows, :] = acc
+    cols[24 : NYL - 24, :] = cols_ref[24 : NYL - 24, :]
+
+
+def spread_kernel(
+    r1, z4, hcols, rows_ref, lo_ref, hi_ref, ay_ref, fy_ref, tz_ref, out, vout, pay_lo, pay_hi, zr
+):
     zr[...] = right(split(rows_ref[...].reshape(8 * NXL, NZL)), tz_ref[...]).reshape(8, NXL, NZL)
+    lane = lane_iota(NYL)
     row8 = lax.broadcasted_iota(jnp.int32, (8, NZL), 0)
+    for c in range(4):
+        xs = slice(4 * c, 4 * c + 4)
+        val = r1[xs].reshape(4 * NYL, NZL)
+        out[xs] = right(split(val), tz_ref[...]).reshape(4, NYL, NZL)
+        for x in range(4 * c, 4 * c + 4):
+            rolled = pltpu.roll(hcols[...], (-2 * (48 + x) - 1) % 128, 1)
+            field = jnp.concatenate(
+                [
+                    z4[x, :, 0:128] + jnp.where(lane == 0, rolled, 0.0),
+                    z4[x, :, 128:256] + jnp.where(lane == 127, rolled, 0.0),
+                ],
+                axis=1,
+            )
+            vout[x] = left(fy_ref[...], split(field))
+    for x in range(NXL):
+        one = slice(x, x + 1)
+        for t in (0, 1, 2, TILES - 3, TILES - 2, TILES - 1):
+            rows = slice(t * 8, t * 8 + 8)
+            val = out[x, rows, :]
+            for k in range(4) if t < 3 else range(4, 8):
+                if np.any(SPREAD[rows, k]):
+                    val = val + ay_ref[rows, k : k + 1] * zr[k, one, :]
+            out[x, rows, :] = val
+        low, high = slice(0, 8), slice(NYL - 8, NYL)
+        vout[x, low, :] = vout[x, low, :] + jnp.where(row8 == 0, lo_ref[5, one, :], 0.0)
+        vout[x, high, :] = vout[x, high, :] + jnp.where(row8 == 7, hi_ref[5, one, :], 0.0)
     for t in range(TILES):
         rows = slice(t * 8, t * 8 + 8)
-        r, w = [], []
-        for x in range(NXL):
-            one = slice(x, x + 1)
-            val, wal = r2[x, rows, :], vu[x, rows, :]
-            if t in (0, 1, 2, TILES - 3, TILES - 2, TILES - 1):
-                for k in range(4):
-                    k = k if t < 3 else k + 4
-                    if np.any(SPREAD[rows, k]):
-                        val = val + ay_ref[rows, k : k + 1] * zr[k, one, :]
-                out[x, rows, :] = val
-            else:
-                out[x, rows, :] = val
-            if t == 0:
-                wal = wal + jnp.where(row8 == 0, lo_ref[5, one, :], 0.0)
-            if t == TILES - 1:
-                wal = wal + jnp.where(row8 == 7, hi_ref[5, one, :], 0.0)
-            vout[x, rows, :] = wal
-            r.append(val)
-            w.append(wal)
-        a = [s + v for s, v in zip(average_x(r), w)]
+        r = [out[x, rows, :] for x in range(NXL)]
+        a = [s + vout[x, rows, :] for x, s in enumerate(average_x(r))]
         pay_lo[0, rows, :] = r[0]
         pay_hi[0, rows, :] = r[15]
         pay_lo[1, rows, :] = sum(float(FM[0, j]) * a[j] for j in range(8))
         pay_hi[1, rows, :] = sum(float(FM[7, j]) * a[8 + j] for j in range(8))
 
 
+def z_vectors():
+    vecs = [[LZ.halo[0], LZ.halo[2]], [LZ.halo[1], LZ.halo[3]]]
+    vecs.append([LZ.both[:, -1], LZ.both[:, 0]])
+    vecs.append([LZ.both @ LZ.res[:, -1], LZ.both @ LZ.res[:, 0]])
+    return vecs
+
+
 def z_spread():
     add = np.zeros((128, NZL))
-    add[0], add[32], add[1], add[33] = LZ.halo
+    for q, pair in enumerate(z_vectors()):
+        for side in range(2):
+            add[32 * q + side] = pair[side]
     return add
 
 
 def z_to_x():
     out = np.zeros((128, 4 * NZL))
-    low = np.zeros(16)
-    low[:] = LX.face[0]
-    high = LX.face[-1]
+    low, high = LX.face[0], LX.face[-1]
     for x in range(NXL):
-        for q in range(2):
+        for q, pair in enumerate(z_vectors()):
             for side in range(2):
-                lane = 2 * (16 * q + x) + side
-                vec = LZ.halo[2 * side + q]
+                lane, vec = 2 * (16 * q + x) + side, pair[side]
                 if x == 0:
                     out[lane, 0:NZL] = vec
                 if x == NXL - 1:
@@ -492,15 +574,16 @@
     return out
 
 
-def face_x2_kernel(par, near, far, lo_ref, hi_ref, mat_ref, pay_lo, pay_hi, hs):
-    low, high = received(par, near, far)
-    halo = jnp.where((lane_iota(NYL) % 2) == 0, low, high)
+def face_x2_kernel(near, far, cval, lo_ref, hi_ref, mat_ref, pay_lo, pay_hi, hs):
+    low, high = received(near, far)
+    lane = lane_iota(NYL)
+    halo = jnp.where((lane % 2) == 0, low, high)
+    halo = jnp.where(lane < 64, halo, pltpu.roll(cval[...], 64, 1))
     hs[...] = halo
     add = right(split(halo), mat_ref[...])
-    pay_lo[0] = lo_ref[0] + add[:, 0:NZL]
-    pay_lo[1] = lo_ref[1] + add[:, NZL : 2 * NZL]
-    pay_hi[0] = hi_ref[0] + add[:, 2 * NZL : 3 * NZL]
-    pay_hi[1] = hi_ref[1] + add[:, 3 * NZL :]
+    for q in range(2):
+        pay_lo[q] = lo_ref[q] + add[:, q * NZL : (q + 1) * NZL]
+        pay_hi[q] = hi_ref[q] + add[:, (q + 2) * NZL : (q + 3) * NZL]
 
 
 def local_x_kernel(r2, vu, hs, add_ref, out):
@@ -557,7 +640,6 @@
     face_x = (2, NYL, NZL)
     face_y = (6, NXL, NZL)
     colshape = (NYL, 128)
-    par = (lax.axis_index("gz") % 2).astype(jnp.int32).reshape(1, 1)
 
     sz, dz, fz = exact_right(LZ.avg.T), on_right(LZ.grad.T), on_right(LZ.filt.T)
     sy, dy, fy = exact_left(LY.avg), on_left(LY.grad), on_left(LY.filt)
@@ -569,43 +651,54 @@
     ay = jnp.asarray(SPREAD.astype(np.float32))
     ty, tz = on_left(LY.both), on_right(LZ.both.T)
 
-    u, lo, hi = call(
-        face_x_kernel, [full, face_x, face_x], u, hbm=(0,),
-        scratch=[pltpu.SemaphoreType.DMA((8,))], name="face_x",
-    )
-    xlo, xhi = exchange(lo, hi, "gx")
+    ulo, uhi = u[:8], u[8:]
+    hi = call(face_hi_kernel, face_x, uhi, name="face_hi")
+    xlo = shift(hi, "gx", 1)
+    lo = call(face_lo_kernel, face_x, ulo, name="face_lo")
+    xhi = shift(lo, "gx", -1)
     z1, z2, z3, z4, cols = call(
-        local_z_kernel, [full] * 4 + [colshape], u, sz, dz, fz,
+        local_z_kernel, [full] * 4 + [colshape], ulo, uhi, sz, dz, fz,
         flops=3 * 10**9, nbytes=8 * 10**6, name="local_z",
     )
-    dlt, cols = call(face_z_kernel, [(2, 3, NYL, NZL), colshape], xlo, xhi, cols, sz, dz, name="face_z")
+    h = call(
+        product_kernel, (3,) + full, ulo, uhi, velocity, cols, flops=10**9, nbytes=8 * 10**6, name="product"
+    )
+    inner = (NXL - 2, NYL, NZL)
+    sx_, sy_, sz_ = call(
+        local_y_kernel, [inner] * 3, z1, z2, z3, sy, dy,
+        flops=10**9, nbytes=9 * 10**6, name="local_y",
+    )
+    dlt, cols = call(
+        face_z_kernel, [(2, 3, NYL, NZL), colshape], xlo, xhi, cols, sz, dz, name="face_z"
+    )
     near, far = swap(cols, "gz", 0), swap(cols, "gz", 1)
-    sx_, sy_, sz_ = call(
-        local_y_kernel, [full] * 3, z1, z2, z3, dlt, sy, dy,
-        flops=10**9, nbytes=9 * 10**6, name="local_y",
-    )
-    r, lo, hi, hcols = call(
-        residue_kernel, [full, face_y, face_y, colshape],
-        par, near, far, sx_, sy_, sz_, z4, u, velocity, sy, dy, ry, rz, smem=(0,),
-        scratch=[pltpu.VMEM(full, F32)] + [pltpu.VMEM(full, BF)] * 2,
-        flops=2 * 10**9, nbytes=12 * 10**6, name="residue",
+    r, lo, hi = call(
+        residue_kernel, [full, face_y, face_y],
+        sx_, sy_, sz_, z1, z2, z3, z4, dlt, h, sy, dy, ry, rz,
+        scratch=[pltpu.VMEM(full, F32)] + [pltpu.VMEM(full, BF)] * 2 + [pltpu.VMEM((2, 3, NYL, NZL), F32)],
+        flops=3 * 10**9, nbytes=12 * 10**6, name="residue",
+    )
+    lo, hi, cval, hcols = call(
+        face_y_kernel, [face_y, face_y, colshape, colshape], near, far, cols, lo, hi, sy, dy, ry,
+        on_right(z_columns_x()), on_right(z_face_vectors()), on_left(y_rows()), name="face_y",
     )
     ylo, yhi = exchange(lo, hi, "gy")
-    r2, vu, cols = call(
-        filter_kernel, [full, full, colshape], r, z4, hcols, ty, fy, pay, tz,
+    r1, cols, cval = call(
+        filter_kernel, [full, colshape, colshape], r, cval, ty, pay, on_right(z_columns_z()),
         flops=2 * 10**9, nbytes=9 * 10**6, name="filter",
     )
     cols, rows = call(
-        face_z2_kernel, [colshape, (8, NXL, NZL)], cols, lo, hi, ylo, yhi, rx, rz, pay, ay, name="face_z2"
+        face_z2_kernel, [colshape, (8, NXL, NZL)], cols, lo, hi, ylo, yhi, rx, rz, pay, ay,
+        name="face_z2",
     )
     near, far = swap(cols, "gz", 0), swap(cols, "gz", 1)
     r2, vu, lo, hi = call(
-        spread_kernel, [full, full, face_x, face_x], r2, vu, rows, ylo, yhi, ay, tz,
-        scratch=[pltpu.VMEM((8, NXL, NZL), F32)], flops=10**9, nbytes=6 * 10**6, name="spread",
+        spread_kernel, [full, full, face_x, face_x], r1, z4, hcols, rows, ylo, yhi, ay, fy, tz,
+        scratch=[pltpu.VMEM((8, NXL, NZL), F32)], flops=2 * 10**9, nbytes=9 * 10**6, name="spread",
     )
     lo, hi, hs = call(
-        face_x2_kernel, [face_x, face_x, colshape], par, near, far, lo, hi, on_right(z_to_x()),
-        smem=(0,), name="face_x2",
+        face_x2_kernel, [face_x, face_x, colshape], near, far, cval, lo, hi, on_right(z_to_x()),
+        name="face_x2",
     )
     xlo, xhi = exchange(lo, hi, "gx")
     val = call(

time: 42.3 us -> 39.6 us (0.936)
  waiting for transfers between devices: 11.4 us -> 8.67 us
  Pallas kernels: 17.4 us -> 14.7 us
  starting transfers between devices: 11.6 us -> 13.5 us
  local copies, waits for them, and re-layouts: 1.5 us -> 2.15 us
    pallas_call x11 -> x14, Pallas kernels: 17.4 us -> 14.7 us  [call(): pl.pallas_call(kernel, out_shape=shapes, in_specs=[kinds.get(i, VM) for i...]
    ppermute x4, starting transfers between devices: 4.17 us -> 5.89 us  [swap(): return lax.ppermute(val, axis, pairs + [(b, a) for a, b in pairs])]
    ppermute x4, waiting for transfers between devices: 3.51 us -> 1.98 us  [swap(): return lax.ppermute(val, axis, pairs + [(b, a) for a, b in pairs])]
    slice x0 -> x1, local copies, waits for them, and re-layouts: none -> 1.51 us  [on_device(): ulo, uhi = (u[:8], u[8:])]
    ppermute x6, waiting for transfers between devices: 7.89 us -> 6.69 us  [shift(): lax.ppermute(val, axis, [(i, (i + step) % count) for i in range(count)])]
    unnamed x34 -> x40, local copies, waits for them, and re-layouts: 1.5 us -> 0.63 us
  transfers between devices with their start and end apart: 10 -> 10, of which waited for: 7 -> 6; matrix products, arithmetic and copies ran while one was open for 0% -> 0% of each run, Pallas kernels for 25% -> 28%
where the time goes in v1:
time: 39.6 us; the launch traced here: 39.4 us
  Pallas kernels  14.7 us (37%)
  starting transfers between devices  13.5 us (34%)
  waiting for transfers between devices  8.67 us (22%)
  local copies, waits for them, and re-layouts  2.15 us (5%)
  between operations  0.46 us (1%)
    pallas_call x14, Pallas kernels, call(): pl.pallas_call(kernel, out_shape=shapes, in_specs=[kinds.get(i, VM) for i...  14.7 us
    ppermute x6, starting transfers between devices, shift(): lax.ppermute(val, axis, [(i, (i + step) % count) for i in range(count)])  7.56 us
    ppermute x6, waiting for transfers between devices, shift(): lax.ppermute(val, axis, [(i, (i + step) % count) for i in range(count)])  6.69 us
    ppermute x4, starting transfers between devices, swap(): return lax.ppermute(val, axis, pairs + [(b, a) for a, b in pairs])  5.89 us
    ppermute x4, waiting for transfers between devices, swap(): return lax.ppermute(val, axis, pairs + [(b, a) for a, b in pairs])  1.98 us
    slice x1, local copies, waits for them, and re-layouts, on_device(): ulo, uhi = (u[:8], u[8:])  1.51 us
  transfers between devices with their start and end apart: 10, of which 6 were waited for; matrix products, arithmetic and copies ran while one was open for 0% of the time, Pallas kernels for 28%

profile of v1, /device:TPU:6, one launch (start us, length us, event | category | flops | bytes accessed | tf_op | source)
XLA Modules:
  0.0 39.4 jit_solution(18114554957438994693)
XLA Ops:
  0.0 1.5 %fusion = (f32[8,96,256]{2,1,0:T(8,128)S(1)}, f32[8,96,256]{2,1,0:T(8,128)S(1)}) fusion(f32[16,96,256]{2,1,0:T(8,128)} %param.21), kind=kLoop, calls=%fused_computation | loop fusion | bytes 3145728 | tf_op jit(solution)/shard_map/slice | solution.py:654
  1.6 0.5 %collective-permute-start = (f32[2,96,256]{2,1,0:T(8,128)S(1)}, f32[2,96,256]{2,1,0:T(8,128)S(1)}, u32[]{:S(2)}, u32[]{:S(2)}) collective-permute-start(f32[2,96,256]{2,1,0:T(8,128)S(1)} %face_hi.1), channel_id=1, source_target_pairs={{0,32},{32,64},{64,96},{96,0},{1,33},{33,65},{65,97},{97,1},{2,34}... | collective-permute-start | bytes 589832 | tf_op jit(solution)/shard_map/ppermute | solution.py:625
  2.2 1.7 %collective-permute-start.1 = (f32[2,96,256]{2,1,0:T(8,128)S(1)}, f32[2,96,256]{2,1,0:T(8,128)S(1)}, u32[]{:S(2)}, u32[]{:S(2)}) collective-permute-start(f32[2,96,256]{2,1,0:T(8,128)S(1)} %face_lo.1), channel_id=1, source_target_pairs={{0,96},{32,0},{64,32},{96,64},{1,97},{33,1},{65,33},{97,65},{2,98}... | collective-permute-start | bytes 589832 | tf_op jit(solution)/shard_map/ppermute | solution.py:625
  3.9 2.6 %local_z.1 = (f32[16,96,256]{2,1,0:T(8,128)S(1)}, f32[16,96,256]{2,1,0:T(8,128)S(1)}, f32[16,96,256]{2,1,0:T(8,128)S(1)}, f32[16,96,256]{2,1,0:T(8,128)S(1)}, f32[96,128]{1,0:T(8,128)S(1)}) custom-call(f32[8,96,256]{2,1,0:T(8,128)S(1)} %get-tuple-element.64.ulo_ref.u_ref, f32[8,96,256]{2,1,0:T(8,128)S(1)} %get-tuple-element.63.uhi_ref.u_ref, ...), custom_call_target="tpu_custom_call" | custom-call | flops 3000000000 | bytes 8000000 | tf_op jit(solution)/shard_map/local_z/pallas_call | solution.py:156
  6.9 0.5 %copy-done.3 = bf16[96,288]{1,0:T(8,128)(2,1)S(1)} copy-done((bf16[96,288]{1,0:T(8,128)(2,1)S(1)}, bf16[96,288]{1,0:T(8,128)(2,1)}, u32[]{:S(2)}) %copy-start.3) | copy-done | bytes 55320
  7.4 1.0 %local_y.1 = (f32[14,96,256]{2,1,0:T(8,128)S(1)}, f32[14,96,256]{2,1,0:T(8,128)S(1)}, f32[14,96,256]{2,1,0:T(8,128)S(1)}) custom-call(f32[16,96,256]{2,1,0:T(8,128)S(1)} %get-tuple-element.34.z1, f32[16,96,256]{2,1,0:T(8,128)S(1)} %get-tuple-element.35.z2, f32[16,96,256]{2,1,0:T(8,128)S(1)} %get-tuple-element.36.z3, bf16[96,192]{1,0:T(8,128)(2,1)S(1)} %copy-done.4, ...), custom_call_target="tpu_custom_call" | custom-call | flops 1000000000 | bytes 9000000 | tf_op jit(solution)/shard_map/local_y/pallas_call | solution.py:156
  8.4 1.3 %collective-permute-done.1.hi_ref = f32[2,96,256]{2,1,0:T(8,128)S(1)} collective-permute-done((f32[2,96,256]{2,1,0:T(8,128)S(1)}, f32[2,96,256]{2,1,0:T(8,128)S(1)}, u32[]{:S(2)}, u32[]{:S(2)}) %collective-permute-start.1) | collective-permute-done | bytes 196640 | tf_op jit(solution)/shard_map/ppermute | solution.py:625
  9.7 0.4 %face_z.1 = (f32[2,3,96,256]{3,2,1,0:T(8,128)S(1)}, f32[96,128]{1,0:T(8,128)S(1)}) custom-call(f32[2,96,256]{2,1,0:T(8,128)S(1)} %collective-permute-done.lo_ref, f32[2,96,256]{2,1,0:T(8,128)S(1)} %collective-permute-done.1.hi_ref, f32[96,128]{1,0:T(8,128)S(1)} %get-tuple-element.41.cols_ref.after_ref, bf16[512,256]{1,0:T(8,128)(2,1)S(1)} %copy-done.7, ...), custom_call_target="tpu_custom_call" | custom-call | tf_op jit(solution)/shard_map/face_z/pallas_call | solution.py:156
  10.2 4.3 %collective-permute-start.3 = (f32[96,128]{1,0:T(8,128)S(1)}, f32[96,128]{1,0:T(8,128)S(1)}, u32[]{:S(2)}, u32[]{:S(2)}) collective-permute-start(f32[96,128]{1,0:T(8,128)S(1)} %get-tuple-element.44.cols), channel_id=1, source_target_pairs={{1,2},{3,4},{5,6},{7,0},{2,1},{4,3},{6,5},{0,7},{9,10},{11,12},{13... | collective-permute-start | bytes 147464 | tf_op jit(solution)/shard_map/ppermute | solution.py:635
  14.6 2.8 %residue.1 = (f32[16,96,256]{2,1,0:T(8,128)S(1)}, f32[6,16,256]{2,1,0:T(8,128)S(1)}, f32[6,16,256]{2,1,0:T(8,128)S(1)}) custom-call(f32[14,96,256]{2,1,0:T(8,128)S(1)} %get-tuple-element.37.sx_, f32[14,96,256]{2,1,0:T(8,128)S(1)} %get-tuple-element.38.sy_, f32[14,96,256]{2,1,0:T(8,128)S(1)} %get-tuple-element.39.sz_, ...), custom_call_target="tpu_custom_call" | custom-call | flops 3000000000 | bytes 12000000 | tf_op jit(solution)/shard_map/residue/pallas_call | solution.py:156
  17.5 0.9 %face_y.1 = (f32[6,16,256]{2,1,0:T(8,128)S(1)}, f32[6,16,256]{2,1,0:T(8,128)S(1)}, f32[96,128]{1,0:T(8,128)S(1)}, f32[96,128]{1,0:T(8,128)S(1)}) custom-call(f32[96,128]{1,0:T(8,128)S(1)} %collective-permute-done.2.near, f32[96,128]{1,0:T(8,128)S(1)} %collective-permute-done.3.far, f32[96,128]{1,0:T(8,128)S(1)} %get-tuple-element.44.cols, ...), custom_call_target="tpu_custom_call" | custom-call | tf_op jit(solution)/shard_map/face_y/pallas_call | solution.py:156
  18.4 1.6 %collective-permute-start.4 = (f32[6,16,256]{2,1,0:T(8,128)S(1)}, f32[6,16,256]{2,1,0:T(8,128)S(1)}, u32[]{:S(2)}, u32[]{:S(2)}) collective-permute-start(f32[6,16,256]{2,1,0:T(8,128)S(1)} %get-tuple-element.52.own_hi), channel_id=1, source_target_pairs={{0,8},{8,16},{16,24},{24,0},{1,9},{9,17},{17,25},{25,1},{2,10},{10... | collective-permute-start | bytes 294920 | tf_op jit(solution)/shard_map/ppermute | solution.py:625
  20.0 1.7 %collective-permute-start.5 = (f32[6,16,256]{2,1,0:T(8,128)S(1)}, f32[6,16,256]{2,1,0:T(8,128)S(1)}, u32[]{:S(2)}, u32[]{:S(2)}) collective-permute-start(f32[6,16,256]{2,1,0:T(8,128)S(1)} %get-tuple-element.51.own_lo), channel_id=1, source_target_pairs={{0,24},{8,0},{16,8},{24,16},{1,25},{9,1},{17,9},{25,17},{2,26},{10... | collective-permute-start | bytes 294920 | tf_op jit(solution)/shard_map/ppermute | solution.py:625
  21.7 1.5 %filter.1 = (f32[16,96,256]{2,1,0:T(8,128)S(1)}, f32[96,128]{1,0:T(8,128)S(1)}, f32[96,128]{1,0:T(8,128)S(1)}) custom-call(f32[16,96,256]{2,1,0:T(8,128)S(1)} %get-tuple-element.43.r_ref, f32[96,128]{1,0:T(8,128)S(1)} %get-tuple-element.47.cval, bf16[96,288]{1,0:T(8,128)(2,1)S(1)} %copy-done.19, bf16[768,128]{1,0:T(8,128)(2,1)S(1)} %copy-done.10, ...), custom_call_target="tpu_custom_call" | custom-call | flops 2000000000 | bytes 9000000 | tf_op jit(solution)/shard_map/filter/pallas_call | solution.py:156
  23.2 1.1 %collective-permute-done.4.lo_ref = f32[6,16,256]{2,1,0:T(8,128)S(1)} collective-permute-done((f32[6,16,256]{2,1,0:T(8,128)S(1)}, f32[6,16,256]{2,1,0:T(8,128)S(1)}, u32[]{:S(2)}, u32[]{:S(2)}) %collective-permute-start.4) | collective-permute-done | bytes 98336 | tf_op jit(solution)/shard_map/ppermute | solution.py:625
  24.6 0.8 %face_z2.1 = (f32[96,128]{1,0:T(8,128)S(1)}, f32[8,16,256]{2,1,0:T(8,128)S(1)}) custom-call(f32[96,128]{1,0:T(8,128)S(1)} %get-tuple-element.50.cols_ref, f32[6,16,256]{2,1,0:T(8,128)S(1)} %get-tuple-element.51.own_lo, f32[6,16,256]{2,1,0:T(8,128)S(1)} %get-tuple-element.52.own_hi, f32[6,16,256]{2,1,0:T(8,128)S(1)} %collective-permute-done.4.lo_ref, ...), custom_call_target="tpu_custom_call" | custom-call | tf_op jit(solution)/shard_map/face_z2/pallas_call | solution.py:156
  25.5 1.4 %collective-permute-start.7 = (f32[96,128]{1,0:T(8,128)S(1)}, f32[96,128]{1,0:T(8,128)S(1)}, u32[]{:S(2)}, u32[]{:S(2)}) collective-permute-start(f32[96,128]{1,0:T(8,128)S(1)} %get-tuple-element.56), channel_id=1, source_target_pairs={{1,2},{3,4},{5,6},{7,0},{2,1},{4,3},{6,5},{0,7},{9,10},{11,12},{13... | collective-permute-start | bytes 147464 | tf_op jit(solution)/shard_map/ppermute | solution.py:635
  26.9 1.6 %spread.1 = (f32[16,96,256]{2,1,0:T(8,128)S(1)}, f32[16,96,256]{2,1,0:T(8,128)S(1)}, f32[2,96,256]{2,1,0:T(8,128)S(1)}, f32[2,96,256]{2,1,0:T(8,128)S(1)}) custom-call(f32[16,96,256]{2,1,0:T(8,128)S(1)} %get-tuple-element.48.r1, f32[16,96,256]{2,1,0:T(8,128)S(1)} %get-tuple-element.40.z4, f32[96,128]{1,0:T(8,128)S(1)} %get-tuple-element.49.hcols, ...), custom_call_target="tpu_custom_call" | custom-call | flops 2000000000 | bytes 9000000 | tf_op jit(solution)/shard_map/spread/pallas_call | solution.py:156
  28.5 2.0 %collective-permute-done.7.far = f32[96,128]{1,0:T(8,128)S(1)} collective-permute-done((f32[96,128]{1,0:T(8,128)S(1)}, f32[96,128]{1,0:T(8,128)S(1)}, u32[]{:S(2)}, u32[]{:S(2)}) %collective-permute-start.7) | collective-permute-done | bytes 49184 | tf_op jit(solution)/shard_map/ppermute | solution.py:635
  31.2 1.7 %collective-permute-start.9 = (f32[2,96,256]{2,1,0:T(8,128)S(1)}, f32[2,96,256]{2,1,0:T(8,128)S(1)}, u32[]{:S(2)}, u32[]{:S(2)}) collective-permute-start(f32[2,96,256]{2,1,0:T(8,128)S(1)} %get-tuple-element.62), channel_id=1, source_target_pairs={{0,96},{32,0},{64,32},{96,64},{1,97},{33,1},{65,33},{97,65},{2,98}... | collective-permute-start | bytes 589832 | tf_op jit(solution)/shard_map/ppermute | solution.py:625
  32.9 1.2 %local_x.1.val_ref = f32[16,96,256]{2,1,0:T(8,128)S(1)} custom-call(f32[16,96,256]{2,1,0:T(8,128)S(1)} %get-tuple-element.54.r2, f32[16,96,256]{2,1,0:T(8,128)S(1)} %get-tuple-element.55.vu, f32[96,128]{1,0:T(8,128)S(1)} %get-tuple-element.60.hs, bf16[384,256]{1,0:T(8,128)(2,1)S(1)} %copy-done.8), custom_call_target="tpu_custom_call" | custom-call | flops 1000000000 | bytes 6000000 | tf_op jit(solution)/shard_map/local_x/pallas_call | solution.py:156
  34.1 2.6 %collective-permute-done.8.lo_ref = f32[2,96,256]{2,1,0:T(8,128)S(1)} collective-permute-done((f32[2,96,256]{2,1,0:T(8,128)S(1)}, f32[2,96,256]{2,1,0:T(8,128)S(1)}, u32[]{:S(2)}, u32[]{:S(2)}) %collective-permute-start.8) | collective-permute-done | bytes 196640 | tf_op jit(solution)/shard_map/ppermute | solution.py:625
  36.7 1.3 %collective-permute-done.9.hi_ref = f32[2,96,256]{2,1,0:T(8,128)S(1)} collective-permute-done((f32[2,96,256]{2,1,0:T(8,128)S(1)}, f32[2,96,256]{2,1,0:T(8,128)S(1)}, u32[]{:S(2)}, u32[]{:S(2)}) %collective-permute-start.9) | collective-permute-done | bytes 196640 | tf_op jit(solution)/shard_map/ppermute | solution.py:625
  38.0 1.2 %final.1 = f32[16,96,256]{2,1,0:T(8,128)} custom-call(f32[16,96,256]{2,1,0:T(8,128)S(1)} %local_x.1.val_ref, f32[2,96,256]{2,1,0:T(8,128)S(1)} %collective-permute-done.8.lo_ref, f32[2,96,256]{2,1,0:T(8,128)S(1)} %collective-permute-done.9.hi_ref), custom_call_target="tpu_custom_call" | custom-call | tf_op jit(solution)/shard_map/final/pallas_call | solution.py:156
  (51 shorter events, 1.8 us)
Async XLA Ops:
  1.6 6.8 %collective-permute-start = (f32[2,96,256]{2,1,0:T(8,128)S(1)}, f32[2,96,256]{2,1,0:T(8,128)S(1)}, u32[]{:S(2)}, u32[]{:S(2)}) collective-permute-start(f32[2,96,256]{2,1,0:T(8,128)S(1)} %face_hi.1), channel_id=1, source_target_pairs={{0,32},{32,64},{64,96},{96,0},{1,33},{33,65},{65,97},{97,1},{2,34}... | collective-permute-start | bytes 589832 | tf_op jit(solution)/shard_map/ppermute | solution.py:625
  2.2 7.5 %collective-permute-start.1 = (f32[2,96,256]{2,1,0:T(8,128)S(1)}, f32[2,96,256]{2,1,0:T(8,128)S(1)}, u32[]{:S(2)}, u32[]{:S(2)}) collective-permute-start(f32[2,96,256]{2,1,0:T(8,128)S(1)} %face_lo.1), channel_id=1, source_target_pairs={{0,96},{32,0},{64,32},{96,64},{1,97},{33,1},{65,33},{97,65},{2,98}... | collective-permute-start | bytes 589832 | tf_op jit(solution)/shard_map/ppermute | solution.py:625
  7.4 7.1 %copy-start.1 = (bf16[768,256]{1,0:T(8,128)(2,1)S(1)}, bf16[768,256]{1,0:T(8,128)(2,1)}, u32[]{:S(2)}) copy-start(bf16[768,256]{1,0:T(8,128)(2,1)} %constant.45.clone.rz_ref) | copy-start | bytes 1179652
  7.4 7.1 %copy-start.6 = (bf16[96,288]{1,0:T(8,128)(2,1)S(1)}, bf16[96,288]{1,0:T(8,128)(2,1)}, u32[]{:S(2)}) copy-start(bf16[96,288]{1,0:T(8,128)(2,1)} %constant.44.clone.ry_ref) | copy-start | bytes 165892
  10.1 7.3 %collective-permute-start.2 = (f32[96,128]{1,0:T(8,128)S(1)}, f32[96,128]{1,0:T(8,128)S(1)}, u32[]{:S(2)}, u32[]{:S(2)}) collective-permute-start(f32[96,128]{1,0:T(8,128)S(1)} %get-tuple-element.44.cols), channel_id=1, source_target_pairs={{0,1},{2,3},{4,5},{6,7},{1,0},{3,2},{5,4},{7,6},{8,9},{10,11},{12,... | collective-permute-start | bytes 147464 | tf_op jit(solution)/shard_map/ppermute | solution.py:635
  10.2 7.2 %collective-permute-start.3 = (f32[96,128]{1,0:T(8,128)S(1)}, f32[96,128]{1,0:T(8,128)S(1)}, u32[]{:S(2)}, u32[]{:S(2)}) collective-permute-start(f32[96,128]{1,0:T(8,128)S(1)} %get-tuple-element.44.cols), channel_id=1, source_target_pairs={{1,2},{3,4},{5,6},{7,0},{2,1},{4,3},{6,5},{0,7},{9,10},{11,12},{13... | collective-permute-start | bytes 147464 | tf_op jit(solution)/shard_map/ppermute | solution.py:635
  14.5 2.9 %copy-start.9 = (bf16[384,256]{1,0:T(8,128)(2,1)S(1)}, bf16[384,256]{1,0:T(8,128)(2,1)}, u32[]{:S(2)}) copy-start(bf16[384,256]{1,0:T(8,128)(2,1)} %constant.52.clone.zv_ref) | copy-start | bytes 589828
  14.5 2.9 %copy-start.11 = (bf16[384,128]{1,0:T(8,128)(2,1)S(1)}, bf16[384,128]{1,0:T(8,128)(2,1)}, u32[]{:S(2)}) copy-start(bf16[384,128]{1,0:T(8,128)(2,1)} %constant.51.clone.rx_ref) | copy-start | bytes 294916
  14.6 2.9 %copy-start.13 = (bf16[8,288]{1,0:T(8,128)(2,1)S(1)}, bf16[8,288]{1,0:T(8,128)(2,1)}, u32[]{:S(2)}) copy-start(bf16[8,288]{1,0:T(8,128)(2,1)} %constant.53.clone.yr_ref) | copy-start | bytes 13828
  14.6 7.1 %copy-start.10 = (bf16[768,128]{1,0:T(8,128)(2,1)S(1)}, bf16[768,128]{1,0:T(8,128)(2,1)}, u32[]{:S(2)}) copy-start(bf16[768,128]{1,0:T(8,128)(2,1)} %constant.47.clone.pay_ref) | copy-start | bytes 589828
  14.6 7.1 %copy-start.17 = (bf16[384,128]{1,0:T(8,128)(2,1)S(1)}, bf16[384,128]{1,0:T(8,128)(2,1)}, u32[]{:S(2)}) copy-start(bf16[384,128]{1,0:T(8,128)(2,1)} %constant.54.clone.zc_ref) | copy-start | bytes 294916
  14.6 7.1 %copy-start.19 = (bf16[96,288]{1,0:T(8,128)(2,1)S(1)}, bf16[96,288]{1,0:T(8,128)(2,1)}, u32[]{:S(2)}) copy-start(bf16[96,288]{1,0:T(8,128)(2,1)} %constant.49.clone.ty_ref) | copy-start | bytes 165892
  18.4 5.9 %collective-permute-start.4 = (f32[6,16,256]{2,1,0:T(8,128)S(1)}, f32[6,16,256]{2,1,0:T(8,128)S(1)}, u32[]{:S(2)}, u32[]{:S(2)}) collective-permute-start(f32[6,16,256]{2,1,0:T(8,128)S(1)} %get-tuple-element.52.own_hi), channel_id=1, source_target_pairs={{0,8},{8,16},{16,24},{24,0},{1,9},{9,17},{17,25},{25,1},{2,10},{10... | collective-permute-start | bytes 294920 | tf_op jit(solution)/shard_map/ppermute | solution.py:625
  20.0 4.6 %collective-permute-start.5 = (f32[6,16,256]{2,1,0:T(8,128)S(1)}, f32[6,16,256]{2,1,0:T(8,128)S(1)}, u32[]{:S(2)}, u32[]{:S(2)}) collective-permute-start(f32[6,16,256]{2,1,0:T(8,128)S(1)} %get-tuple-element.51.own_lo), channel_id=1, source_target_pairs={{0,24},{8,0},{16,8},{24,16},{1,25},{9,1},{17,9},{25,17},{2,26},{10... | collective-permute-start | bytes 294920 | tf_op jit(solution)/shard_map/ppermute | solution.py:625
  21.7 2.9 %copy-start.12 = (f32[96,8]{1,0:T(8,128)S(1)}, f32[96,8]{1,0:T(8,128)}, u32[]{:S(2)}) copy-start(f32[96,8]{1,0:T(8,128)} %constant.48.clone.ay_ref) | copy-start | bytes 9220
  21.7 2.9 %copy-start.14 = (bf16[16,48]{1,0:T(8,128)(2,1)S(1)}, bf16[16,48]{1,0:T(8,128)(2,1)}, u32[]{:S(2)}) copy-start(bf16[16,48]{1,0:T(8,128)(2,1)} %constant.46.clone.rx_ref) | copy-start | bytes 4612
  21.7 5.2 %copy-start.15 = (bf16[768,256]{1,0:T(8,128)(2,1)S(1)}, bf16[768,256]{1,0:T(8,128)(2,1)}, u32[]{:S(2)}) copy-start(bf16[768,256]{1,0:T(8,128)(2,1)} %constant.50.clone.tz_ref) | copy-start | bytes 1179652
  21.7 5.2 %copy-start.18 = (bf16[96,288]{1,0:T(8,128)(2,1)S(1)}, bf16[96,288]{1,0:T(8,128)(2,1)}, u32[]{:S(2)}) copy-start(bf16[96,288]{1,0:T(8,128)(2,1)} %constant.43.clone.fy_ref) | copy-start | bytes 165892
  25.4 3.1 %collective-permute-start.6 = (f32[96,128]{1,0:T(8,128)S(1)}, f32[96,128]{1,0:T(8,128)S(1)}, u32[]{:S(2)}, u32[]{:S(2)}) collective-permute-start(f32[96,128]{1,0:T(8,128)S(1)} %get-tuple-element.56), channel_id=1, source_target_pairs={{0,1},{2,3},{4,5},{6,7},{1,0},{3,2},{5,4},{7,6},{8,9},{10,11},{12,... | collective-permute-start | bytes 147464 | tf_op jit(solution)/shard_map/ppermute | solution.py:635
  25.5 5.0 %collective-permute-start.7 = (f32[96,128]{1,0:T(8,128)S(1)}, f32[96,128]{1,0:T(8,128)S(1)}, u32[]{:S(2)}, u32[]{:S(2)}) collective-permute-start(f32[96,128]{1,0:T(8,128)S(1)} %get-tuple-element.56), channel_id=1, source_target_pairs={{1,2},{3,4},{5,6},{7,0},{2,1},{4,3},{6,5},{0,7},{9,10},{11,12},{13... | collective-permute-start | bytes 147464 | tf_op jit(solution)/shard_map/ppermute | solution.py:635
  26.9 3.6 %copy-start.2 = (bf16[384,1024]{1,0:T(8,128)(2,1)S(1)}, bf16[384,1024]{1,0:T(8,128)(2,1)}, u32[]{:S(2)}) copy-start(bf16[384,1024]{1,0:T(8,128)(2,1)} %constant.55.clone.mat_ref) | copy-start | bytes 2359300
  26.9 6.0 %copy-start.8 = (bf16[384,256]{1,0:T(8,128)(2,1)S(1)}, bf16[384,256]{1,0:T(8,128)(2,1)}, u32[]{:S(2)}) copy-start(bf16[384,256]{1,0:T(8,128)(2,1)} %constant.56.clone.add_ref) | copy-start | bytes 589828
  30.8 5.9 %collective-permute-start.8 = (f32[2,96,256]{2,1,0:T(8,128)S(1)}, f32[2,96,256]{2,1,0:T(8,128)S(1)}, u32[]{:S(2)}, u32[]{:S(2)}) collective-permute-start(f32[2,96,256]{2,1,0:T(8,128)S(1)} %get-tuple-element.61), channel_id=1, source_target_pairs={{0,32},{32,64},{64,96},{96,0},{1,33},{33,65},{65,97},{97,1},{2,34}... | collective-permute-start | bytes 589832 | tf_op jit(solution)/shard_map/ppermute | solution.py:625
  31.2 6.9 %collective-permute-start.9 = (f32[2,96,256]{2,1,0:T(8,128)S(1)}, f32[2,96,256]{2,1,0:T(8,128)S(1)}, u32[]{:S(2)}, u32[]{:S(2)}) collective-permute-start(f32[2,96,256]{2,1,0:T(8,128)S(1)} %get-tuple-element.62), channel_id=1, source_target_pairs={{0,96},{32,0},{64,32},{96,64},{1,97},{33,1},{65,33},{97,65},{2,98}... | collective-permute-start | bytes 589832 | tf_op jit(solution)/shard_map/ppermute | solution.py:625
  (6 other events, 11.4 us)

commit v2 on v1

--- a/solution.py
+++ b/solution.py
@@ -465,7 +465,7 @@
 
 
 def face_z2_kernel(
-    cols_ref, own_lo, own_hi, lo_ref, hi_ref, rx_ref, rz_ref, pay_ref, ay_ref, cols, rows_ref
+    cols_ref, after_ref, own_lo, own_hi, lo_ref, hi_ref, rx_ref, rz_ref, pay_ref, ay_ref, cols, rows_ref
 ):
     both = ((own_lo, lo_ref), (own_hi, hi_ref))
     flux = []
@@ -501,12 +501,8 @@
     cols[24 : NYL - 24, :] = cols_ref[24 : NYL - 24, :]
 
 
-def spread_kernel(
-    r1, z4, hcols, rows_ref, lo_ref, hi_ref, ay_ref, fy_ref, tz_ref, out, vout, pay_lo, pay_hi, zr
-):
-    zr[...] = right(split(rows_ref[...].reshape(8 * NXL, NZL)), tz_ref[...]).reshape(8, NXL, NZL)
+def filter_z_kernel(r1, z4, hcols, fy_ref, tz_ref, out, vout):
     lane = lane_iota(NYL)
-    row8 = lax.broadcasted_iota(jnp.int32, (8, NZL), 0)
     for c in range(4):
         xs = slice(4 * c, 4 * c + 4)
         val = r1[xs].reshape(4 * NYL, NZL)
@@ -521,26 +517,36 @@
                 axis=1,
             )
             vout[x] = left(fy_ref[...], split(field))
-    for x in range(NXL):
-        one = slice(x, x + 1)
-        for t in (0, 1, 2, TILES - 3, TILES - 2, TILES - 1):
-            rows = slice(t * 8, t * 8 + 8)
-            val = out[x, rows, :]
-            for k in range(4) if t < 3 else range(4, 8):
+
+
+def spread_kernel(
+    r2, vu, rows_ref, lo_ref, hi_ref, cval, ay_ref, tz_ref, mat_ref, out, vout, pay_lo, pay_hi, zr
+):
+    zr[...] = right(split(rows_ref[...].reshape(8 * NXL, NZL)), tz_ref[...]).reshape(8, NXL, NZL)
+    add = right(split(cval[...]), mat_ref[...])
+    row8 = lax.broadcasted_iota(jnp.int32, (8, NZL), 0)
+    for t in range(TILES):
+        rows = slice(t * 8, t * 8 + 8)
+        r, w = [], []
+        for x in range(NXL):
+            one = slice(x, x + 1)
+            val, wal = r2[x, rows, :], vu[x, rows, :]
+            for k in range(8):
                 if np.any(SPREAD[rows, k]):
                     val = val + ay_ref[rows, k : k + 1] * zr[k, one, :]
+            if t == 0:
+                wal = wal + jnp.where(row8 == 0, lo_ref[5, one, :], 0.0)
+            if t == TILES - 1:
+                wal = wal + jnp.where(row8 == 7, hi_ref[5, one, :], 0.0)
             out[x, rows, :] = val
-        low, high = slice(0, 8), slice(NYL - 8, NYL)
-        vout[x, low, :] = vout[x, low, :] + jnp.where(row8 == 0, lo_ref[5, one, :], 0.0)
-        vout[x, high, :] = vout[x, high, :] + jnp.where(row8 == 7, hi_ref[5, one, :], 0.0)
-    for t in range(TILES):
-        rows = slice(t * 8, t * 8 + 8)
-        r = [out[x, rows, :] for x in range(NXL)]
-        a = [s + vout[x, rows, :] for x, s in enumerate(average_x(r))]
-        pay_lo[0, rows, :] = r[0]
-        pay_hi[0, rows, :] = r[15]
-        pay_lo[1, rows, :] = sum(float(FM[0, j]) * a[j] for j in range(8))
-        pay_hi[1, rows, :] = sum(float(FM[7, j]) * a[8 + j] for j in range(8))
+            vout[x, rows, :] = wal
+            r.append(val)
+            w.append(wal)
+        a = [s + v for s, v in zip(average_x(r), w)]
+        low = sum(float(FM[0, j]) * a[j] for j in range(8))
+        high = sum(float(FM[7, j]) * a[8 + j] for j in range(8))
+        for q, (ref, val) in enumerate(((pay_lo, r[0]), (pay_lo, low), (pay_hi, r[15]), (pay_hi, high))):
+            ref[q % 2, rows, :] = val + add[rows, q * NZL : (q + 1) * NZL]
 
 
 def z_vectors():
@@ -562,7 +568,7 @@
     out = np.zeros((128, 4 * NZL))
     low, high = LX.face[0], LX.face[-1]
     for x in range(NXL):
-        for q, pair in enumerate(z_vectors()):
+        for q, pair in enumerate(z_vectors()[2:]):
             for side in range(2):
                 lane, vec = 2 * (16 * q + x) + side, pair[side]
                 if x == 0:
@@ -574,16 +580,59 @@
     return out
 
 
-def face_x2_kernel(near, far, cval, lo_ref, hi_ref, mat_ref, pay_lo, pay_hi, hs):
+def z_short():
+    out = np.zeros((128, 128))
+    low, high = LX.face[0], LX.face[-1]
+    for x in range(NXL):
+        for q in range(2):
+            for side in range(2):
+                lane, c = 2 * (16 * q + x) + side, 2 * q + side
+                if x == 0:
+                    out[lane, c] = 1.0
+                if x == NXL - 1:
+                    out[lane, 8 + c] = 1.0
+                out[lane, 4 + c], out[lane, 12 + c] = low[x], high[x]
+    return out
+
+
+def z_long():
+    out = np.zeros((16, 4 * NZL))
+    for q, pair in enumerate(z_vectors()[:2]):
+        for side in range(2):
+            for k in range(4):
+                out[4 * k + 2 * q + side, k * NZL : (k + 1) * NZL] = pair[side]
+    high, low = halves(out)
+    rest = np.zeros((80, 4 * NZL)).astype(jnp.bfloat16)
+    return jnp.asarray(np.concatenate([high, high, low, rest], axis=0))
+
+
+def forward_kernel(near, far, cval, mat_ref, flo, fhi, hs):
     low, high = received(near, far)
     lane = lane_iota(NYL)
     halo = jnp.where((lane % 2) == 0, low, high)
-    halo = jnp.where(lane < 64, halo, pltpu.roll(cval[...], 64, 1))
-    hs[...] = halo
-    add = right(split(halo), mat_ref[...])
-    for q in range(2):
-        pay_lo[q] = lo_ref[q] + add[:, q * NZL : (q + 1) * NZL]
-        pay_hi[q] = hi_ref[q] + add[:, (q + 2) * NZL : (q + 3) * NZL]
+    hs[...] = jnp.where(lane < 64, halo, pltpu.roll(cval[...], 64, 1))
+    short = right(split(halo), mat_ref[...])
+    lane8 = lane_iota(8)
+    for ref, base in ((flo, 0), (fhi, 8)):
+        acc = None
+        for t in range(TILES):
+            piece = pltpu.roll(short[8 * t : 8 * t + 8], (8 * t - base) % 128, 1)
+            piece = jnp.where((lane8 // 8) == t, piece, 0.0)
+            acc = piece if acc is None else acc + piece
+        ref[...] = acc
+
+
+def forwarded(glo, ghi, mat):
+    lane8 = lane_iota(8)
+    tiles = []
+    for t in range(TILES):
+        low = pltpu.roll(glo, (-8 * t) % 128, 1)
+        high = pltpu.roll(ghi, (8 - 8 * t) % 128, 1)
+        tiles.append(jnp.where(lane8 < 8, low, jnp.where(lane8 < 16, high, 0.0)))
+    val = jnp.concatenate(tiles, axis=0)
+    top = val.astype(BF).astype(F32)
+    val = top + pltpu.roll(val - top, 16, 1) + pltpu.roll(top, 32, 1)
+    return mm(val.astype(BF), mat)
 
 
 def local_x_kernel(r2, vu, hs, add_ref, out):
@@ -601,12 +650,14 @@
             out[k, rows, :] = f[k]
 
 
-def final_kernel(val_ref, lo_ref, hi_ref, out_hbm, buf, sems):
+def final_kernel(val_ref, lo_ref, hi_ref, glo_ref, ghi_ref, mat_ref, out_hbm, buf, sems):
     copies = []
+    add = forwarded(glo_ref[...], ghi_ref[...], mat_ref[...])
     for c in range(4):
         for t in range(3):
             rows = slice(c * 24 + t * 8, c * 24 + t * 8 + 8)
             halo = [lo_ref[0, rows, :], lo_ref[1, rows, :], hi_ref[0, rows, :], hi_ref[1, rows, :]]
+            halo = [v + add[rows, j * NZL : (j + 1) * NZL] for j, v in enumerate(halo)]
             for k in range(NXL):
                 val = val_ref[k, rows, :]
                 for j in range(4):
@@ -687,26 +738,29 @@
         filter_kernel, [full, colshape, colshape], r, cval, ty, pay, on_right(z_columns_z()),
         flops=2 * 10**9, nbytes=9 * 10**6, name="filter",
     )
+    r2, vu = call(
+        filter_z_kernel, [full, full], r1, z4, hcols, fy, tz, flops=2 * 10**9, nbytes=9 * 10**6, name="filter_z"
+    )
     cols, rows = call(
-        face_z2_kernel, [colshape, (8, NXL, NZL)], cols, lo, hi, ylo, yhi, rx, rz, pay, ay,
+        face_z2_kernel, [colshape, (8, NXL, NZL)], cols, r2, lo, hi, ylo, yhi, rx, rz, pay, ay,
         name="face_z2",
     )
     near, far = swap(cols, "gz", 0), swap(cols, "gz", 1)
     r2, vu, lo, hi = call(
-        spread_kernel, [full, full, face_x, face_x], r1, z4, hcols, rows, ylo, yhi, ay, fy, tz,
-        scratch=[pltpu.VMEM((8, NXL, NZL), F32)], flops=2 * 10**9, nbytes=9 * 10**6, name="spread",
-    )
-    lo, hi, hs = call(
-        face_x2_kernel, [face_x, face_x, colshape], near, far, cval, lo, hi, on_right(z_to_x()),
-        name="face_x2",
+        spread_kernel, [full, full, face_x, face_x], r2, vu, rows, ylo, yhi, cval, ay, tz, on_right(z_to_x()),
+        scratch=[pltpu.VMEM((8, NXL, NZL), F32)], flops=10**9, nbytes=9 * 10**6, name="spread",
     )
     xlo, xhi = exchange(lo, hi, "gx")
+    flo, fhi, hs = call(
+        forward_kernel, [(8, 128), (8, 128), colshape], near, far, cval, on_right(z_short()), name="forward"
+    )
+    glo, ghi = exchange(flo, fhi, "gx")
     val = call(
         local_x_kernel, full, r2, vu, hs, on_right(z_spread()),
-        flops=10**9, nbytes=6 * 10**6, name="local_x",
+        flops=10**11, nbytes=10**8, name="local_x",
     )
     return call(
-        final_kernel, full, val, xlo, xhi, hbm_out=True,
+        final_kernel, full, val, xlo, xhi, glo, ghi, z_long(), hbm_out=True,
         scratch=[pltpu.VMEM(full, F32), pltpu.SemaphoreType.DMA((4,))], name="final",
     )
 

time: 39.6 us -> 38.6 us (0.975)
  waiting for transfers between devices: 8.67 us -> 4.45 us
  starting transfers between devices: 13.5 us -> 15.8 us
  Pallas kernels: 14.7 us -> 15.6 us
    ppermute x6 -> x8, waiting for transfers between devices: 6.69 us -> 4.09 us  [shift(): lax.ppermute(val, axis, [(i, (i + step) % count) for i in range(count)])]
    ppermute x6 -> x8, starting transfers between devices: 7.56 us -> 9.69 us  [shift(): lax.ppermute(val, axis, [(i, (i + step) % count) for i in range(count)])]
    ppermute x4, waiting for transfers between devices: 1.98 us -> 0.36 us  [swap(): return lax.ppermute(val, axis, pairs + [(b, a) for a, b in pairs])]
    pallas_call x14 -> x15, Pallas kernels: 14.7 us -> 15.6 us  [call(): pl.pallas_call(kernel, out_shape=shapes, in_specs=[kinds.get(i, VM) for i...]
  transfers between devices with their start and end apart: 10 -> 12, of which waited for: 6 -> 4; matrix products, arithmetic and copies ran while one was open for 0% -> 0% of each run, Pallas kernels for 28% -> 31%
where the time goes in v2:
time: 38.6 us; the launch traced here: 38.4 us
  starting transfers between devices  15.8 us (41%)
  Pallas kernels  15.6 us (40%)
  waiting for transfers between devices  4.45 us (12%)
  local copies, waits for them, and re-layouts  2.16 us (6%)
  between operations  0.5 us (1%)
    pallas_call x15, Pallas kernels, call(): pl.pallas_call(kernel, out_shape=shapes, in_specs=[kinds.get(i, VM) for i...  15.6 us
    ppermute x8, starting transfers between devices, shift(): lax.ppermute(val, axis, [(i, (i + step) % count) for i in range(count)])  9.69 us
    ppermute x4, starting transfers between devices, swap(): return lax.ppermute(val, axis, pairs + [(b, a) for a, b in pairs])  6.06 us
    ppermute x8, waiting for transfers between devices, shift(): lax.ppermute(val, axis, [(i, (i + step) % count) for i in range(count)])  4.09 us
    slice x1, local copies, waits for them, and re-layouts, on_device(): ulo, uhi = (u[:8], u[8:])  1.51 us
  transfers between devices with their start and end apart: 12, of which 4 were waited for; matrix products, arithmetic and copies ran while one was open for 0% of the time, Pallas kernels for 31%

profile of v2, /device:TPU:6, one launch (start us, length us, event | category | flops | bytes accessed | tf_op | source)
XLA Modules:
  0.0 38.4 jit_solution(6417725594562123018)
XLA Ops:
  0.0 1.5 %fusion = (f32[8,96,256]{2,1,0:T(8,128)S(1)}, f32[8,96,256]{2,1,0:T(8,128)S(1)}) fusion(f32[16,96,256]{2,1,0:T(8,128)} %param.23), kind=kLoop, calls=%fused_computation | loop fusion | bytes 3145728 | tf_op jit(solution)/shard_map/slice | solution.py:705
  1.6 0.5 %collective-permute-start = (f32[2,96,256]{2,1,0:T(8,128)S(1)}, f32[2,96,256]{2,1,0:T(8,128)S(1)}, u32[]{:S(2)}, u32[]{:S(2)}) collective-permute-start(f32[2,96,256]{2,1,0:T(8,128)S(1)} %face_hi.1), channel_id=1, source_target_pairs={{0,32},{32,64},{64,96},{96,0},{1,33},{33,65},{65,97},{97,1},{2,34}... | collective-permute-start | bytes 589832 | tf_op jit(solution)/shard_map/ppermute | solution.py:676
  2.2 1.7 %collective-permute-start.1 = (f32[2,96,256]{2,1,0:T(8,128)S(1)}, f32[2,96,256]{2,1,0:T(8,128)S(1)}, u32[]{:S(2)}, u32[]{:S(2)}) collective-permute-start(f32[2,96,256]{2,1,0:T(8,128)S(1)} %face_lo.1), channel_id=1, source_target_pairs={{0,96},{32,0},{64,32},{96,64},{1,97},{33,1},{65,33},{97,65},{2,98}... | collective-permute-start | bytes 589832 | tf_op jit(solution)/shard_map/ppermute | solution.py:676
  3.9 2.6 %local_z.1 = (f32[16,96,256]{2,1,0:T(8,128)S(1)}, f32[16,96,256]{2,1,0:T(8,128)S(1)}, f32[16,96,256]{2,1,0:T(8,128)S(1)}, f32[16,96,256]{2,1,0:T(8,128)S(1)}, f32[96,128]{1,0:T(8,128)S(1)}) custom-call(f32[8,96,256]{2,1,0:T(8,128)S(1)} %get-tuple-element.68.ulo_ref.u_ref, f32[8,96,256]{2,1,0:T(8,128)S(1)} %get-tuple-element.67.uhi_ref.u_ref, ...), custom_call_target="tpu_custom_call" | custom-call | flops 3000000000 | bytes 8000000 | tf_op jit(solution)/shard_map/local_z/pallas_call | solution.py:156
  6.9 0.5 %copy-done.3 = bf16[96,288]{1,0:T(8,128)(2,1)S(1)} copy-done((bf16[96,288]{1,0:T(8,128)(2,1)S(1)}, bf16[96,288]{1,0:T(8,128)(2,1)}, u32[]{:S(2)}) %copy-start.3) | copy-done | bytes 55320
  7.4 1.0 %local_y.1 = (f32[14,96,256]{2,1,0:T(8,128)S(1)}, f32[14,96,256]{2,1,0:T(8,128)S(1)}, f32[14,96,256]{2,1,0:T(8,128)S(1)}) custom-call(f32[16,96,256]{2,1,0:T(8,128)S(1)} %get-tuple-element.36.z1, f32[16,96,256]{2,1,0:T(8,128)S(1)} %get-tuple-element.37.z2, f32[16,96,256]{2,1,0:T(8,128)S(1)} %get-tuple-element.38.z3, bf16[96,192]{1,0:T(8,128)(2,1)S(1)} %copy-done.4, ...), custom_call_target="tpu_custom_call" | custom-call | flops 1000000000 | bytes 9000000 | tf_op jit(solution)/shard_map/local_y/pallas_call | solution.py:156
  8.4 1.3 %collective-permute-done.1.hi_ref = f32[2,96,256]{2,1,0:T(8,128)S(1)} collective-permute-done((f32[2,96,256]{2,1,0:T(8,128)S(1)}, f32[2,96,256]{2,1,0:T(8,128)S(1)}, u32[]{:S(2)}, u32[]{:S(2)}) %collective-permute-start.1) | collective-permute-done | bytes 196640 | tf_op jit(solution)/shard_map/ppermute | solution.py:676
  9.7 0.4 %face_z.1 = (f32[2,3,96,256]{3,2,1,0:T(8,128)S(1)}, f32[96,128]{1,0:T(8,128)S(1)}) custom-call(f32[2,96,256]{2,1,0:T(8,128)S(1)} %collective-permute-done.lo_ref, f32[2,96,256]{2,1,0:T(8,128)S(1)} %collective-permute-done.1.hi_ref, f32[96,128]{1,0:T(8,128)S(1)} %get-tuple-element.43.cols_ref.after_ref, bf16[512,256]{1,0:T(8,128)(2,1)S(1)} %copy-done.8, ...), custom_call_target="tpu_custom_call" | custom-call | tf_op jit(solution)/shard_map/face_z/pallas_call | solution.py:156
  10.2 4.3 %collective-permute-start.3 = (f32[96,128]{1,0:T(8,128)S(1)}, f32[96,128]{1,0:T(8,128)S(1)}, u32[]{:S(2)}, u32[]{:S(2)}) collective-permute-start(f32[96,128]{1,0:T(8,128)S(1)} %get-tuple-element.46.cols), channel_id=1, source_target_pairs={{1,2},{3,4},{5,6},{7,0},{2,1},{4,3},{6,5},{0,7},{9,10},{11,12},{13... | collective-permute-start | bytes 147464 | tf_op jit(solution)/shard_map/ppermute | solution.py:686
  14.6 2.8 %residue.1 = (f32[16,96,256]{2,1,0:T(8,128)S(1)}, f32[6,16,256]{2,1,0:T(8,128)S(1)}, f32[6,16,256]{2,1,0:T(8,128)S(1)}) custom-call(f32[14,96,256]{2,1,0:T(8,128)S(1)} %get-tuple-element.39.sx_, f32[14,96,256]{2,1,0:T(8,128)S(1)} %get-tuple-element.40.sy_, f32[14,96,256]{2,1,0:T(8,128)S(1)} %get-tuple-element.41.sz_, ...), custom_call_target="tpu_custom_call" | custom-call | flops 3000000000 | bytes 12000000 | tf_op jit(solution)/shard_map/residue/pallas_call | solution.py:156
  17.5 0.9 %face_y.1 = (f32[6,16,256]{2,1,0:T(8,128)S(1)}, f32[6,16,256]{2,1,0:T(8,128)S(1)}, f32[96,128]{1,0:T(8,128)S(1)}, f32[96,128]{1,0:T(8,128)S(1)}) custom-call(f32[96,128]{1,0:T(8,128)S(1)} %collective-permute-done.2.near, f32[96,128]{1,0:T(8,128)S(1)} %collective-permute-done.3.far, f32[96,128]{1,0:T(8,128)S(1)} %get-tuple-element.46.cols, ...), custom_call_target="tpu_custom_call" | custom-call | tf_op jit(solution)/shard_map/face_y/pallas_call | solution.py:156
  18.4 1.6 %collective-permute-start.4 = (f32[6,16,256]{2,1,0:T(8,128)S(1)}, f32[6,16,256]{2,1,0:T(8,128)S(1)}, u32[]{:S(2)}, u32[]{:S(2)}) collective-permute-start(f32[6,16,256]{2,1,0:T(8,128)S(1)} %get-tuple-element.56.own_hi), channel_id=1, source_target_pairs={{0,8},{8,16},{16,24},{24,0},{1,9},{9,17},{17,25},{25,1},{2,10},{10... | collective-permute-start | bytes 294920 | tf_op jit(solution)/shard_map/ppermute | solution.py:676
  20.0 1.7 %collective-permute-start.5 = (f32[6,16,256]{2,1,0:T(8,128)S(1)}, f32[6,16,256]{2,1,0:T(8,128)S(1)}, u32[]{:S(2)}, u32[]{:S(2)}) collective-permute-start(f32[6,16,256]{2,1,0:T(8,128)S(1)} %get-tuple-element.55.own_lo), channel_id=1, source_target_pairs={{0,24},{8,0},{16,8},{24,16},{1,25},{9,1},{17,9},{25,17},{2,26},{10... | collective-permute-start | bytes 294920 | tf_op jit(solution)/shard_map/ppermute | solution.py:676
  21.7 1.5 %filter.1 = (f32[16,96,256]{2,1,0:T(8,128)S(1)}, f32[96,128]{1,0:T(8,128)S(1)}, f32[96,128]{1,0:T(8,128)S(1)}) custom-call(f32[16,96,256]{2,1,0:T(8,128)S(1)} %get-tuple-element.45.r_ref, f32[96,128]{1,0:T(8,128)S(1)} %get-tuple-element.49.cval, bf16[96,288]{1,0:T(8,128)(2,1)S(1)} %copy-done.21, bf16[768,128]{1,0:T(8,128)(2,1)S(1)} %copy-done.11, ...), custom_call_target="tpu_custom_call" | custom-call | flops 2000000000 | bytes 9000000 | tf_op jit(solution)/shard_map/filter/pallas_call | solution.py:156
  23.3 1.4 %filter_z.1 = (f32[16,96,256]{2,1,0:T(8,128)S(1)}, f32[16,96,256]{2,1,0:T(8,128)S(1)}) custom-call(f32[16,96,256]{2,1,0:T(8,128)S(1)} %get-tuple-element.50.r1, f32[16,96,256]{2,1,0:T(8,128)S(1)} %get-tuple-element.42.z4, f32[96,128]{1,0:T(8,128)S(1)} %get-tuple-element.51.hcols, bf16[96,288]{1,0:T(8,128)(2,1)S(1)} %copy-done.20, bf16[768,256]{1,0:T(8,128)(2,1)S(1)} %copy-done.5), custom_call_target="tpu_custom_call" | custom-call | flops 2000000000 | bytes 9000000 | tf_op jit(solution)/shard_map/filter_z/pallas_call | solution.py:156
  24.8 0.8 %face_z2.1 = (f32[96,128]{1,0:T(8,128)S(1)}, f32[8,16,256]{2,1,0:T(8,128)S(1)}) custom-call(f32[96,128]{1,0:T(8,128)S(1)} %get-tuple-element.54.cols_ref, f32[16,96,256]{2,1,0:T(8,128)S(1)} %get-tuple-element.52.after_ref.r2, f32[6,16,256]{2,1,0:T(8,128)S(1)} %get-tuple-element.55.own_lo, f32[6,16,256]{2,1,0:T(8,128)S(1)} %get-tuple-element.56.own_hi, ...), custom_call_target="tpu_custom_call" | custom-call | tf_op jit(solution)/shard_map/face_z2/pallas_call | solution.py:156
  25.6 1.6 %collective-permute-start.7 = (f32[96,128]{1,0:T(8,128)S(1)}, f32[96,128]{1,0:T(8,128)S(1)}, u32[]{:S(2)}, u32[]{:S(2)}) collective-permute-start(f32[96,128]{1,0:T(8,128)S(1)} %get-tuple-element.61), channel_id=1, source_target_pairs={{1,2},{3,4},{5,6},{7,0},{2,1},{4,3},{6,5},{0,7},{9,10},{11,12},{13... | collective-permute-start | bytes 147464 | tf_op jit(solution)/shard_map/ppermute | solution.py:686
  27.2 0.8 %spread.1 = (f32[16,96,256]{2,1,0:T(8,128)S(1)}, f32[16,96,256]{2,1,0:T(8,128)S(1)}, f32[2,96,256]{2,1,0:T(8,128)S(1)}, f32[2,96,256]{2,1,0:T(8,128)S(1)}) custom-call(f32[16,96,256]{2,1,0:T(8,128)S(1)} %get-tuple-element.52.after_ref.r2, f32[16,96,256]{2,1,0:T(8,128)S(1)} %get-tuple-element.53.vu, f32[8,16,256]{2,1,0:T(8,128)S(1)} %get-tuple-element.57.rows_ref, ...), custom_call_target="tpu_custom_call" | custom-call | flops 1000000000 | bytes 9000000 | tf_op jit(solution)/shard_map/spread/pallas_call | solution.py:156
  28.3 1.7 %collective-permute-start.9 = (f32[2,96,256]{2,1,0:T(8,128)S(1)}, f32[2,96,256]{2,1,0:T(8,128)S(1)}, u32[]{:S(2)}, u32[]{:S(2)}) collective-permute-start(f32[2,96,256]{2,1,0:T(8,128)S(1)} %get-tuple-element.64), channel_id=1, source_target_pairs={{0,96},{32,0},{64,32},{96,64},{1,97},{33,1},{65,33},{97,65},{2,98}... | collective-permute-start | bytes 589832 | tf_op jit(solution)/shard_map/ppermute | solution.py:676
  30.7 1.2 %collective-permute-start.10 = (f32[8,128]{1,0:T(8,128)S(1)}, f32[8,128]{1,0:T(8,128)S(1)}, u32[]{:S(2)}, u32[]{:S(2)}) collective-permute-start(f32[8,128]{1,0:T(8,128)S(1)} %get-tuple-element.65), channel_id=1, source_target_pairs={{0,32},{32,64},{64,96},{96,0},{1,33},{33,65},{65,97},{97,1},{2,34}... | collective-permute-start | bytes 12296 | tf_op jit(solution)/shard_map/ppermute | solution.py:676
  31.9 0.9 %collective-permute-start.11 = (f32[8,128]{1,0:T(8,128)S(1)}, f32[8,128]{1,0:T(8,128)S(1)}, u32[]{:S(2)}, u32[]{:S(2)}) collective-permute-start(f32[8,128]{1,0:T(8,128)S(1)} %get-tuple-element.66), channel_id=1, source_target_pairs={{0,96},{32,0},{64,32},{96,64},{1,97},{33,1},{65,33},{97,65},{2,98}... | collective-permute-start | bytes 12296 | tf_op jit(solution)/shard_map/ppermute | solution.py:676
  32.8 1.2 %local_x.1.val_ref = f32[16,96,256]{2,1,0:T(8,128)S(1)} custom-call(f32[16,96,256]{2,1,0:T(8,128)S(1)} %get-tuple-element.59.r2, f32[16,96,256]{2,1,0:T(8,128)S(1)} %get-tuple-element.60.vu, f32[96,128]{1,0:T(8,128)S(1)} %get-tuple-element.62.hs, bf16[384,256]{1,0:T(8,128)(2,1)S(1)} %copy-done.18), custom_call_target="tpu_custom_call" | custom-call | flops 99999997952 | bytes 100000000 | tf_op jit(solution)/shard_map/local_x/pallas_call | solution.py:156
  34.3 2.4 %collective-permute-done.11.ghi_ref = f32[8,128]{1,0:T(8,128)S(1)} collective-permute-done((f32[8,128]{1,0:T(8,128)S(1)}, f32[8,128]{1,0:T(8,128)S(1)}, u32[]{:S(2)}, u32[]{:S(2)}) %collective-permute-start.11) | collective-permute-done | bytes 4128 | tf_op jit(solution)/shard_map/ppermute | solution.py:676
  36.7 1.6 %final.1 = f32[16,96,256]{2,1,0:T(8,128)} custom-call(f32[16,96,256]{2,1,0:T(8,128)S(1)} %local_x.1.val_ref, f32[2,96,256]{2,1,0:T(8,128)S(1)} %collective-permute-done.8.lo_ref, f32[2,96,256]{2,1,0:T(8,128)S(1)} %collective-permute-done.9.hi_ref, f32[8,128]{1,0:T(8,128)S(1)} %collective-permute-done.10.glo_ref, ...), custom_call_target="tpu_custom_call" | custom-call | tf_op jit(solution)/shard_map/final/pallas_call | solution.py:156
  (60 shorter events, 2.1 us)
Async XLA Ops:
  1.6 6.8 %collective-permute-start = (f32[2,96,256]{2,1,0:T(8,128)S(1)}, f32[2,96,256]{2,1,0:T(8,128)S(1)}, u32[]{:S(2)}, u32[]{:S(2)}) collective-permute-start(f32[2,96,256]{2,1,0:T(8,128)S(1)} %face_hi.1), channel_id=1, source_target_pairs={{0,32},{32,64},{64,96},{96,0},{1,33},{33,65},{65,97},{97,1},{2,34}... | collective-permute-start | bytes 589832 | tf_op jit(solution)/shard_map/ppermute | solution.py:676
  2.2 7.5 %collective-permute-start.1 = (f32[2,96,256]{2,1,0:T(8,128)S(1)}, f32[2,96,256]{2,1,0:T(8,128)S(1)}, u32[]{:S(2)}, u32[]{:S(2)}) collective-permute-start(f32[2,96,256]{2,1,0:T(8,128)S(1)} %face_lo.1), channel_id=1, source_target_pairs={{0,96},{32,0},{64,32},{96,64},{1,97},{33,1},{65,33},{97,65},{2,98}... | collective-permute-start | bytes 589832 | tf_op jit(solution)/shard_map/ppermute | solution.py:676
  3.9 2.6 %copy-start = (bf16[3,16,96,256]{3,2,1,0:T(8,128)(2,1)S(1)}, bf16[3,16,96,256]{3,2,1,0:T(8,128)(2,1)}, u32[]{:S(2)}) copy-start(bf16[3,16,96,256]{3,2,1,0:T(8,128)(2,1)} %v_ref.1) | copy-start | bytes 7077892
  7.4 7.1 %copy-start.1 = (bf16[768,256]{1,0:T(8,128)(2,1)S(1)}, bf16[768,256]{1,0:T(8,128)(2,1)}, u32[]{:S(2)}) copy-start(bf16[768,256]{1,0:T(8,128)(2,1)} %constant.49.clone.rz_ref) | copy-start | bytes 1179652
  7.4 7.1 %copy-start.7 = (bf16[96,288]{1,0:T(8,128)(2,1)S(1)}, bf16[96,288]{1,0:T(8,128)(2,1)}, u32[]{:S(2)}) copy-start(bf16[96,288]{1,0:T(8,128)(2,1)} %constant.48.clone.ry_ref) | copy-start | bytes 165892
  10.1 7.3 %collective-permute-start.2 = (f32[96,128]{1,0:T(8,128)S(1)}, f32[96,128]{1,0:T(8,128)S(1)}, u32[]{:S(2)}, u32[]{:S(2)}) collective-permute-start(f32[96,128]{1,0:T(8,128)S(1)} %get-tuple-element.46.cols), channel_id=1, source_target_pairs={{0,1},{2,3},{4,5},{6,7},{1,0},{3,2},{5,4},{7,6},{8,9},{10,11},{12,... | collective-permute-start | bytes 147464 | tf_op jit(solution)/shard_map/ppermute | solution.py:686
  10.2 7.2 %collective-permute-start.3 = (f32[96,128]{1,0:T(8,128)S(1)}, f32[96,128]{1,0:T(8,128)S(1)}, u32[]{:S(2)}, u32[]{:S(2)}) collective-permute-start(f32[96,128]{1,0:T(8,128)S(1)} %get-tuple-element.46.cols), channel_id=1, source_target_pairs={{1,2},{3,4},{5,6},{7,0},{2,1},{4,3},{6,5},{0,7},{9,10},{11,12},{13... | collective-permute-start | bytes 147464 | tf_op jit(solution)/shard_map/ppermute | solution.py:686
  14.5 2.9 %copy-start.10 = (bf16[384,256]{1,0:T(8,128)(2,1)S(1)}, bf16[384,256]{1,0:T(8,128)(2,1)}, u32[]{:S(2)}) copy-start(bf16[384,256]{1,0:T(8,128)(2,1)} %constant.56.clone.zv_ref) | copy-start | bytes 589828
  14.5 2.9 %copy-start.13 = (bf16[384,128]{1,0:T(8,128)(2,1)S(1)}, bf16[384,128]{1,0:T(8,128)(2,1)}, u32[]{:S(2)}) copy-start(bf16[384,128]{1,0:T(8,128)(2,1)} %constant.55.clone.rx_ref) | copy-start | bytes 294916
  14.6 2.9 %copy-start.15 = (bf16[8,288]{1,0:T(8,128)(2,1)S(1)}, bf16[8,288]{1,0:T(8,128)(2,1)}, u32[]{:S(2)}) copy-start(bf16[8,288]{1,0:T(8,128)(2,1)} %constant.57.clone.yr_ref) | copy-start | bytes 13828
  14.6 7.1 %copy-start.11 = (bf16[768,128]{1,0:T(8,128)(2,1)S(1)}, bf16[768,128]{1,0:T(8,128)(2,1)}, u32[]{:S(2)}) copy-start(bf16[768,128]{1,0:T(8,128)(2,1)} %constant.51.clone.pay_ref) | copy-start | bytes 589828
  14.6 7.1 %copy-start.19 = (bf16[384,128]{1,0:T(8,128)(2,1)S(1)}, bf16[384,128]{1,0:T(8,128)(2,1)}, u32[]{:S(2)}) copy-start(bf16[384,128]{1,0:T(8,128)(2,1)} %constant.58.clone.zc_ref) | copy-start | bytes 294916
  14.6 7.1 %copy-start.21 = (bf16[96,288]{1,0:T(8,128)(2,1)S(1)}, bf16[96,288]{1,0:T(8,128)(2,1)}, u32[]{:S(2)}) copy-start(bf16[96,288]{1,0:T(8,128)(2,1)} %constant.53.clone.ty_ref) | copy-start | bytes 165892
  18.4 6.3 %collective-permute-start.4 = (f32[6,16,256]{2,1,0:T(8,128)S(1)}, f32[6,16,256]{2,1,0:T(8,128)S(1)}, u32[]{:S(2)}, u32[]{:S(2)}) collective-permute-start(f32[6,16,256]{2,1,0:T(8,128)S(1)} %get-tuple-element.56.own_hi), channel_id=1, source_target_pairs={{0,8},{8,16},{16,24},{24,0},{1,9},{9,17},{17,25},{25,1},{2,10},{10... | collective-permute-start | bytes 294920 | tf_op jit(solution)/shard_map/ppermute | solution.py:676
  20.0 4.7 %collective-permute-start.5 = (f32[6,16,256]{2,1,0:T(8,128)S(1)}, f32[6,16,256]{2,1,0:T(8,128)S(1)}, u32[]{:S(2)}, u32[]{:S(2)}) collective-permute-start(f32[6,16,256]{2,1,0:T(8,128)S(1)} %get-tuple-element.55.own_lo), channel_id=1, source_target_pairs={{0,24},{8,0},{16,8},{24,16},{1,25},{9,1},{17,9},{25,17},{2,26},{10... | collective-permute-start | bytes 294920 | tf_op jit(solution)/shard_map/ppermute | solution.py:676
  25.5 4.5 %collective-permute-start.6 = (f32[96,128]{1,0:T(8,128)S(1)}, f32[96,128]{1,0:T(8,128)S(1)}, u32[]{:S(2)}, u32[]{:S(2)}) collective-permute-start(f32[96,128]{1,0:T(8,128)S(1)} %get-tuple-element.61), channel_id=1, source_target_pairs={{0,1},{2,3},{4,5},{6,7},{1,0},{3,2},{5,4},{7,6},{8,9},{10,11},{12,... | collective-permute-start | bytes 147464 | tf_op jit(solution)/shard_map/ppermute | solution.py:686
  25.6 4.8 %collective-permute-start.7 = (f32[96,128]{1,0:T(8,128)S(1)}, f32[96,128]{1,0:T(8,128)S(1)}, u32[]{:S(2)}, u32[]{:S(2)}) collective-permute-start(f32[96,128]{1,0:T(8,128)S(1)} %get-tuple-element.61), channel_id=1, source_target_pairs={{1,2},{3,4},{5,6},{7,0},{2,1},{4,3},{6,5},{0,7},{9,10},{11,12},{13... | collective-permute-start | bytes 147464 | tf_op jit(solution)/shard_map/ppermute | solution.py:686
  27.2 3.2 %copy-start.14 = (bf16[384,128]{1,0:T(8,128)(2,1)S(1)}, bf16[384,128]{1,0:T(8,128)(2,1)}, u32[]{:S(2)}) copy-start(bf16[384,128]{1,0:T(8,128)(2,1)} %constant.60.clone.mat_ref) | copy-start | bytes 294916
  27.2 5.6 %copy-start.18 = (bf16[384,256]{1,0:T(8,128)(2,1)S(1)}, bf16[384,256]{1,0:T(8,128)(2,1)}, u32[]{:S(2)}) copy-start(bf16[384,256]{1,0:T(8,128)(2,1)} %constant.61.clone.add_ref) | copy-start | bytes 589828
  28.0 8.7 %collective-permute-start.8 = (f32[2,96,256]{2,1,0:T(8,128)S(1)}, f32[2,96,256]{2,1,0:T(8,128)S(1)}, u32[]{:S(2)}, u32[]{:S(2)}) collective-permute-start(f32[2,96,256]{2,1,0:T(8,128)S(1)} %get-tuple-element.63), channel_id=1, source_target_pairs={{0,32},{32,64},{64,96},{96,0},{1,33},{33,65},{65,97},{97,1},{2,34}... | collective-permute-start | bytes 589832 | tf_op jit(solution)/shard_map/ppermute | solution.py:676
  28.3 8.4 %collective-permute-start.9 = (f32[2,96,256]{2,1,0:T(8,128)S(1)}, f32[2,96,256]{2,1,0:T(8,128)S(1)}, u32[]{:S(2)}, u32[]{:S(2)}) collective-permute-start(f32[2,96,256]{2,1,0:T(8,128)S(1)} %get-tuple-element.64), channel_id=1, source_target_pairs={{0,96},{32,0},{64,32},{96,64},{1,97},{33,1},{65,33},{97,65},{2,98}... | collective-permute-start | bytes 589832 | tf_op jit(solution)/shard_map/ppermute | solution.py:676
  30.7 3.7 %collective-permute-start.10 = (f32[8,128]{1,0:T(8,128)S(1)}, f32[8,128]{1,0:T(8,128)S(1)}, u32[]{:S(2)}, u32[]{:S(2)}) collective-permute-start(f32[8,128]{1,0:T(8,128)S(1)} %get-tuple-element.65), channel_id=1, source_target_pairs={{0,32},{32,64},{64,96},{96,0},{1,33},{33,65},{65,97},{97,1},{2,34}... | collective-permute-start | bytes 12296 | tf_op jit(solution)/shard_map/ppermute | solution.py:676
  31.9 4.8 %collective-permute-start.11 = (f32[8,128]{1,0:T(8,128)S(1)}, f32[8,128]{1,0:T(8,128)S(1)}, u32[]{:S(2)}, u32[]{:S(2)}) collective-permute-start(f32[8,128]{1,0:T(8,128)S(1)} %get-tuple-element.66), channel_id=1, source_target_pairs={{0,96},{32,0},{64,32},{96,64},{1,97},{33,1},{65,33},{97,65},{2,98}... | collective-permute-start | bytes 12296 | tf_op jit(solution)/shard_map/ppermute | solution.py:676
  32.8 3.9 %copy-start.9 = (bf16[128,1024]{1,0:T(8,128)(2,1)S(1)}, bf16[128,1024]{1,0:T(8,128)(2,1)}, u32[]{:S(2)}) copy-start(bf16[128,1024]{1,0:T(8,128)(2,1)} %constant.62.clone.mat_ref) | copy-start | bytes 786436
  (10 other events, 17.2 us)

commit v3 on v2

--- a/solution.py
+++ b/solution.py
@@ -150,7 +150,8 @@
 def call(kernel, outs, *args, scratch=(), flops=0, nbytes=0, name=None, hbm=(), hbm_out=False, smem=(), limit=6 << 20):
     single = not isinstance(outs, list)
     place_at = pltpu.HBM if hbm_out else pltpu.VMEM
-    shapes = [place_at(tuple(o), F32) for o in ([outs] if single else outs)]
+    pairs = [o if isinstance(o[0], tuple) else (o, F32) for o in ([outs] if single else outs)]
+    shapes = [place_at(shape, dtype) for shape, dtype in pairs]
     kinds = {i: pl.BlockSpec(memory_space=pltpu.HBM) for i in hbm}
     kinds.update({i: pl.BlockSpec(memory_space=pltpu.SMEM) for i in smem})
     res = pl.pallas_call(
@@ -235,24 +236,24 @@
     return jnp.where((lane_iota(NYL) % 2) == 0, pltpu.roll(high, 127, 1), pltpu.roll(low, 1, 1))
 
 
-def local_z_kernel(ulo_ref, uhi_ref, sz_ref, dz_ref, fz_ref, z1, z2, z3, z4, cols):
+def local_z_kernel(ulo_ref, uhi_ref, sz_ref, dfz_ref, z1, z2, z3, z4, cols):
     lane = lane_iota(16)
     for t in range(NYL // 16):
         rows = slice(t * 16, t * 16 + 16)
-        nodes = [ref[k, rows, :] for ref in (ulo_ref, uhi_ref) for k in range(8)]
-        grads = even_odd(D, nodes[:8], -1) + even_odd(D, nodes[8:], -1)
-        flat = lambda vals: jnp.concatenate(vals, axis=0)
-        p = split(flat(average_x(nodes)))
-        g = split(flat(average_x(grads)))
+        p = split(jnp.concatenate([ref[k, rows, :] for ref in (ulo_ref, uhi_ref) for k in range(8)], axis=0))
+        slabs = lambda val: [val[16 * k : 16 * k + 16] for k in range(NXL)]
+        avg = slabs(right_exact(p, sz_ref[...]))
+        both = right(p, dfz_ref[...])
+        grads = even_odd(D, avg[:8], -1) + even_odd(D, avg[8:], -1)
         outs = [
-            right_exact(p, sz_ref[...]),
-            right(p, dz_ref[...]),
-            right_exact(g, sz_ref[...]),
-            right(split(flat(nodes)), fz_ref[...]),
+            average_x(avg),
+            average_x(slabs(both[:, 0:NZL])),
+            average_x(grads),
+            slabs(both[:, NZL:]),
         ]
         acc = None
         for k in range(NXL):
-            vals = [o[16 * k : 16 * k + 16] for o in outs]
+            vals = [o[k] for o in outs]
             for ref, val in zip((z1, z2, z3, z4), vals):
                 ref[k, rows, :] = val
             piece = pack_columns(vals, k, lane)
@@ -274,20 +275,6 @@
     cols[...] = acc
 
 
-def local_y_kernel(z1, z2, z3, sy_ref, dy_ref, sx_, sy_, sz_):
-    for x in range(1, NXL - 1):
-        sy_[x - 1] = left(dy_ref[...], split(z1[x]))
-        sz_[x - 1] = left_exact(sy_ref[...], split(z2[x]))
-        sx_[x - 1] = left_exact(sy_ref[...], split(z3[x]))
-
-
-def product_kernel(ulo_ref, uhi_ref, v_ref, after_ref, h_ref):
-    for x in range(NXL):
-        u = ulo_ref[x] if x < 8 else uhi_ref[x - 8]
-        for d in range(3):
-            h_ref[d, x] = v_ref[d, x].astype(F32) * u
-
-
 def row_sum(vals, coefs):
     row = lax.broadcasted_iota(jnp.int32, vals.shape, 0)
     weight = jnp.zeros(vals.shape, F32)
@@ -301,59 +288,92 @@
     return NU_BASE + SGS_COEF * (mag * lax.rsqrt(mag))
 
 
+def face_mask():
+    row = lax.broadcasted_iota(jnp.int32, (NYL, NZL), 0)
+    lane = lax.broadcasted_iota(jnp.int32, (NYL, NZL), 1)
+    inner = (lane != 0) & (lane != NZL - 1) & (row != 0) & (row != NYL - 1)
+    return inner.astype(F32)
+
+
+def flux_slab(vals, u, vel, avg, grad, mask, row_lo, row_hi):
+    sy = left(grad, split(vals[0]))
+    sz, sx = left_exact(avg, split(vals[1])), left_exact(avg, split(vals[2]))
+    lane = lax.broadcasted_iota(jnp.int32, (1, NZL), 1)
+    inner = (lane != 0) & (lane != NZL - 1)
+    for q, val in enumerate((sx, sy, sz)):
+        row_lo(q, jnp.where(inner, val[0:1, :], 0.0))
+        row_hi(q, jnp.where(inner, val[NYL - 1 : NYL, :], 0.0))
+    nu = eddy(sx, sy, sz) * mask
+    return [nu * s - vel[d].astype(F32) * u for d, s in enumerate((sx, sy, sz))]
+
+
+def setter(ref, x):
+    def put(q, val):
+        ref[q, x : x + 1, :] = val
+
+    return put
+
+
+def flux_kernel(
+    z1, z2, z3, ulo_ref, uhi_ref, v_ref, avg_ref, dy_ref, fx, fyh, fyl, fzh, fzl, row_lo, row_hi
+):
+    mask = face_mask()
+    row_lo[...] = jnp.zeros_like(row_lo)
+    row_hi[...] = jnp.zeros_like(row_hi)
+    for x in range(1, NXL - 1):
+        u = ulo_ref[x] if x < 8 else uhi_ref[x - 8]
+        f = flux_slab(
+            [z1[x], z2[x], z3[x]], u, [v_ref[d, x] for d in range(3)], avg_ref[...], dy_ref[...], mask,
+            setter(row_lo, x), setter(row_hi, x),
+        )
+        fx[x - 1] = f[0]
+        fyh[x - 1], fyl[x - 1] = split(f[1])
+        fzh[x - 1], fzl[x - 1] = split(f[2])
+
+
 def residue_kernel(
-    sx_, sy_, sz_, z1, z2, z3, z4, dlt, h_ref, avg_ref, dy_ref, ry_ref, rz_ref,
-    r_ref, out_lo, out_hi, fx, fyh, fyl, edge,
+    fx, fyh, fyl, fzh, fzl, row_lo, row_hi, z1, z2, z3, z4, dlt, ulo_ref, uhi_ref, v_ref,
+    avg_ref, dy_ref, ry_ref, rz_ref, r_ref, out_lo, out_hi, edge,
 ):
+    out_lo[0:3] = row_lo[...]
+    out_hi[0:3] = row_hi[...]
+    mask = face_mask()
+    ends = []
     for s, x in ((0, 0), (1, NXL - 1)):
-        edge[s, 1] = left(dy_ref[...], split(z1[x] + dlt[s, 0]))
-        edge[s, 2] = left_exact(avg_ref[...], split(z2[x] + dlt[s, 1]))
-        edge[s, 0] = left_exact(avg_ref[...], split(z3[x] + dlt[s, 2]))
-    row16 = lax.broadcasted_iota(jnp.int32, (16, NZL), 0)
-    lane16 = lax.broadcasted_iota(jnp.int32, (16, NZL), 1)
-    inner = (lane16 != 0) & (lane16 != NZL - 1)
-    last = NYL // 16 - 1
-    for t in range(last + 1):
-        rows = slice(t * 16, t * 16 + 16)
-        mask = inner
-        if t == 0:
-            mask = mask & (row16 != 0)
-        if t == last:
-            mask = mask & (row16 != 15)
-        mask = mask.astype(F32)
-        fz = []
-        for x in range(NXL):
-            if x in (0, NXL - 1):
-                sx, sy, sz = [edge[0 if x == 0 else 1, q, rows, :] for q in range(3)]
-            else:
-                sx, sy, sz = [ref[x - 1, rows, :] for ref in (sx_, sy_, sz_)]
-            nu = eddy(sx, sy, sz) * mask
-            if t in (0, last):
-                face, out = (0, out_lo) if t == 0 else (15, out_hi)
-                coefs = 0.5 * FM[0] if t == 0 else np.concatenate([np.zeros(8), 0.5 * FM[7]])
-                one = slice(x, x + 1)
-                for q, val in enumerate((sx, sy, sz)):
-                    row = val[face : face + 1, :]
-                    out[q, one, :] = jnp.where(inner[0:1, :], row, 0.0)
-                out[5, one, :] = row_sum(z4[x, rows, :], coefs)
-            fx[x, rows, :] = nu * sx - h_ref[0, x, rows, :]
-            a, b = split(nu * sy - h_ref[1, x, rows, :])
-            fyh[x, rows, :] = a
-            fyl[x, rows, :] = b
-            fz.append(nu * sz - h_ref[2, x, rows, :])
-        nodes = [fx[k, rows, :] for k in range(NXL)]
-        rx = jnp.concatenate(even_odd(DR, nodes[:8], -1) + even_odd(DR, nodes[8:], -1), axis=0)
-        val = rx + right(split(jnp.concatenate(fz, axis=0)), rz_ref[...])
-        for x in range(NXL):
-            fx[x, rows, :] = val[16 * x : 16 * x + 16]
+        vals = [ref[x] + dlt[s, q] for q, ref in enumerate((z1, z2, z3))]
+        f = flux_slab(
+            vals, ulo_ref[0] if s == 0 else uhi_ref[7], [v_ref[d, x] for d in range(3)],
+            avg_ref[...], dy_ref[...], mask, setter(out_lo, x), setter(out_hi, x),
+        )
+        edge[s] = f[0]
+        ends.append([split(f[1]), split(f[2])])
+    for t in range(TILES):
+        rows = slice(t * 8, t * 8 + 8)
+        nodes = [edge[0, rows, :]] + [fx[k, rows, :] for k in range(NXL - 2)] + [edge[1, rows, :]]
+        for e in range(2):
+            for k, val in enumerate(even_odd(DR, nodes[8 * e : 8 * e + 8], -1)):
+                r_ref[8 * e + k, rows, :] = val
     face = LY.face
+    rz = rz_ref[...]
+    groups = [(0, NXL - 1)] + [tuple(range(1 + 7 * c, 8 + 7 * c)) for c in range(2)]
+    for group in groups:
+        if 0 in group:
+            pair = [jnp.concatenate([ends[0][1][i], ends[1][1][i]], axis=0) for i in range(2)]
+        else:
+            xs = slice(group[0] - 1, group[-1])
+            pair = [ref[xs].reshape(len(group) * NYL, NZL) for ref in (fzh, fzl)]
+        along_z = right(pair, rz)
+        for i, x in enumerate(group):
+            ypair = ends[i][0] if 0 in group else (fyh[x - 1], fyl[x - 1])
+            r_ref[x] = r_ref[x] + (left(ry_ref[...], ypair) + along_z[i * NYL : (i + 1) * NYL])
     for x in range(NXL):
-        r_ref[x] = fx[x] + left(ry_ref[...], (fyh[x], fyl[x]))
         one = slice(x, x + 1)
         out_lo[3, one, :] = r_ref[x, 0:1, :]
         out_hi[3, one, :] = r_ref[x, NYL - 1 : NYL, :]
         out_lo[4, one, :] = row_sum(r_ref[x, 0:16, :], face[0, 0:16])
         out_hi[4, one, :] = row_sum(r_ref[x, NYL - 16 : NYL, :], face[-1, NYL - 16 :])
+        out_lo[5, one, :] = row_sum(z4[x, 0:8, :], 0.5 * FM[0])
+        out_hi[5, one, :] = row_sum(z4[x, NYL - 8 : NYL, :], 0.5 * FM[7])
 
 
 def z_columns_x():
@@ -692,7 +712,7 @@
     face_y = (6, NXL, NZL)
     colshape = (NYL, 128)
 
-    sz, dz, fz = exact_right(LZ.avg.T), on_right(LZ.grad.T), on_right(LZ.filt.T)
+    sz, dz = exact_right(LZ.avg.T), on_right(LZ.grad.T)
     sy, dy, fy = exact_left(LY.avg), on_left(LY.grad), on_left(LY.filt)
     ry, rz, rx = on_left(LY.res), on_right(LZ.res.T), on_left(LX.res)
     pay = np.zeros((NZL, 128))
@@ -708,16 +728,13 @@
     lo = call(face_lo_kernel, face_x, ulo, name="face_lo")
     xhi = shift(lo, "gx", -1)
     z1, z2, z3, z4, cols = call(
-        local_z_kernel, [full] * 4 + [colshape], ulo, uhi, sz, dz, fz,
+        local_z_kernel, [full] * 4 + [colshape], ulo, uhi, sz, on_right(np.concatenate([LZ.grad.T, LZ.filt.T], axis=1)),
         flops=3 * 10**9, nbytes=8 * 10**6, name="local_z",
     )
-    h = call(
-        product_kernel, (3,) + full, ulo, uhi, velocity, cols, flops=10**9, nbytes=8 * 10**6, name="product"
-    )
     inner = (NXL - 2, NYL, NZL)
-    sx_, sy_, sz_ = call(
-        local_y_kernel, [inner] * 3, z1, z2, z3, sy, dy,
-        flops=10**9, nbytes=9 * 10**6, name="local_y",
+    flux = call(
+        flux_kernel, [inner] + [(inner, BF)] * 4 + [(3, NXL, NZL)] * 2,
+        z1, z2, z3, ulo, uhi, velocity, sy, dy, flops=10**9, nbytes=12 * 10**6, name="flux",
     )
     dlt, cols = call(
         face_z_kernel, [(2, 3, NYL, NZL), colshape], xlo, xhi, cols, sz, dz, name="face_z"
@@ -725,9 +742,8 @@
     near, far = swap(cols, "gz", 0), swap(cols, "gz", 1)
     r, lo, hi = call(
         residue_kernel, [full, face_y, face_y],
-        sx_, sy_, sz_, z1, z2, z3, z4, dlt, h, sy, dy, ry, rz,
-        scratch=[pltpu.VMEM(full, F32)] + [pltpu.VMEM(full, BF)] * 2 + [pltpu.VMEM((2, 3, NYL, NZL), F32)],
-        flops=3 * 10**9, nbytes=12 * 10**6, name="residue",
+        *flux, z1, z2, z3, z4, dlt, ulo, uhi, velocity, sy, dy, ry, rz,
+        scratch=[pltpu.VMEM((2, NYL, NZL), F32)], flops=3 * 10**9, nbytes=12 * 10**6, name="residue",
     )
     lo, hi, cval, hcols = call(
         face_y_kernel, [face_y, face_y, colshape, colshape], near, far, cols, lo, hi, sy, dy, ry,

time: 38.6 us -> 38.5 us (level)
  starting transfers between devices: 15.8 us -> 16.6 us
  Pallas kernels: 15.6 us -> 15 us
  local copies, waits for them, and re-layouts: 2.16 us -> 1.63 us
    ppermute x4, starting transfers between devices: 6.06 us -> 6.91 us  [swap(): return lax.ppermute(val, axis, pairs + [(b, a) for a, b in pairs])]
    pallas_call x15 -> x14, Pallas kernels: 15.6 us -> 15 us  [call(): pl.pallas_call(kernel, out_shape=shapes, in_specs=[kinds.get(i, VM) for i...]
    ppermute x8, waiting for transfers between devices: 4.09 us -> 4.62 us  [shift(): lax.ppermute(val, axis, [(i, (i + step) % count) for i in range(count)])]
    unnamed x44, local copies, waits for them, and re-layouts: 0.64 us -> 0.13 us
  transfers between devices with their start and end apart: 12 -> 12, of which waited for: 4 -> 4; matrix products, arithmetic and copies ran while one was open for 0% -> 0% of each run, Pallas kernels for 31% -> 30%
where the time goes in v3:
time: 38.5 us; the launch traced here: 38.4 us
  starting transfers between devices  16.6 us (43%)
  Pallas kernels  15 us (39%)
  waiting for transfers between devices  4.63 us (12%)
  local copies, waits for them, and re-layouts  1.63 us (4%)
  between operations  0.52 us (1%)
    pallas_call x14, Pallas kernels, call(): pl.pallas_call(kernel, out_shape=shapes, in_specs=[kinds.get(i, VM) for i...  15 us
    ppermute x8, starting transfers between devices, shift(): lax.ppermute(val, axis, [(i, (i + step) % count) for i in range(count)])  9.69 us
    ppermute x4, starting transfers between devices, swap(): return lax.ppermute(val, axis, pairs + [(b, a) for a, b in pairs])  6.91 us
    ppermute x8, waiting for transfers between devices, shift(): lax.ppermute(val, axis, [(i, (i + step) % count) for i in range(count)])  4.62 us
    slice x1, local copies, waits for them, and re-layouts, on_device(): ulo, uhi = (u[:8], u[8:])  1.5 us
  transfers between devices with their start and end apart: 12, of which 4 were waited for; matrix products, arithmetic and copies ran while one was open for 0% of the time, Pallas kernels for 30%

profile of v3, /device:TPU:6, one launch (start us, length us, event | category | flops | bytes accessed | tf_op | source)
XLA Modules:
  0.0 38.4 jit_solution(16360753555761742228)
XLA Ops:
  0.0 1.5 %fusion = (f32[8,96,256]{2,1,0:T(8,128)S(1)}, f32[8,96,256]{2,1,0:T(8,128)S(1)}) fusion(f32[16,96,256]{2,1,0:T(8,128)} %param.23), kind=kLoop, calls=%fused_computation | loop fusion | bytes 3145728 | tf_op jit(solution)/shard_map/slice | solution.py:725
  1.6 0.5 %collective-permute-start = (f32[2,96,256]{2,1,0:T(8,128)S(1)}, f32[2,96,256]{2,1,0:T(8,128)S(1)}, u32[]{:S(2)}, u32[]{:S(2)}) collective-permute-start(f32[2,96,256]{2,1,0:T(8,128)S(1)} %face_hi.1), channel_id=1, source_target_pairs={{0,32},{32,64},{64,96},{96,0},{1,33},{33,65},{65,97},{97,1},{2,34}... | collective-permute-start | bytes 589832 | tf_op jit(solution)/shard_map/ppermute | solution.py:696
  2.2 1.7 %collective-permute-start.1 = (f32[2,96,256]{2,1,0:T(8,128)S(1)}, f32[2,96,256]{2,1,0:T(8,128)S(1)}, u32[]{:S(2)}, u32[]{:S(2)}) collective-permute-start(f32[2,96,256]{2,1,0:T(8,128)S(1)} %face_lo.1), channel_id=1, source_target_pairs={{0,96},{32,0},{64,32},{96,64},{1,97},{33,1},{65,33},{97,65},{2,98}... | collective-permute-start | bytes 589832 | tf_op jit(solution)/shard_map/ppermute | solution.py:696
  3.9 2.2 %local_z.1 = (f32[16,96,256]{2,1,0:T(8,128)S(1)}, f32[16,96,256]{2,1,0:T(8,128)S(1)}, f32[16,96,256]{2,1,0:T(8,128)S(1)}, f32[16,96,256]{2,1,0:T(8,128)S(1)}, f32[96,128]{1,0:T(8,128)S(1)}) custom-call(f32[8,96,256]{2,1,0:T(8,128)S(1)} %get-tuple-element.76.ulo_ref.u_ref, f32[8,96,256]{2,1,0:T(8,128)S(1)} %get-tuple-element.75.uhi_ref.u_ref, ...), custom_call_target="tpu_custom_call" | custom-call | flops 3000000000 | bytes 8000000 | tf_op jit(solution)/shard_map/local_z/pallas_call | solution.py:157
  6.1 2.1 %flux.1 = (f32[14,96,256]{2,1,0:T(8,128)S(1)}, bf16[14,96,256]{2,1,0:T(8,128)(2,1)S(1)}, bf16[14,96,256]{2,1,0:T(8,128)(2,1)S(1)}, bf16[14,96,256]{2,1,0:T(8,128...) custom-call(f32[16,96,256]{2,1,0:T(8,128)S(1)} %get-tuple-element.40.z1, ...), custom_call_target="tpu_custom_call" | custom-call | flops 1000000000 | bytes 12000000 | tf_op jit(solution)/shard_map/flux/pallas_call | solution.py:157
  8.3 1.4 %collective-permute-done.1.hi_ref = f32[2,96,256]{2,1,0:T(8,128)S(1)} collective-permute-done((f32[2,96,256]{2,1,0:T(8,128)S(1)}, f32[2,96,256]{2,1,0:T(8,128)S(1)}, u32[]{:S(2)}, u32[]{:S(2)}) %collective-permute-start.1) | collective-permute-done | bytes 196640 | tf_op jit(solution)/shard_map/ppermute | solution.py:696
  9.7 0.4 %face_z.1 = (f32[2,3,96,256]{3,2,1,0:T(8,128)S(1)}, f32[96,128]{1,0:T(8,128)S(1)}) custom-call(f32[2,96,256]{2,1,0:T(8,128)S(1)} %collective-permute-done.lo_ref, f32[2,96,256]{2,1,0:T(8,128)S(1)} %collective-permute-done.1.hi_ref, f32[96,128]{1,0:T(8,128)S(1)} %get-tuple-element.51.cols_ref, bf16[512,256]{1,0:T(8,128)(2,1)S(1)} %copy-done.8, ...), custom_call_target="tpu_custom_call" | custom-call | tf_op jit(solution)/shard_map/face_z/pallas_call | solution.py:157
  10.2 4.3 %collective-permute-start.3 = (f32[96,128]{1,0:T(8,128)S(1)}, f32[96,128]{1,0:T(8,128)S(1)}, u32[]{:S(2)}, u32[]{:S(2)}) collective-permute-start(f32[96,128]{1,0:T(8,128)S(1)} %get-tuple-element.54.cols), channel_id=1, source_target_pairs={{1,2},{3,4},{5,6},{7,0},{2,1},{4,3},{6,5},{0,7},{9,10},{11,12},{13... | collective-permute-start | bytes 147464 | tf_op jit(solution)/shard_map/ppermute | solution.py:706
  14.6 2.0 %residue.1 = (f32[16,96,256]{2,1,0:T(8,128)S(1)}, f32[6,16,256]{2,1,0:T(8,128)S(1)}, f32[6,16,256]{2,1,0:T(8,128)S(1)}) custom-call(f32[14,96,256]{2,1,0:T(8,128)S(1)} %get-tuple-element.43.fx, bf16[14,96,256]{2,1,0:T(8,128)(2,1)S(1)} %get-tuple-element.44.fyh, bf16[14,96,256]{2,1,0:T(8,128)(2,1)S(1)} %get-tuple-element.45.fyl, ...), custom_call_target="tpu_custom_call" | custom-call | flops 3000000000 | bytes 12000000 | tf_op jit(solution)/shard_map/residue/pallas_call | solution.py:157
  16.7 0.9 %face_y.1 = (f32[6,16,256]{2,1,0:T(8,128)S(1)}, f32[6,16,256]{2,1,0:T(8,128)S(1)}, f32[96,128]{1,0:T(8,128)S(1)}, f32[96,128]{1,0:T(8,128)S(1)}) custom-call(f32[96,128]{1,0:T(8,128)S(1)} %collective-permute-done.2.near, f32[96,128]{1,0:T(8,128)S(1)} %collective-permute-done.3.far, f32[96,128]{1,0:T(8,128)S(1)} %get-tuple-element.54.cols, ...), custom_call_target="tpu_custom_call" | custom-call | tf_op jit(solution)/shard_map/face_y/pallas_call | solution.py:157
  17.5 1.6 %collective-permute-start.4 = (f32[6,16,256]{2,1,0:T(8,128)S(1)}, f32[6,16,256]{2,1,0:T(8,128)S(1)}, u32[]{:S(2)}, u32[]{:S(2)}) collective-permute-start(f32[6,16,256]{2,1,0:T(8,128)S(1)} %get-tuple-element.64.own_hi), channel_id=1, source_target_pairs={{0,8},{8,16},{16,24},{24,0},{1,9},{9,17},{17,25},{25,1},{2,10},{10... | collective-permute-start | bytes 294920 | tf_op jit(solution)/shard_map/ppermute | solution.py:696
  19.2 1.7 %collective-permute-start.5 = (f32[6,16,256]{2,1,0:T(8,128)S(1)}, f32[6,16,256]{2,1,0:T(8,128)S(1)}, u32[]{:S(2)}, u32[]{:S(2)}) collective-permute-start(f32[6,16,256]{2,1,0:T(8,128)S(1)} %get-tuple-element.63.own_lo), channel_id=1, source_target_pairs={{0,24},{8,0},{16,8},{24,16},{1,25},{9,1},{17,9},{25,17},{2,26},{10... | collective-permute-start | bytes 294920 | tf_op jit(solution)/shard_map/ppermute | solution.py:696
  20.9 1.5 %filter.1 = (f32[16,96,256]{2,1,0:T(8,128)S(1)}, f32[96,128]{1,0:T(8,128)S(1)}, f32[96,128]{1,0:T(8,128)S(1)}) custom-call(f32[16,96,256]{2,1,0:T(8,128)S(1)} %get-tuple-element.53.r_ref, f32[96,128]{1,0:T(8,128)S(1)} %get-tuple-element.57.cval, bf16[96,288]{1,0:T(8,128)(2,1)S(1)} %copy-done.21, bf16[768,128]{1,0:T(8,128)(2,1)S(1)} %copy-done.11, ...), custom_call_target="tpu_custom_call" | custom-call | flops 2000000000 | bytes 9000000 | tf_op jit(solution)/shard_map/filter/pallas_call | solution.py:157
  22.4 1.4 %filter_z.1 = (f32[16,96,256]{2,1,0:T(8,128)S(1)}, f32[16,96,256]{2,1,0:T(8,128)S(1)}) custom-call(f32[16,96,256]{2,1,0:T(8,128)S(1)} %get-tuple-element.58.r1, f32[16,96,256]{2,1,0:T(8,128)S(1)} %get-tuple-element.50.z4, f32[96,128]{1,0:T(8,128)S(1)} %get-tuple-element.59.hcols, bf16[96,288]{1,0:T(8,128)(2,1)S(1)} %copy-done.20, bf16[768,256]{1,0:T(8,128)(2,1)S(1)} %copy-done.5), custom_call_target="tpu_custom_call" | custom-call | flops 2000000000 | bytes 9000000 | tf_op jit(solution)/shard_map/filter_z/pallas_call | solution.py:157
  23.8 0.8 %face_z2.1 = (f32[96,128]{1,0:T(8,128)S(1)}, f32[8,16,256]{2,1,0:T(8,128)S(1)}) custom-call(f32[96,128]{1,0:T(8,128)S(1)} %get-tuple-element.62.cols_ref, f32[16,96,256]{2,1,0:T(8,128)S(1)} %get-tuple-element.60.after_ref.r2, f32[6,16,256]{2,1,0:T(8,128)S(1)} %get-tuple-element.63.own_lo, f32[6,16,256]{2,1,0:T(8,128)S(1)} %get-tuple-element.64.own_hi, ...), custom_call_target="tpu_custom_call" | custom-call | tf_op jit(solution)/shard_map/face_z2/pallas_call | solution.py:157
  24.7 2.4 %collective-permute-start.7 = (f32[96,128]{1,0:T(8,128)S(1)}, f32[96,128]{1,0:T(8,128)S(1)}, u32[]{:S(2)}, u32[]{:S(2)}) collective-permute-start(f32[96,128]{1,0:T(8,128)S(1)} %get-tuple-element.69), channel_id=1, source_target_pairs={{1,2},{3,4},{5,6},{7,0},{2,1},{4,3},{6,5},{0,7},{9,10},{11,12},{13... | collective-permute-start | bytes 147464 | tf_op jit(solution)/shard_map/ppermute | solution.py:706
  27.1 0.8 %spread.1 = (f32[16,96,256]{2,1,0:T(8,128)S(1)}, f32[16,96,256]{2,1,0:T(8,128)S(1)}, f32[2,96,256]{2,1,0:T(8,128)S(1)}, f32[2,96,256]{2,1,0:T(8,128)S(1)}) custom-call(f32[16,96,256]{2,1,0:T(8,128)S(1)} %get-tuple-element.60.after_ref.r2, f32[16,96,256]{2,1,0:T(8,128)S(1)} %get-tuple-element.61.vu, f32[8,16,256]{2,1,0:T(8,128)S(1)} %get-tuple-element.65.rows_ref, ...), custom_call_target="tpu_custom_call" | custom-call | flops 1000000000 | bytes 9000000 | tf_op jit(solution)/shard_map/spread/pallas_call | solution.py:157
  28.3 1.7 %collective-permute-start.9 = (f32[2,96,256]{2,1,0:T(8,128)S(1)}, f32[2,96,256]{2,1,0:T(8,128)S(1)}, u32[]{:S(2)}, u32[]{:S(2)}) collective-permute-start(f32[2,96,256]{2,1,0:T(8,128)S(1)} %get-tuple-element.72), channel_id=1, source_target_pairs={{0,96},{32,0},{64,32},{96,64},{1,97},{33,1},{65,33},{97,65},{2,98}... | collective-permute-start | bytes 589832 | tf_op jit(solution)/shard_map/ppermute | solution.py:696
  30.3 1.6 %collective-permute-start.10 = (f32[8,128]{1,0:T(8,128)S(1)}, f32[8,128]{1,0:T(8,128)S(1)}, u32[]{:S(2)}, u32[]{:S(2)}) collective-permute-start(f32[8,128]{1,0:T(8,128)S(1)} %get-tuple-element.73), channel_id=1, source_target_pairs={{0,32},{32,64},{64,96},{96,0},{1,33},{33,65},{65,97},{97,1},{2,34}... | collective-permute-start | bytes 12296 | tf_op jit(solution)/shard_map/ppermute | solution.py:696
  31.8 0.5 %collective-permute-start.11 = (f32[8,128]{1,0:T(8,128)S(1)}, f32[8,128]{1,0:T(8,128)S(1)}, u32[]{:S(2)}, u32[]{:S(2)}) collective-permute-start(f32[8,128]{1,0:T(8,128)S(1)} %get-tuple-element.74), channel_id=1, source_target_pairs={{0,96},{32,0},{64,32},{96,64},{1,97},{33,1},{65,33},{97,65},{2,98}... | collective-permute-start | bytes 12296 | tf_op jit(solution)/shard_map/ppermute | solution.py:696
  32.4 1.2 %local_x.1.val_ref = f32[16,96,256]{2,1,0:T(8,128)S(1)} custom-call(f32[16,96,256]{2,1,0:T(8,128)S(1)} %get-tuple-element.67.r2, f32[16,96,256]{2,1,0:T(8,128)S(1)} %get-tuple-element.68.vu, f32[96,128]{1,0:T(8,128)S(1)} %get-tuple-element.70.hs, bf16[384,256]{1,0:T(8,128)(2,1)S(1)} %copy-done.18), custom_call_target="tpu_custom_call" | custom-call | flops 99999997952 | bytes 100000000 | tf_op jit(solution)/shard_map/local_x/pallas_call | solution.py:157
  33.5 0.4 %collective-permute-done.10.glo_ref = f32[8,128]{1,0:T(8,128)S(1)} collective-permute-done((f32[8,128]{1,0:T(8,128)S(1)}, f32[8,128]{1,0:T(8,128)S(1)}, u32[]{:S(2)}, u32[]{:S(2)}) %collective-permute-start.10) | collective-permute-done | bytes 4128 | tf_op jit(solution)/shard_map/ppermute | solution.py:696
  33.9 2.7 %collective-permute-done.11.ghi_ref = f32[8,128]{1,0:T(8,128)S(1)} collective-permute-done((f32[8,128]{1,0:T(8,128)S(1)}, f32[8,128]{1,0:T(8,128)S(1)}, u32[]{:S(2)}, u32[]{:S(2)}) %collective-permute-start.11) | collective-permute-done | bytes 4128 | tf_op jit(solution)/shard_map/ppermute | solution.py:696
  36.7 1.5 %final.1 = f32[16,96,256]{2,1,0:T(8,128)} custom-call(f32[16,96,256]{2,1,0:T(8,128)S(1)} %local_x.1.val_ref, f32[2,96,256]{2,1,0:T(8,128)S(1)} %collective-permute-done.8.lo_ref, f32[2,96,256]{2,1,0:T(8,128)S(1)} %collective-permute-done.9.hi_ref, f32[8,128]{1,0:T(8,128)S(1)} %collective-permute-done.10.glo_ref, ...), custom_call_target="tpu_custom_call" | custom-call | tf_op jit(solution)/shard_map/final/pallas_call | solution.py:157
  (59 shorter events, 1.1 us)
Async XLA Ops:
  1.6 6.7 %collective-permute-start = (f32[2,96,256]{2,1,0:T(8,128)S(1)}, f32[2,96,256]{2,1,0:T(8,128)S(1)}, u32[]{:S(2)}, u32[]{:S(2)}) collective-permute-start(f32[2,96,256]{2,1,0:T(8,128)S(1)} %face_hi.1), channel_id=1, source_target_pairs={{0,32},{32,64},{64,96},{96,0},{1,33},{33,65},{65,97},{97,1},{2,34}... | collective-permute-start | bytes 589832 | tf_op jit(solution)/shard_map/ppermute | solution.py:696
  2.1 3.9 %copy-start.3 = (bf16[96,288]{1,0:T(8,128)(2,1)S(1)}, bf16[96,288]{1,0:T(8,128)(2,1)}, u32[]{:S(2)}) copy-start(bf16[96,288]{1,0:T(8,128)(2,1)} %constant.45.clone.dy_ref) | copy-start | bytes 165892
  2.1 3.9 %copy-start.4 = (bf16[96,192]{1,0:T(8,128)(2,1)S(1)}, bf16[96,192]{1,0:T(8,128)(2,1)}, u32[]{:S(2)}) copy-start(bf16[96,192]{1,0:T(8,128)(2,1)} %constant.44.clone.avg_ref) | copy-start | bytes 110596
  2.2 7.5 %collective-permute-start.1 = (f32[2,96,256]{2,1,0:T(8,128)S(1)}, f32[2,96,256]{2,1,0:T(8,128)S(1)}, u32[]{:S(2)}, u32[]{:S(2)}) collective-permute-start(f32[2,96,256]{2,1,0:T(8,128)S(1)} %face_lo.1), channel_id=1, source_target_pairs={{0,96},{32,0},{64,32},{96,64},{1,97},{33,1},{65,33},{97,65},{2,98}... | collective-permute-start | bytes 589832 | tf_op jit(solution)/shard_map/ppermute | solution.py:696
  6.1 3.6 %copy-start.6 = (bf16[768,256]{1,0:T(8,128)(2,1)S(1)}, bf16[768,256]{1,0:T(8,128)(2,1)}, u32[]{:S(2)}) copy-start(bf16[768,256]{1,0:T(8,128)(2,1)} %constant.43.clone.dz_ref) | copy-start | bytes 1179652
  6.1 8.5 %copy-start.1 = (bf16[768,256]{1,0:T(8,128)(2,1)S(1)}, bf16[768,256]{1,0:T(8,128)(2,1)}, u32[]{:S(2)}) copy-start(bf16[768,256]{1,0:T(8,128)(2,1)} %constant.48.clone.rz_ref) | copy-start | bytes 1179652
  6.1 8.5 %copy-start.7 = (bf16[96,288]{1,0:T(8,128)(2,1)S(1)}, bf16[96,288]{1,0:T(8,128)(2,1)}, u32[]{:S(2)}) copy-start(bf16[96,288]{1,0:T(8,128)(2,1)} %constant.47.clone.ry_ref) | copy-start | bytes 165892
  10.1 6.5 %collective-permute-start.2 = (f32[96,128]{1,0:T(8,128)S(1)}, f32[96,128]{1,0:T(8,128)S(1)}, u32[]{:S(2)}, u32[]{:S(2)}) collective-permute-start(f32[96,128]{1,0:T(8,128)S(1)} %get-tuple-element.54.cols), channel_id=1, source_target_pairs={{0,1},{2,3},{4,5},{6,7},{1,0},{3,2},{5,4},{7,6},{8,9},{10,11},{12,... | collective-permute-start | bytes 147464 | tf_op jit(solution)/shard_map/ppermute | solution.py:706
  10.2 6.4 %collective-permute-start.3 = (f32[96,128]{1,0:T(8,128)S(1)}, f32[96,128]{1,0:T(8,128)S(1)}, u32[]{:S(2)}, u32[]{:S(2)}) collective-permute-start(f32[96,128]{1,0:T(8,128)S(1)} %get-tuple-element.54.cols), channel_id=1, source_target_pairs={{1,2},{3,4},{5,6},{7,0},{2,1},{4,3},{6,5},{0,7},{9,10},{11,12},{13... | collective-permute-start | bytes 147464 | tf_op jit(solution)/shard_map/ppermute | solution.py:706
  14.6 6.3 %copy-start.11 = (bf16[768,128]{1,0:T(8,128)(2,1)S(1)}, bf16[768,128]{1,0:T(8,128)(2,1)}, u32[]{:S(2)}) copy-start(bf16[768,128]{1,0:T(8,128)(2,1)} %constant.50.clone.pay_ref) | copy-start | bytes 589828
  14.6 6.3 %copy-start.19 = (bf16[384,128]{1,0:T(8,128)(2,1)S(1)}, bf16[384,128]{1,0:T(8,128)(2,1)}, u32[]{:S(2)}) copy-start(bf16[384,128]{1,0:T(8,128)(2,1)} %constant.58.clone.zc_ref) | copy-start | bytes 294916
  14.6 6.3 %copy-start.21 = (bf16[96,288]{1,0:T(8,128)(2,1)S(1)}, bf16[96,288]{1,0:T(8,128)(2,1)}, u32[]{:S(2)}) copy-start(bf16[96,288]{1,0:T(8,128)(2,1)} %constant.52.clone.ty_ref) | copy-start | bytes 165892
  17.5 6.3 %collective-permute-start.4 = (f32[6,16,256]{2,1,0:T(8,128)S(1)}, f32[6,16,256]{2,1,0:T(8,128)S(1)}, u32[]{:S(2)}, u32[]{:S(2)}) collective-permute-start(f32[6,16,256]{2,1,0:T(8,128)S(1)} %get-tuple-element.64.own_hi), channel_id=1, source_target_pairs={{0,8},{8,16},{16,24},{24,0},{1,9},{9,17},{17,25},{25,1},{2,10},{10... | collective-permute-start | bytes 294920 | tf_op jit(solution)/shard_map/ppermute | solution.py:696
  19.2 4.7 %collective-permute-start.5 = (f32[6,16,256]{2,1,0:T(8,128)S(1)}, f32[6,16,256]{2,1,0:T(8,128)S(1)}, u32[]{:S(2)}, u32[]{:S(2)}) collective-permute-start(f32[6,16,256]{2,1,0:T(8,128)S(1)} %get-tuple-element.63.own_lo), channel_id=1, source_target_pairs={{0,24},{8,0},{16,8},{24,16},{1,25},{9,1},{17,9},{25,17},{2,26},{10... | collective-permute-start | bytes 294920 | tf_op jit(solution)/shard_map/ppermute | solution.py:696
  23.8 3.3 %copy-start.2 = (bf16[384,1024]{1,0:T(8,128)(2,1)S(1)}, bf16[384,1024]{1,0:T(8,128)(2,1)}, u32[]{:S(2)}) copy-start(bf16[384,1024]{1,0:T(8,128)(2,1)} %constant.59.clone.mat_ref) | copy-start | bytes 2359300
  24.6 5.4 %collective-permute-start.6 = (f32[96,128]{1,0:T(8,128)S(1)}, f32[96,128]{1,0:T(8,128)S(1)}, u32[]{:S(2)}, u32[]{:S(2)}) collective-permute-start(f32[96,128]{1,0:T(8,128)S(1)} %get-tuple-element.69), channel_id=1, source_target_pairs={{0,1},{2,3},{4,5},{6,7},{1,0},{3,2},{5,4},{7,6},{8,9},{10,11},{12,... | collective-permute-start | bytes 147464 | tf_op jit(solution)/shard_map/ppermute | solution.py:706
  24.7 5.3 %collective-permute-start.7 = (f32[96,128]{1,0:T(8,128)S(1)}, f32[96,128]{1,0:T(8,128)S(1)}, u32[]{:S(2)}, u32[]{:S(2)}) collective-permute-start(f32[96,128]{1,0:T(8,128)S(1)} %get-tuple-element.69), channel_id=1, source_target_pairs={{1,2},{3,4},{5,6},{7,0},{2,1},{4,3},{6,5},{0,7},{9,10},{11,12},{13... | collective-permute-start | bytes 147464 | tf_op jit(solution)/shard_map/ppermute | solution.py:706
  27.1 2.9 %copy-start.14 = (bf16[384,128]{1,0:T(8,128)(2,1)S(1)}, bf16[384,128]{1,0:T(8,128)(2,1)}, u32[]{:S(2)}) copy-start(bf16[384,128]{1,0:T(8,128)(2,1)} %constant.60.clone.mat_ref) | copy-start | bytes 294916
  27.1 5.2 %copy-start.18 = (bf16[384,256]{1,0:T(8,128)(2,1)S(1)}, bf16[384,256]{1,0:T(8,128)(2,1)}, u32[]{:S(2)}) copy-start(bf16[384,256]{1,0:T(8,128)(2,1)} %constant.61.clone.add_ref) | copy-start | bytes 589828
  27.9 8.7 %collective-permute-start.8 = (f32[2,96,256]{2,1,0:T(8,128)S(1)}, f32[2,96,256]{2,1,0:T(8,128)S(1)}, u32[]{:S(2)}, u32[]{:S(2)}) collective-permute-start(f32[2,96,256]{2,1,0:T(8,128)S(1)} %get-tuple-element.71), channel_id=1, source_target_pairs={{0,32},{32,64},{64,96},{96,0},{1,33},{33,65},{65,97},{97,1},{2,34}... | collective-permute-start | bytes 589832 | tf_op jit(solution)/shard_map/ppermute | solution.py:696
  28.3 8.4 %collective-permute-start.9 = (f32[2,96,256]{2,1,0:T(8,128)S(1)}, f32[2,96,256]{2,1,0:T(8,128)S(1)}, u32[]{:S(2)}, u32[]{:S(2)}) collective-permute-start(f32[2,96,256]{2,1,0:T(8,128)S(1)} %get-tuple-element.72), channel_id=1, source_target_pairs={{0,96},{32,0},{64,32},{96,64},{1,97},{33,1},{65,33},{97,65},{2,98}... | collective-permute-start | bytes 589832 | tf_op jit(solution)/shard_map/ppermute | solution.py:696
  30.3 3.7 %collective-permute-start.10 = (f32[8,128]{1,0:T(8,128)S(1)}, f32[8,128]{1,0:T(8,128)S(1)}, u32[]{:S(2)}, u32[]{:S(2)}) collective-permute-start(f32[8,128]{1,0:T(8,128)S(1)} %get-tuple-element.73), channel_id=1, source_target_pairs={{0,32},{32,64},{64,96},{96,0},{1,33},{33,65},{65,97},{97,1},{2,34}... | collective-permute-start | bytes 12296 | tf_op jit(solution)/shard_map/ppermute | solution.py:696
  31.8 4.8 %collective-permute-start.11 = (f32[8,128]{1,0:T(8,128)S(1)}, f32[8,128]{1,0:T(8,128)S(1)}, u32[]{:S(2)}, u32[]{:S(2)}) collective-permute-start(f32[8,128]{1,0:T(8,128)S(1)} %get-tuple-element.74), channel_id=1, source_target_pairs={{0,96},{32,0},{64,32},{96,64},{1,97},{33,1},{65,33},{97,65},{2,98}... | collective-permute-start | bytes 12296 | tf_op jit(solution)/shard_map/ppermute | solution.py:696
  32.4 4.3 %copy-start.9 = (bf16[128,1024]{1,0:T(8,128)(2,1)S(1)}, bf16[128,1024]{1,0:T(8,128)(2,1)}, u32[]{:S(2)}) copy-start(bf16[128,1024]{1,0:T(8,128)(2,1)} %constant.62.clone.mat_ref) | copy-start | bytes 786436
  (10 other events, 19.0 us)

commit v4 on v3

--- a/solution.py
+++ b/solution.py
@@ -175,8 +175,15 @@
 LX, LY, LZ = Line(NXL), Line(NYL), Line(NZL)
 
 
-def face_hi_kernel(u_ref, hi_ref):
+def face_hi_kernel(u_hbm, hi_ref, u_ref, sems):
+    copies = []
+    for c in range(4):
+        rows = slice(c * 24, c * 24 + 24)
+        copies.append(pltpu.make_async_copy(u_hbm.at[8:16, rows, :], u_ref.at[:, rows, :], sems.at[c]))
+        copies[-1].start()
     for t in range(TILES):
+        if t % 3 == 0:
+            copies[t // 3].wait()
         rows = slice(t * 8, t * 8 + 8)
         hi_ref[0, rows, :] = 0.5 * u_ref[7, rows, :]
         hi_ref[1, rows, :] = sum(float(0.5 * D[7, j]) * u_ref[j, rows, :] for j in range(8))
@@ -236,11 +243,11 @@
     return jnp.where((lane_iota(NYL) % 2) == 0, pltpu.roll(high, 127, 1), pltpu.roll(low, 1, 1))
 
 
-def local_z_kernel(ulo_ref, uhi_ref, sz_ref, dfz_ref, z1, z2, z3, z4, cols):
+def local_z_kernel(u_ref, sz_ref, dfz_ref, z1, z2, z3, z4, cols):
     lane = lane_iota(16)
     for t in range(NYL // 16):
         rows = slice(t * 16, t * 16 + 16)
-        p = split(jnp.concatenate([ref[k, rows, :] for ref in (ulo_ref, uhi_ref) for k in range(8)], axis=0))
+        p = split(jnp.concatenate([u_ref[k, rows, :] for k in range(NXL)], axis=0))
         slabs = lambda val: [val[16 * k : 16 * k + 16] for k in range(NXL)]
         avg = slabs(right_exact(p, sz_ref[...]))
         both = right(p, dfz_ref[...])
@@ -315,13 +322,13 @@
 
 
 def flux_kernel(
-    z1, z2, z3, ulo_ref, uhi_ref, v_ref, avg_ref, dy_ref, fx, fyh, fyl, fzh, fzl, row_lo, row_hi
+    z1, z2, z3, u_ref, v_ref, avg_ref, dy_ref, fx, fyh, fyl, fzh, fzl, row_lo, row_hi
 ):
     mask = face_mask()
     row_lo[...] = jnp.zeros_like(row_lo)
     row_hi[...] = jnp.zeros_like(row_hi)
     for x in range(1, NXL - 1):
-        u = ulo_ref[x] if x < 8 else uhi_ref[x - 8]
+        u = u_ref[x]
         f = flux_slab(
             [z1[x], z2[x], z3[x]], u, [v_ref[d, x] for d in range(3)], avg_ref[...], dy_ref[...], mask,
             setter(row_lo, x), setter(row_hi, x),
@@ -332,7 +339,7 @@
 
 
 def residue_kernel(
-    fx, fyh, fyl, fzh, fzl, row_lo, row_hi, z1, z2, z3, z4, dlt, ulo_ref, uhi_ref, v_ref,
+    fx, fyh, fyl, fzh, fzl, row_lo, row_hi, z1, z2, z3, z4, dlt, u_ref, v_ref,
     avg_ref, dy_ref, ry_ref, rz_ref, r_ref, out_lo, out_hi, edge,
 ):
     out_lo[0:3] = row_lo[...]
@@ -342,7 +349,7 @@
     for s, x in ((0, 0), (1, NXL - 1)):
         vals = [ref[x] + dlt[s, q] for q, ref in enumerate((z1, z2, z3))]
         f = flux_slab(
-            vals, ulo_ref[0] if s == 0 else uhi_ref[7], [v_ref[d, x] for d in range(3)],
+            vals, u_ref[x], [v_ref[d, x] for d in range(3)],
             avg_ref[...], dy_ref[...], mask, setter(out_lo, x), setter(out_hi, x),
         )
         edge[s] = f[0]
@@ -436,21 +443,30 @@
 
 
 def place(pay, x, lane):
-    keep = ((lane % 32) // 2) == x
-    return jnp.where(keep, pltpu.roll(pay, 2 * x, 1) if x else pay, 0.0)
-
-
-def filter_kernel(r_ref, cval, ty_ref, pay_ref, zc_ref, r1, cols, cout):
+    return jnp.where(((lane % 32) // 2) == x, pay, 0.0)
+
+
+def filter_kernel(r_ref, cval, z4, hcols, ty_ref, fy_ref, tp_ref, zc_ref, r2, vu, cols, cout):
     lane = lane_iota(NYL)
     acc = None
     for c in range(4):
-        for x in range(4 * c, 4 * c + 4):
-            r1[x] = left(ty_ref[...], split(r_ref[x]))
-        val = r1[4 * c : 4 * c + 4].reshape(4 * NYL, NZL)
-        out = right(split(val), pay_ref[...])
-        for k in range(4):
-            piece = place(out[k * NYL : (k + 1) * NYL], 4 * c + k, lane)
+        xs = range(4 * c, 4 * c + 4)
+        val = jnp.concatenate([left(ty_ref[...], split(r_ref[x])) for x in xs], axis=0)
+        out = right(split(val), tp_ref[...])
+        for k, x in enumerate(xs):
+            part = out[k * NYL : (k + 1) * NYL]
+            r2[x] = part[:, 0:NZL]
+            piece = place(part[:, NZL:], x, lane)
             acc = piece if acc is None else acc + piece
+            rolled = pltpu.roll(hcols[...], (-2 * (48 + x) - 1) % 128, 1)
+            field = jnp.concatenate(
+                [
+                    z4[x, :, 0:128] + jnp.where(lane == 0, rolled, 0.0),
+                    z4[x, :, 128:256] + jnp.where(lane == 127, rolled, 0.0),
+                ],
+                axis=1,
+            )
+            vu[x] = left(fy_ref[...], split(field))
     val = left(ty_ref[...], split(cval[...]))
     cout[...] = val
     cols[...] = acc + right(split(val), zc_ref[...])
@@ -508,10 +524,7 @@
     vecs = []
     for k in range(8):
         val = pay[16 * k : 16 * k + 16]
-        moved = val
-        for bit in (1, 2, 4, 8):
-            moved = jnp.where((row16 & bit) != 0, pltpu.roll(moved, 2 * bit, 1), moved)
-        vec = jnp.sum(jnp.where(keep, moved, 0.0), axis=0, keepdims=True)
+        vec = jnp.sum(jnp.where(keep, val, 0.0), axis=0, keepdims=True)
         vecs.append(vec)
     for rows, ks in ((slice(0, 24), range(4)), (slice(NYL - 24, NYL), range(4, 8))):
         acc = cols_ref[rows, :]
@@ -519,24 +532,6 @@
             acc = acc + ay_ref[rows, k : k + 1] * vecs[k]
         cols[rows, :] = acc
     cols[24 : NYL - 24, :] = cols_ref[24 : NYL - 24, :]
-
-
-def filter_z_kernel(r1, z4, hcols, fy_ref, tz_ref, out, vout):
-    lane = lane_iota(NYL)
-    for c in range(4):
-        xs = slice(4 * c, 4 * c + 4)
-        val = r1[xs].reshape(4 * NYL, NZL)
-        out[xs] = right(split(val), tz_ref[...]).reshape(4, NYL, NZL)
-        for x in range(4 * c, 4 * c + 4):
-            rolled = pltpu.roll(hcols[...], (-2 * (48 + x) - 1) % 128, 1)
-            field = jnp.concatenate(
-                [
-                    z4[x, :, 0:128] + jnp.where(lane == 0, rolled, 0.0),
-                    z4[x, :, 128:256] + jnp.where(lane == 127, rolled, 0.0),
-                ],
-                axis=1,
-            )
-            vout[x] = left(fy_ref[...], split(field))
 
 
 def spread_kernel(
@@ -716,25 +711,28 @@
     sy, dy, fy = exact_left(LY.avg), on_left(LY.grad), on_left(LY.filt)
     ry, rz, rx = on_left(LY.res), on_right(LZ.res.T), on_left(LX.res)
     pay = np.zeros((NZL, 128))
-    pay[NZL - 1, 0] = pay[0, 1] = 1.0
-    pay[:, 32], pay[:, 33] = LZ.face[-1], LZ.face[0]
+    pay[NZL - 1, 0:32:2] = pay[0, 1:32:2] = 1.0
+    pay[:, 32:64:2], pay[:, 33:64:2] = LZ.face[-1][:, None], LZ.face[0][:, None]
+    pay_mat = pay
     pay = on_right(pay)
     ay = jnp.asarray(SPREAD.astype(np.float32))
     ty, tz = on_left(LY.both), on_right(LZ.both.T)
 
-    ulo, uhi = u[:8], u[8:]
-    hi = call(face_hi_kernel, face_x, uhi, name="face_hi")
+    hi = call(
+        face_hi_kernel, face_x, pltpu.with_memory_space_constraint(u, pltpu.HBM), hbm=(0,),
+        scratch=[pltpu.VMEM((8, NYL, NZL), F32), pltpu.SemaphoreType.DMA((4,))], name="face_hi",
+    )
     xlo = shift(hi, "gx", 1)
-    lo = call(face_lo_kernel, face_x, ulo, name="face_lo")
+    lo = call(face_lo_kernel, face_x, u, name="face_lo")
     xhi = shift(lo, "gx", -1)
     z1, z2, z3, z4, cols = call(
-        local_z_kernel, [full] * 4 + [colshape], ulo, uhi, sz, on_right(np.concatenate([LZ.grad.T, LZ.filt.T], axis=1)),
+        local_z_kernel, [full] * 4 + [colshape], u, sz, on_right(np.concatenate([LZ.grad.T, LZ.filt.T], axis=1)),
         flops=3 * 10**9, nbytes=8 * 10**6, name="local_z",
     )
     inner = (NXL - 2, NYL, NZL)
     flux = call(
         flux_kernel, [inner] + [(inner, BF)] * 4 + [(3, NXL, NZL)] * 2,
-        z1, z2, z3, ulo, uhi, velocity, sy, dy, flops=10**9, nbytes=12 * 10**6, name="flux",
+        z1, z2, z3, u, velocity, sy, dy, flops=10**9, nbytes=12 * 10**6, name="flux",
     )
     dlt, cols = call(
         face_z_kernel, [(2, 3, NYL, NZL), colshape], xlo, xhi, cols, sz, dz, name="face_z"
@@ -742,7 +740,7 @@
     near, far = swap(cols, "gz", 0), swap(cols, "gz", 1)
     r, lo, hi = call(
         residue_kernel, [full, face_y, face_y],
-        *flux, z1, z2, z3, z4, dlt, ulo, uhi, velocity, sy, dy, ry, rz,
+        *flux, z1, z2, z3, z4, dlt, u, velocity, sy, dy, ry, rz,
         scratch=[pltpu.VMEM((2, NYL, NZL), F32)], flops=3 * 10**9, nbytes=12 * 10**6, name="residue",
     )
     lo, hi, cval, hcols = call(
@@ -750,12 +748,11 @@
         on_right(z_columns_x()), on_right(z_face_vectors()), on_left(y_rows()), name="face_y",
     )
     ylo, yhi = exchange(lo, hi, "gy")
-    r1, cols, cval = call(
-        filter_kernel, [full, colshape, colshape], r, cval, ty, pay, on_right(z_columns_z()),
-        flops=2 * 10**9, nbytes=9 * 10**6, name="filter",
-    )
-    r2, vu = call(
-        filter_z_kernel, [full, full], r1, z4, hcols, fy, tz, flops=2 * 10**9, nbytes=9 * 10**6, name="filter_z"
+    both = np.concatenate([LZ.both.T, pay_mat], axis=1)
+    r2, vu, cols, cval = call(
+        filter_kernel, [full, full, colshape, colshape],
+        r, cval, z4, hcols, ty, fy, on_right(both), on_right(z_columns_z()),
+        flops=3 * 10**9, nbytes=9 * 10**6, name="filter",
     )
     cols, rows = call(
         face_z2_kernel, [colshape, (8, NXL, NZL)], cols, r2, lo, hi, ylo, yhi, rx, rz, pay, ay,

time: 38.5 us -> 37.9 us (0.984)
  local copies, waits for them, and re-layouts: 1.63 us -> 0.14 us
  Pallas kernels: 15 us -> 16 us
    slice x1 -> x0, local copies, waits for them, and re-layouts: 1.5 us -> none  [on_device(): ulo, uhi = (u[:8], u[8:])]
    pallas_call x14 -> x13, Pallas kernels: 15 us -> 16 us  [call(): pl.pallas_call(kernel, out_shape=shapes, in_specs=[kinds.get(i, VM) for i...]
  transfers between devices with their start and end apart: 12 -> 12, of which waited for: 4 -> 5; matrix products, arithmetic and copies ran while one was open for 0% -> 0% of each run, Pallas kernels for 30% -> 30%
where the time goes in v4:
time: 37.9 us; the launch traced here: 37.8 us
  starting transfers between devices  16.3 us (43%)
  Pallas kernels  16 us (42%)
  waiting for transfers between devices  4.89 us (13%)
  between operations  0.47 us (1%)
    pallas_call x13, Pallas kernels, call(): pl.pallas_call(kernel, out_shape=shapes, in_specs=[kinds.get(i, VM) for i...  16 us
    ppermute x8, starting transfers between devices, shift(): lax.ppermute(val, axis, [(i, (i + step) % count) for i in range(count)])  9.65 us
    ppermute x4, starting transfers between devices, swap(): return lax.ppermute(val, axis, pairs + [(b, a) for a, b in pairs])  6.68 us
    ppermute x8, waiting for transfers between devices, shift(): lax.ppermute(val, axis, [(i, (i + step) % count) for i in range(count)])  4.88 us
  transfers between devices with their start and end apart: 12, of which 5 were waited for; matrix products, arithmetic and copies ran while one was open for 0% of the time, Pallas kernels for 30%

profile of v4, /device:TPU:6, one launch (start us, length us, event | category | flops | bytes accessed | tf_op | source)
XLA Modules:
  0.0 37.8 jit_solution(14654045735851104625)
XLA Ops:
  0.0 1.4 %face_hi.1 = f32[2,96,256]{2,1,0:T(8,128)S(1)} custom-call(f32[16,96,256]{2,1,0:T(8,128)} %u_ref.7), custom_call_target="tpu_custom_call" | custom-call | tf_op jit(solution)/shard_map/face_hi/pallas_call | solution.py:157
  1.4 0.5 %collective-permute-start = (f32[2,96,256]{2,1,0:T(8,128)S(1)}, f32[2,96,256]{2,1,0:T(8,128)S(1)}, u32[]{:S(2)}, u32[]{:S(2)}) collective-permute-start(f32[2,96,256]{2,1,0:T(8,128)S(1)} %face_hi.1), channel_id=1, source_target_pairs={{0,32},{32,64},{64,96},{96,0},{1,33},{33,65},{65,97},{97,1},{2,34}... | collective-permute-start | bytes 589832 | tf_op jit(solution)/shard_map/ppermute | solution.py:691
  2.0 1.7 %collective-permute-start.1 = (f32[2,96,256]{2,1,0:T(8,128)S(1)}, f32[2,96,256]{2,1,0:T(8,128)S(1)}, u32[]{:S(2)}, u32[]{:S(2)}) collective-permute-start(f32[2,96,256]{2,1,0:T(8,128)S(1)} %face_lo.1), channel_id=1, source_target_pairs={{0,96},{32,0},{64,32},{96,64},{1,97},{33,1},{65,33},{97,65},{2,98}... | collective-permute-start | bytes 589832 | tf_op jit(solution)/shard_map/ppermute | solution.py:691
  3.7 2.2 %local_z.1 = (f32[16,96,256]{2,1,0:T(8,128)S(1)}, f32[16,96,256]{2,1,0:T(8,128)S(1)}, f32[16,96,256]{2,1,0:T(8,128)S(1)}, f32[16,96,256]{2,1,0:T(8,128)S(1)}, f32[96,128]{1,0:T(8,128)S(1)}) custom-call(f32[16,96,256]{2,1,0:T(8,128)S(1)} %copy-done, bf16[512,256]{1,0:T(8,128)(2,1)S(1)} %copy-done.9, bf16[768,512]{1,0:T(8,128)(2,1)S(1)} %copy-done.18), custom_call_target="tpu_custom_call" | custom-call | flops 3000000000 | bytes 8000000 | tf_op jit(solution)/shard_map/local_z/pallas_call | solution.py:157
  5.9 2.1 %flux.1 = (f32[14,96,256]{2,1,0:T(8,128)S(1)}, bf16[14,96,256]{2,1,0:T(8,128)(2,1)S(1)}, bf16[14,96,256]{2,1,0:T(8,128)(2,1)S(1)}, bf16[14,96,256]{2,1,0:T(8,128...) custom-call(f32[16,96,256]{2,1,0:T(8,128)S(1)} %get-tuple-element.39.z1, ...), custom_call_target="tpu_custom_call" | custom-call | flops 1000000000 | bytes 12000000 | tf_op jit(solution)/shard_map/flux/pallas_call | solution.py:157
  8.1 1.6 %collective-permute-done.1.hi_ref = f32[2,96,256]{2,1,0:T(8,128)S(1)} collective-permute-done((f32[2,96,256]{2,1,0:T(8,128)S(1)}, f32[2,96,256]{2,1,0:T(8,128)S(1)}, u32[]{:S(2)}, u32[]{:S(2)}) %collective-permute-start.1) | collective-permute-done | bytes 196640 | tf_op jit(solution)/shard_map/ppermute | solution.py:691
  9.8 0.4 %face_z.1 = (f32[2,3,96,256]{3,2,1,0:T(8,128)S(1)}, f32[96,128]{1,0:T(8,128)S(1)}) custom-call(f32[2,96,256]{2,1,0:T(8,128)S(1)} %collective-permute-done.lo_ref, f32[2,96,256]{2,1,0:T(8,128)S(1)} %collective-permute-done.1.hi_ref, f32[96,128]{1,0:T(8,128)S(1)} %get-tuple-element.50.cols_ref, bf16[512,256]{1,0:T(8,128)(2,1)S(1)} %copy-done.9, ...), custom_call_target="tpu_custom_call" | custom-call | tf_op jit(solution)/shard_map/face_z/pallas_call | solution.py:157
  10.3 4.1 %collective-permute-start.3 = (f32[96,128]{1,0:T(8,128)S(1)}, f32[96,128]{1,0:T(8,128)S(1)}, u32[]{:S(2)}, u32[]{:S(2)}) collective-permute-start(f32[96,128]{1,0:T(8,128)S(1)} %get-tuple-element.53.cols), channel_id=1, source_target_pairs={{1,2},{3,4},{5,6},{7,0},{2,1},{4,3},{6,5},{0,7},{9,10},{11,12},{13... | collective-permute-start | bytes 147464 | tf_op jit(solution)/shard_map/ppermute | solution.py:701
  14.5 2.0 %residue.1 = (f32[16,96,256]{2,1,0:T(8,128)S(1)}, f32[6,16,256]{2,1,0:T(8,128)S(1)}, f32[6,16,256]{2,1,0:T(8,128)S(1)}) custom-call(f32[14,96,256]{2,1,0:T(8,128)S(1)} %get-tuple-element.42.fx, bf16[14,96,256]{2,1,0:T(8,128)(2,1)S(1)} %get-tuple-element.43.fyh, bf16[14,96,256]{2,1,0:T(8,128)(2,1)S(1)} %get-tuple-element.44.fyl, ...), custom_call_target="tpu_custom_call" | custom-call | flops 3000000000 | bytes 12000000 | tf_op jit(solution)/shard_map/residue/pallas_call | solution.py:157
  16.6 0.9 %face_y.1 = (f32[6,16,256]{2,1,0:T(8,128)S(1)}, f32[6,16,256]{2,1,0:T(8,128)S(1)}, f32[96,128]{1,0:T(8,128)S(1)}, f32[96,128]{1,0:T(8,128)S(1)}) custom-call(f32[96,128]{1,0:T(8,128)S(1)} %collective-permute-done.2.near, f32[96,128]{1,0:T(8,128)S(1)} %collective-permute-done.3.far, f32[96,128]{1,0:T(8,128)S(1)} %get-tuple-element.53.cols, ...), custom_call_target="tpu_custom_call" | custom-call | tf_op jit(solution)/shard_map/face_y/pallas_call | solution.py:157
  17.4 1.6 %collective-permute-start.4 = (f32[6,16,256]{2,1,0:T(8,128)S(1)}, f32[6,16,256]{2,1,0:T(8,128)S(1)}, u32[]{:S(2)}, u32[]{:S(2)}) collective-permute-start(f32[6,16,256]{2,1,0:T(8,128)S(1)} %get-tuple-element.62.own_hi), channel_id=1, source_target_pairs={{0,8},{8,16},{16,24},{24,0},{1,9},{9,17},{17,25},{25,1},{2,10},{10... | collective-permute-start | bytes 294920 | tf_op jit(solution)/shard_map/ppermute | solution.py:691
  19.1 1.7 %collective-permute-start.5 = (f32[6,16,256]{2,1,0:T(8,128)S(1)}, f32[6,16,256]{2,1,0:T(8,128)S(1)}, u32[]{:S(2)}, u32[]{:S(2)}) collective-permute-start(f32[6,16,256]{2,1,0:T(8,128)S(1)} %get-tuple-element.61.own_lo), channel_id=1, source_target_pairs={{0,24},{8,0},{16,8},{24,16},{1,25},{9,1},{17,9},{25,17},{2,26},{10... | collective-permute-start | bytes 294920 | tf_op jit(solution)/shard_map/ppermute | solution.py:691
  20.8 2.8 %filter.1 = (f32[16,96,256]{2,1,0:T(8,128)S(1)}, f32[16,96,256]{2,1,0:T(8,128)S(1)}, f32[96,128]{1,0:T(8,128)S(1)}, f32[96,128]{1,0:T(8,128)S(1)}) custom-call(f32[16,96,256]{2,1,0:T(8,128)S(1)} %get-tuple-element.52.r_ref, f32[96,128]{1,0:T(8,128)S(1)} %get-tuple-element.56.cval, f32[16,96,256]{2,1,0:T(8,128)S(1)} %get-tuple-element.49.z4, ...), custom_call_target="tpu_custom_call" | custom-call | flops 3000000000 | bytes 9000000 | tf_op jit(solution)/shard_map/filter/pallas_call | solution.py:157
  23.7 0.5 %face_z2.1 = (f32[96,128]{1,0:T(8,128)S(1)}, f32[8,16,256]{2,1,0:T(8,128)S(1)}) custom-call(f32[96,128]{1,0:T(8,128)S(1)} %get-tuple-element.60.cols_ref, f32[16,96,256]{2,1,0:T(8,128)S(1)} %get-tuple-element.58.after_ref.r2, f32[6,16,256]{2,1,0:T(8,128)S(1)} %get-tuple-element.61.own_lo, f32[6,16,256]{2,1,0:T(8,128)S(1)} %get-tuple-element.62.own_hi, ...), custom_call_target="tpu_custom_call" | custom-call | tf_op jit(solution)/shard_map/face_z2/pallas_call | solution.py:157
  24.3 2.4 %collective-permute-start.7 = (f32[96,128]{1,0:T(8,128)S(1)}, f32[96,128]{1,0:T(8,128)S(1)}, u32[]{:S(2)}, u32[]{:S(2)}) collective-permute-start(f32[96,128]{1,0:T(8,128)S(1)} %get-tuple-element.67), channel_id=1, source_target_pairs={{1,2},{3,4},{5,6},{7,0},{2,1},{4,3},{6,5},{0,7},{9,10},{11,12},{13... | collective-permute-start | bytes 147464 | tf_op jit(solution)/shard_map/ppermute | solution.py:701
  26.7 0.8 %spread.1 = (f32[16,96,256]{2,1,0:T(8,128)S(1)}, f32[16,96,256]{2,1,0:T(8,128)S(1)}, f32[2,96,256]{2,1,0:T(8,128)S(1)}, f32[2,96,256]{2,1,0:T(8,128)S(1)}) custom-call(f32[16,96,256]{2,1,0:T(8,128)S(1)} %get-tuple-element.58.after_ref.r2, f32[16,96,256]{2,1,0:T(8,128)S(1)} %get-tuple-element.59.vu, f32[8,16,256]{2,1,0:T(8,128)S(1)} %get-tuple-element.63.rows_ref, ...), custom_call_target="tpu_custom_call" | custom-call | flops 1000000000 | bytes 9000000 | tf_op jit(solution)/shard_map/spread/pallas_call | solution.py:157
  27.4 0.3 collective-permute-start.8
  27.7 1.8 %collective-permute-start.9 = (f32[2,96,256]{2,1,0:T(8,128)S(1)}, f32[2,96,256]{2,1,0:T(8,128)S(1)}, u32[]{:S(2)}, u32[]{:S(2)}) collective-permute-start(f32[2,96,256]{2,1,0:T(8,128)S(1)} %get-tuple-element.70), channel_id=1, source_target_pairs={{0,96},{32,0},{64,32},{96,64},{1,97},{33,1},{65,33},{97,65},{2,98}... | collective-permute-start | bytes 589832 | tf_op jit(solution)/shard_map/ppermute | solution.py:691
  29.8 1.5 %collective-permute-start.10 = (f32[8,128]{1,0:T(8,128)S(1)}, f32[8,128]{1,0:T(8,128)S(1)}, u32[]{:S(2)}, u32[]{:S(2)}) collective-permute-start(f32[8,128]{1,0:T(8,128)S(1)} %get-tuple-element.71), channel_id=1, source_target_pairs={{0,32},{32,64},{64,96},{96,0},{1,33},{33,65},{65,97},{97,1},{2,34}... | collective-permute-start | bytes 12296 | tf_op jit(solution)/shard_map/ppermute | solution.py:691
  31.3 0.6 %collective-permute-start.11 = (f32[8,128]{1,0:T(8,128)S(1)}, f32[8,128]{1,0:T(8,128)S(1)}, u32[]{:S(2)}, u32[]{:S(2)}) collective-permute-start(f32[8,128]{1,0:T(8,128)S(1)} %get-tuple-element.72), channel_id=1, source_target_pairs={{0,96},{32,0},{64,32},{96,64},{1,97},{33,1},{65,33},{97,65},{2,98}... | collective-permute-start | bytes 12296 | tf_op jit(solution)/shard_map/ppermute | solution.py:691
  31.9 1.2 %local_x.1.val_ref = f32[16,96,256]{2,1,0:T(8,128)S(1)} custom-call(f32[16,96,256]{2,1,0:T(8,128)S(1)} %get-tuple-element.65.r2, f32[16,96,256]{2,1,0:T(8,128)S(1)} %get-tuple-element.66.vu, f32[96,128]{1,0:T(8,128)S(1)} %get-tuple-element.68.hs, bf16[384,256]{1,0:T(8,128)(2,1)S(1)} %copy-done.20), custom_call_target="tpu_custom_call" | custom-call | flops 99999997952 | bytes 100000000 | tf_op jit(solution)/shard_map/local_x/pallas_call | solution.py:157
  33.0 0.4 %collective-permute-done.10.glo_ref = f32[8,128]{1,0:T(8,128)S(1)} collective-permute-done((f32[8,128]{1,0:T(8,128)S(1)}, f32[8,128]{1,0:T(8,128)S(1)}, u32[]{:S(2)}, u32[]{:S(2)}) %collective-permute-start.10) | collective-permute-done | bytes 4128 | tf_op jit(solution)/shard_map/ppermute | solution.py:691
  33.5 2.7 %collective-permute-done.11.ghi_ref = f32[8,128]{1,0:T(8,128)S(1)} collective-permute-done((f32[8,128]{1,0:T(8,128)S(1)}, f32[8,128]{1,0:T(8,128)S(1)}, u32[]{:S(2)}, u32[]{:S(2)}) %collective-permute-start.11) | collective-permute-done | bytes 4128 | tf_op jit(solution)/shard_map/ppermute | solution.py:691
  36.1 1.5 %final.1 = f32[16,96,256]{2,1,0:T(8,128)} custom-call(f32[16,96,256]{2,1,0:T(8,128)S(1)} %local_x.1.val_ref, f32[2,96,256]{2,1,0:T(8,128)S(1)} %collective-permute-done.8.lo_ref, f32[2,96,256]{2,1,0:T(8,128)S(1)} %collective-permute-done.9.hi_ref, f32[8,128]{1,0:T(8,128)S(1)} %collective-permute-done.10.glo_ref, ...), custom_call_target="tpu_custom_call" | custom-call | tf_op jit(solution)/shard_map/final/pallas_call | solution.py:157
  (61 shorter events, 0.8 us)
Async XLA Ops:
  0.0 3.7 %copy-start.18 = (bf16[768,512]{1,0:T(8,128)(2,1)S(1)}, bf16[768,512]{1,0:T(8,128)(2,1)}, u32[]{:S(2)}) copy-start(bf16[768,512]{1,0:T(8,128)(2,1)} %constant.56.clone.dfz_ref) | copy-start | bytes 2359300
  1.4 6.7 %collective-permute-start = (f32[2,96,256]{2,1,0:T(8,128)S(1)}, f32[2,96,256]{2,1,0:T(8,128)S(1)}, u32[]{:S(2)}, u32[]{:S(2)}) collective-permute-start(f32[2,96,256]{2,1,0:T(8,128)S(1)} %face_hi.1), channel_id=1, source_target_pairs={{0,32},{32,64},{64,96},{96,0},{1,33},{33,65},{65,97},{97,1},{2,34}... | collective-permute-start | bytes 589832 | tf_op jit(solution)/shard_map/ppermute | solution.py:691
  2.0 3.9 %copy-start.4 = (bf16[96,288]{1,0:T(8,128)(2,1)S(1)}, bf16[96,288]{1,0:T(8,128)(2,1)}, u32[]{:S(2)}) copy-start(bf16[96,288]{1,0:T(8,128)(2,1)} %constant.47.clone.dy_ref) | copy-start | bytes 165892
  2.0 3.9 %copy-start.5 = (bf16[96,192]{1,0:T(8,128)(2,1)S(1)}, bf16[96,192]{1,0:T(8,128)(2,1)}, u32[]{:S(2)}) copy-start(bf16[96,192]{1,0:T(8,128)(2,1)} %constant.46.clone.avg_ref) | copy-start | bytes 110596
  2.0 7.8 %collective-permute-start.1 = (f32[2,96,256]{2,1,0:T(8,128)S(1)}, f32[2,96,256]{2,1,0:T(8,128)S(1)}, u32[]{:S(2)}, u32[]{:S(2)}) collective-permute-start(f32[2,96,256]{2,1,0:T(8,128)S(1)} %face_lo.1), channel_id=1, source_target_pairs={{0,96},{32,0},{64,32},{96,64},{1,97},{33,1},{65,33},{97,65},{2,98}... | collective-permute-start | bytes 589832 | tf_op jit(solution)/shard_map/ppermute | solution.py:691
  5.9 3.9 %copy-start.7 = (bf16[768,256]{1,0:T(8,128)(2,1)S(1)}, bf16[768,256]{1,0:T(8,128)(2,1)}, u32[]{:S(2)}) copy-start(bf16[768,256]{1,0:T(8,128)(2,1)} %constant.45.clone.dz_ref) | copy-start | bytes 1179652
  5.9 8.5 %copy-start.2 = (bf16[768,256]{1,0:T(8,128)(2,1)S(1)}, bf16[768,256]{1,0:T(8,128)(2,1)}, u32[]{:S(2)}) copy-start(bf16[768,256]{1,0:T(8,128)(2,1)} %constant.50.clone.rz_ref) | copy-start | bytes 1179652
  5.9 8.5 %copy-start.8 = (bf16[96,288]{1,0:T(8,128)(2,1)S(1)}, bf16[96,288]{1,0:T(8,128)(2,1)}, u32[]{:S(2)}) copy-start(bf16[96,288]{1,0:T(8,128)(2,1)} %constant.49.clone.ry_ref) | copy-start | bytes 165892
  10.2 6.3 %collective-permute-start.2 = (f32[96,128]{1,0:T(8,128)S(1)}, f32[96,128]{1,0:T(8,128)S(1)}, u32[]{:S(2)}, u32[]{:S(2)}) collective-permute-start(f32[96,128]{1,0:T(8,128)S(1)} %get-tuple-element.53.cols), channel_id=1, source_target_pairs={{0,1},{2,3},{4,5},{6,7},{1,0},{3,2},{5,4},{7,6},{8,9},{10,11},{12,... | collective-permute-start | bytes 147464 | tf_op jit(solution)/shard_map/ppermute | solution.py:701
  10.3 6.2 %collective-permute-start.3 = (f32[96,128]{1,0:T(8,128)S(1)}, f32[96,128]{1,0:T(8,128)S(1)}, u32[]{:S(2)}, u32[]{:S(2)}) collective-permute-start(f32[96,128]{1,0:T(8,128)S(1)} %get-tuple-element.53.cols), channel_id=1, source_target_pairs={{1,2},{3,4},{5,6},{7,0},{2,1},{4,3},{6,5},{0,7},{9,10},{11,12},{13... | collective-permute-start | bytes 147464 | tf_op jit(solution)/shard_map/ppermute | solution.py:701
  14.5 6.3 %copy-start.19 = (bf16[768,384]{1,0:T(8,128)(2,1)S(1)}, bf16[768,384]{1,0:T(8,128)(2,1)}, u32[]{:S(2)}) copy-start(bf16[768,384]{1,0:T(8,128)(2,1)} %constant.60.clone.tp_ref) | copy-start | bytes 1769476
  14.5 6.3 %copy-start.21 = (bf16[384,128]{1,0:T(8,128)(2,1)S(1)}, bf16[384,128]{1,0:T(8,128)(2,1)}, u32[]{:S(2)}) copy-start(bf16[384,128]{1,0:T(8,128)(2,1)} %constant.61.clone.zc_ref) | copy-start | bytes 294916
  14.5 6.3 %copy-start.22 = (bf16[96,288]{1,0:T(8,128)(2,1)S(1)}, bf16[96,288]{1,0:T(8,128)(2,1)}, u32[]{:S(2)}) copy-start(bf16[96,288]{1,0:T(8,128)(2,1)} %constant.48.clone.fy_ref) | copy-start | bytes 165892
  14.5 6.2 %copy-start.23 = (bf16[96,288]{1,0:T(8,128)(2,1)S(1)}, bf16[96,288]{1,0:T(8,128)(2,1)}, u32[]{:S(2)}) copy-start(bf16[96,288]{1,0:T(8,128)(2,1)} %constant.54.clone.ty_ref) | copy-start | bytes 165892
  17.4 6.2 %collective-permute-start.4 = (f32[6,16,256]{2,1,0:T(8,128)S(1)}, f32[6,16,256]{2,1,0:T(8,128)S(1)}, u32[]{:S(2)}, u32[]{:S(2)}) collective-permute-start(f32[6,16,256]{2,1,0:T(8,128)S(1)} %get-tuple-element.62.own_hi), channel_id=1, source_target_pairs={{0,8},{8,16},{16,24},{24,0},{1,9},{9,17},{17,25},{25,1},{2,10},{10... | collective-permute-start | bytes 294920 | tf_op jit(solution)/shard_map/ppermute | solution.py:691
  19.1 4.6 %collective-permute-start.5 = (f32[6,16,256]{2,1,0:T(8,128)S(1)}, f32[6,16,256]{2,1,0:T(8,128)S(1)}, u32[]{:S(2)}, u32[]{:S(2)}) collective-permute-start(f32[6,16,256]{2,1,0:T(8,128)S(1)} %get-tuple-element.61.own_lo), channel_id=1, source_target_pairs={{0,24},{8,0},{16,8},{24,16},{1,25},{9,1},{17,9},{25,17},{2,26},{10... | collective-permute-start | bytes 294920 | tf_op jit(solution)/shard_map/ppermute | solution.py:691
  24.2 5.3 %collective-permute-start.6 = (f32[96,128]{1,0:T(8,128)S(1)}, f32[96,128]{1,0:T(8,128)S(1)}, u32[]{:S(2)}, u32[]{:S(2)}) collective-permute-start(f32[96,128]{1,0:T(8,128)S(1)} %get-tuple-element.67), channel_id=1, source_target_pairs={{0,1},{2,3},{4,5},{6,7},{1,0},{3,2},{5,4},{7,6},{8,9},{10,11},{12,... | collective-permute-start | bytes 147464 | tf_op jit(solution)/shard_map/ppermute | solution.py:701
  24.3 5.3 %collective-permute-start.7 = (f32[96,128]{1,0:T(8,128)S(1)}, f32[96,128]{1,0:T(8,128)S(1)}, u32[]{:S(2)}, u32[]{:S(2)}) collective-permute-start(f32[96,128]{1,0:T(8,128)S(1)} %get-tuple-element.67), channel_id=1, source_target_pairs={{1,2},{3,4},{5,6},{7,0},{2,1},{4,3},{6,5},{0,7},{9,10},{11,12},{13... | collective-permute-start | bytes 147464 | tf_op jit(solution)/shard_map/ppermute | solution.py:701
  26.7 5.2 %copy-start.20 = (bf16[384,256]{1,0:T(8,128)(2,1)S(1)}, bf16[384,256]{1,0:T(8,128)(2,1)}, u32[]{:S(2)}) copy-start(bf16[384,256]{1,0:T(8,128)(2,1)} %constant.64.clone.add_ref) | copy-start | bytes 589828
  27.4 8.7 %collective-permute-start.8 = (f32[2,96,256]{2,1,0:T(8,128)S(1)}, f32[2,96,256]{2,1,0:T(8,128)S(1)}, u32[]{:S(2)}, u32[]{:S(2)}) collective-permute-start(f32[2,96,256]{2,1,0:T(8,128)S(1)} %get-tuple-element.69), channel_id=1, source_target_pairs={{0,32},{32,64},{64,96},{96,0},{1,33},{33,65},{65,97},{97,1},{2,34}... | collective-permute-start | bytes 589832 | tf_op jit(solution)/shard_map/ppermute | solution.py:691
  27.7 8.4 %collective-permute-start.9 = (f32[2,96,256]{2,1,0:T(8,128)S(1)}, f32[2,96,256]{2,1,0:T(8,128)S(1)}, u32[]{:S(2)}, u32[]{:S(2)}) collective-permute-start(f32[2,96,256]{2,1,0:T(8,128)S(1)} %get-tuple-element.70), channel_id=1, source_target_pairs={{0,96},{32,0},{64,32},{96,64},{1,97},{33,1},{65,33},{97,65},{2,98}... | collective-permute-start | bytes 589832 | tf_op jit(solution)/shard_map/ppermute | solution.py:691
  29.8 3.7 %collective-permute-start.10 = (f32[8,128]{1,0:T(8,128)S(1)}, f32[8,128]{1,0:T(8,128)S(1)}, u32[]{:S(2)}, u32[]{:S(2)}) collective-permute-start(f32[8,128]{1,0:T(8,128)S(1)} %get-tuple-element.71), channel_id=1, source_target_pairs={{0,32},{32,64},{64,96},{96,0},{1,33},{33,65},{65,97},{97,1},{2,34}... | collective-permute-start | bytes 12296 | tf_op jit(solution)/shard_map/ppermute | solution.py:691
  31.3 4.8 %collective-permute-start.11 = (f32[8,128]{1,0:T(8,128)S(1)}, f32[8,128]{1,0:T(8,128)S(1)}, u32[]{:S(2)}, u32[]{:S(2)}) collective-permute-start(f32[8,128]{1,0:T(8,128)S(1)} %get-tuple-element.72), channel_id=1, source_target_pairs={{0,96},{32,0},{64,32},{96,64},{1,97},{33,1},{65,33},{97,65},{2,98}... | collective-permute-start | bytes 12296 | tf_op jit(solution)/shard_map/ppermute | solution.py:691
  31.9 4.2 %copy-start.10 = (bf16[128,1024]{1,0:T(8,128)(2,1)S(1)}, bf16[128,1024]{1,0:T(8,128)(2,1)}, u32[]{:S(2)}) copy-start(bf16[128,1024]{1,0:T(8,128)(2,1)} %constant.65.clone.mat_ref) | copy-start | bytes 786436
  (12 other events, 32.0 us)

commit v5 on v4

--- a/solution.py
+++ b/solution.py
@@ -668,9 +668,9 @@
 def final_kernel(val_ref, lo_ref, hi_ref, glo_ref, ghi_ref, mat_ref, out_hbm, buf, sems):
     copies = []
     add = forwarded(glo_ref[...], ghi_ref[...], mat_ref[...])
-    for c in range(4):
-        for t in range(3):
-            rows = slice(c * 24 + t * 8, c * 24 + t * 8 + 8)
+    for c in range(6):
+        for t in range(2):
+            rows = slice(c * 16 + t * 8, c * 16 + t * 8 + 8)
             halo = [lo_ref[0, rows, :], lo_ref[1, rows, :], hi_ref[0, rows, :], hi_ref[1, rows, :]]
             halo = [v + add[rows, j * NZL : (j + 1) * NZL] for j, v in enumerate(halo)]
             for k in range(NXL):
@@ -679,7 +679,7 @@
                     if LX.halo[j][k] != 0.0:
                         val = val + float(LX.halo[j][k]) * halo[j]
                 buf[k, rows, :] = val
-        rows = slice(c * 24, c * 24 + 24)
+        rows = slice(c * 16, c * 16 + 16)
         copies.append(pltpu.make_async_copy(buf.at[:, rows, :], out_hbm.at[:, rows, :], sems.at[c]))
         copies[-1].start()
     for copy in copies:
@@ -774,7 +774,7 @@
     )
     return call(
         final_kernel, full, val, xlo, xhi, glo, ghi, z_long(), hbm_out=True,
-        scratch=[pltpu.VMEM(full, F32), pltpu.SemaphoreType.DMA((4,))], name="final",
+        scratch=[pltpu.VMEM(full, F32), pltpu.SemaphoreType.DMA((6,))], name="final",
     )
 
 

time: 37.9 us -> 37.9 us (level)
  no operation moved by 1% of the time
where the time goes in v5:
time: 37.9 us; the launch traced here: 37.8 us
  starting transfers between devices  16.3 us (43%)
  Pallas kernels  16 us (42%)
  waiting for transfers between devices  4.89 us (13%)
  between operations  0.47 us (1%)
    pallas_call x13, Pallas kernels, call(): pl.pallas_call(kernel, out_shape=shapes, in_specs=[kinds.get(i, VM) for i...  16 us
    ppermute x8, starting transfers between devices, shift(): lax.ppermute(val, axis, [(i, (i + step) % count) for i in range(count)])  9.65 us
    ppermute x4, starting transfers between devices, swap(): return lax.ppermute(val, axis, pairs + [(b, a) for a, b in pairs])  6.68 us
    ppermute x8, waiting for transfers between devices, shift(): lax.ppermute(val, axis, [(i, (i + step) % count) for i in range(count)])  4.88 us
  transfers between devices with their start and end apart: 12, of which 5 were waited for; matrix products, arithmetic and copies ran while one was open for 0% of the time, Pallas kernels for 30%

profile of v5, /device:TPU:6, one launch (start us, length us, event | category | flops | bytes accessed | tf_op | source)
XLA Modules:
  0.0 37.8 jit_solution(1916035000957452531)
XLA Ops:
  0.0 1.4 %face_hi.1 = f32[2,96,256]{2,1,0:T(8,128)S(1)} custom-call(f32[16,96,256]{2,1,0:T(8,128)} %u_ref.7), custom_call_target="tpu_custom_call" | custom-call | tf_op jit(solution)/shard_map/face_hi/pallas_call | solution.py:157
  1.4 0.5 %collective-permute-start = (f32[2,96,256]{2,1,0:T(8,128)S(1)}, f32[2,96,256]{2,1,0:T(8,128)S(1)}, u32[]{:S(2)}, u32[]{:S(2)}) collective-permute-start(f32[2,96,256]{2,1,0:T(8,128)S(1)} %face_hi.1), channel_id=1, source_target_pairs={{0,32},{32,64},{64,96},{96,0},{1,33},{33,65},{65,97},{97,1},{2,34}... | collective-permute-start | bytes 589832 | tf_op jit(solution)/shard_map/ppermute | solution.py:691
  2.0 1.7 %collective-permute-start.1 = (f32[2,96,256]{2,1,0:T(8,128)S(1)}, f32[2,96,256]{2,1,0:T(8,128)S(1)}, u32[]{:S(2)}, u32[]{:S(2)}) collective-permute-start(f32[2,96,256]{2,1,0:T(8,128)S(1)} %face_lo.1), channel_id=1, source_target_pairs={{0,96},{32,0},{64,32},{96,64},{1,97},{33,1},{65,33},{97,65},{2,98}... | collective-permute-start | bytes 589832 | tf_op jit(solution)/shard_map/ppermute | solution.py:691
  3.7 2.2 %local_z.1 = (f32[16,96,256]{2,1,0:T(8,128)S(1)}, f32[16,96,256]{2,1,0:T(8,128)S(1)}, f32[16,96,256]{2,1,0:T(8,128)S(1)}, f32[16,96,256]{2,1,0:T(8,128)S(1)}, f32[96,128]{1,0:T(8,128)S(1)}) custom-call(f32[16,96,256]{2,1,0:T(8,128)S(1)} %copy-done, bf16[512,256]{1,0:T(8,128)(2,1)S(1)} %copy-done.9, bf16[768,512]{1,0:T(8,128)(2,1)S(1)} %copy-done.18), custom_call_target="tpu_custom_call" | custom-call | flops 3000000000 | bytes 8000000 | tf_op jit(solution)/shard_map/local_z/pallas_call | solution.py:157
  5.9 2.1 %flux.1 = (f32[14,96,256]{2,1,0:T(8,128)S(1)}, bf16[14,96,256]{2,1,0:T(8,128)(2,1)S(1)}, bf16[14,96,256]{2,1,0:T(8,128)(2,1)S(1)}, bf16[14,96,256]{2,1,0:T(8,128...) custom-call(f32[16,96,256]{2,1,0:T(8,128)S(1)} %get-tuple-element.39.z1, ...), custom_call_target="tpu_custom_call" | custom-call | flops 1000000000 | bytes 12000000 | tf_op jit(solution)/shard_map/flux/pallas_call | solution.py:157
  8.1 1.6 %collective-permute-done.1.hi_ref = f32[2,96,256]{2,1,0:T(8,128)S(1)} collective-permute-done((f32[2,96,256]{2,1,0:T(8,128)S(1)}, f32[2,96,256]{2,1,0:T(8,128)S(1)}, u32[]{:S(2)}, u32[]{:S(2)}) %collective-permute-start.1) | collective-permute-done | bytes 196640 | tf_op jit(solution)/shard_map/ppermute | solution.py:691
  9.8 0.4 %face_z.1 = (f32[2,3,96,256]{3,2,1,0:T(8,128)S(1)}, f32[96,128]{1,0:T(8,128)S(1)}) custom-call(f32[2,96,256]{2,1,0:T(8,128)S(1)} %collective-permute-done.lo_ref, f32[2,96,256]{2,1,0:T(8,128)S(1)} %collective-permute-done.1.hi_ref, f32[96,128]{1,0:T(8,128)S(1)} %get-tuple-element.50.cols_ref, bf16[512,256]{1,0:T(8,128)(2,1)S(1)} %copy-done.9, ...), custom_call_target="tpu_custom_call" | custom-call | tf_op jit(solution)/shard_map/face_z/pallas_call | solution.py:157
  10.3 4.1 %collective-permute-start.3 = (f32[96,128]{1,0:T(8,128)S(1)}, f32[96,128]{1,0:T(8,128)S(1)}, u32[]{:S(2)}, u32[]{:S(2)}) collective-permute-start(f32[96,128]{1,0:T(8,128)S(1)} %get-tuple-element.53.cols), channel_id=1, source_target_pairs={{1,2},{3,4},{5,6},{7,0},{2,1},{4,3},{6,5},{0,7},{9,10},{11,12},{13... | collective-permute-start | bytes 147464 | tf_op jit(solution)/shard_map/ppermute | solution.py:701
  14.5 2.0 %residue.1 = (f32[16,96,256]{2,1,0:T(8,128)S(1)}, f32[6,16,256]{2,1,0:T(8,128)S(1)}, f32[6,16,256]{2,1,0:T(8,128)S(1)}) custom-call(f32[14,96,256]{2,1,0:T(8,128)S(1)} %get-tuple-element.42.fx, bf16[14,96,256]{2,1,0:T(8,128)(2,1)S(1)} %get-tuple-element.43.fyh, bf16[14,96,256]{2,1,0:T(8,128)(2,1)S(1)} %get-tuple-element.44.fyl, ...), custom_call_target="tpu_custom_call" | custom-call | flops 3000000000 | bytes 12000000 | tf_op jit(solution)/shard_map/residue/pallas_call | solution.py:157
  16.6 0.9 %face_y.1 = (f32[6,16,256]{2,1,0:T(8,128)S(1)}, f32[6,16,256]{2,1,0:T(8,128)S(1)}, f32[96,128]{1,0:T(8,128)S(1)}, f32[96,128]{1,0:T(8,128)S(1)}) custom-call(f32[96,128]{1,0:T(8,128)S(1)} %collective-permute-done.2.near, f32[96,128]{1,0:T(8,128)S(1)} %collective-permute-done.3.far, f32[96,128]{1,0:T(8,128)S(1)} %get-tuple-element.53.cols, ...), custom_call_target="tpu_custom_call" | custom-call | tf_op jit(solution)/shard_map/face_y/pallas_call | solution.py:157
  17.4 1.6 %collective-permute-start.4 = (f32[6,16,256]{2,1,0:T(8,128)S(1)}, f32[6,16,256]{2,1,0:T(8,128)S(1)}, u32[]{:S(2)}, u32[]{:S(2)}) collective-permute-start(f32[6,16,256]{2,1,0:T(8,128)S(1)} %get-tuple-element.62.own_hi), channel_id=1, source_target_pairs={{0,8},{8,16},{16,24},{24,0},{1,9},{9,17},{17,25},{25,1},{2,10},{10... | collective-permute-start | bytes 294920 | tf_op jit(solution)/shard_map/ppermute | solution.py:691
  19.1 1.7 %collective-permute-start.5 = (f32[6,16,256]{2,1,0:T(8,128)S(1)}, f32[6,16,256]{2,1,0:T(8,128)S(1)}, u32[]{:S(2)}, u32[]{:S(2)}) collective-permute-start(f32[6,16,256]{2,1,0:T(8,128)S(1)} %get-tuple-element.61.own_lo), channel_id=1, source_target_pairs={{0,24},{8,0},{16,8},{24,16},{1,25},{9,1},{17,9},{25,17},{2,26},{10... | collective-permute-start | bytes 294920 | tf_op jit(solution)/shard_map/ppermute | solution.py:691
  20.8 2.8 %filter.1 = (f32[16,96,256]{2,1,0:T(8,128)S(1)}, f32[16,96,256]{2,1,0:T(8,128)S(1)}, f32[96,128]{1,0:T(8,128)S(1)}, f32[96,128]{1,0:T(8,128)S(1)}) custom-call(f32[16,96,256]{2,1,0:T(8,128)S(1)} %get-tuple-element.52.r_ref, f32[96,128]{1,0:T(8,128)S(1)} %get-tuple-element.56.cval, f32[16,96,256]{2,1,0:T(8,128)S(1)} %get-tuple-element.49.z4, ...), custom_call_target="tpu_custom_call" | custom-call | flops 3000000000 | bytes 9000000 | tf_op jit(solution)/shard_map/filter/pallas_call | solution.py:157
  23.7 0.5 %face_z2.1 = (f32[96,128]{1,0:T(8,128)S(1)}, f32[8,16,256]{2,1,0:T(8,128)S(1)}) custom-call(f32[96,128]{1,0:T(8,128)S(1)} %get-tuple-element.60.cols_ref, f32[16,96,256]{2,1,0:T(8,128)S(1)} %get-tuple-element.58.after_ref.r2, f32[6,16,256]{2,1,0:T(8,128)S(1)} %get-tuple-element.61.own_lo, f32[6,16,256]{2,1,0:T(8,128)S(1)} %get-tuple-element.62.own_hi, ...), custom_call_target="tpu_custom_call" | custom-call | tf_op jit(solution)/shard_map/face_z2/pallas_call | solution.py:157
  24.3 2.4 %collective-permute-start.7 = (f32[96,128]{1,0:T(8,128)S(1)}, f32[96,128]{1,0:T(8,128)S(1)}, u32[]{:S(2)}, u32[]{:S(2)}) collective-permute-start(f32[96,128]{1,0:T(8,128)S(1)} %get-tuple-element.67), channel_id=1, source_target_pairs={{1,2},{3,4},{5,6},{7,0},{2,1},{4,3},{6,5},{0,7},{9,10},{11,12},{13... | collective-permute-start | bytes 147464 | tf_op jit(solution)/shard_map/ppermute | solution.py:701
  26.7 0.8 %spread.1 = (f32[16,96,256]{2,1,0:T(8,128)S(1)}, f32[16,96,256]{2,1,0:T(8,128)S(1)}, f32[2,96,256]{2,1,0:T(8,128)S(1)}, f32[2,96,256]{2,1,0:T(8,128)S(1)}) custom-call(f32[16,96,256]{2,1,0:T(8,128)S(1)} %get-tuple-element.58.after_ref.r2, f32[16,96,256]{2,1,0:T(8,128)S(1)} %get-tuple-element.59.vu, f32[8,16,256]{2,1,0:T(8,128)S(1)} %get-tuple-element.63.rows_ref, ...), custom_call_target="tpu_custom_call" | custom-call | flops 1000000000 | bytes 9000000 | tf_op jit(solution)/shard_map/spread/pallas_call | solution.py:157
  27.4 0.3 collective-permute-start.8
  27.7 1.8 %collective-permute-start.9 = (f32[2,96,256]{2,1,0:T(8,128)S(1)}, f32[2,96,256]{2,1,0:T(8,128)S(1)}, u32[]{:S(2)}, u32[]{:S(2)}) collective-permute-start(f32[2,96,256]{2,1,0:T(8,128)S(1)} %get-tuple-element.70), channel_id=1, source_target_pairs={{0,96},{32,0},{64,32},{96,64},{1,97},{33,1},{65,33},{97,65},{2,98}... | collective-permute-start | bytes 589832 | tf_op jit(solution)/shard_map/ppermute | solution.py:691
  29.8 1.5 %collective-permute-start.10 = (f32[8,128]{1,0:T(8,128)S(1)}, f32[8,128]{1,0:T(8,128)S(1)}, u32[]{:S(2)}, u32[]{:S(2)}) collective-permute-start(f32[8,128]{1,0:T(8,128)S(1)} %get-tuple-element.71), channel_id=1, source_target_pairs={{0,32},{32,64},{64,96},{96,0},{1,33},{33,65},{65,97},{97,1},{2,34}... | collective-permute-start | bytes 12296 | tf_op jit(solution)/shard_map/ppermute | solution.py:691
  31.3 0.6 %collective-permute-start.11 = (f32[8,128]{1,0:T(8,128)S(1)}, f32[8,128]{1,0:T(8,128)S(1)}, u32[]{:S(2)}, u32[]{:S(2)}) collective-permute-start(f32[8,128]{1,0:T(8,128)S(1)} %get-tuple-element.72), channel_id=1, source_target_pairs={{0,96},{32,0},{64,32},{96,64},{1,97},{33,1},{65,33},{97,65},{2,98}... | collective-permute-start | bytes 12296 | tf_op jit(solution)/shard_map/ppermute | solution.py:691
  31.9 1.2 %local_x.1.val_ref = f32[16,96,256]{2,1,0:T(8,128)S(1)} custom-call(f32[16,96,256]{2,1,0:T(8,128)S(1)} %get-tuple-element.65.r2, f32[16,96,256]{2,1,0:T(8,128)S(1)} %get-tuple-element.66.vu, f32[96,128]{1,0:T(8,128)S(1)} %get-tuple-element.68.hs, bf16[384,256]{1,0:T(8,128)(2,1)S(1)} %copy-done.20), custom_call_target="tpu_custom_call" | custom-call | flops 99999997952 | bytes 100000000 | tf_op jit(solution)/shard_map/local_x/pallas_call | solution.py:157
  33.0 0.4 %collective-permute-done.10.glo_ref = f32[8,128]{1,0:T(8,128)S(1)} collective-permute-done((f32[8,128]{1,0:T(8,128)S(1)}, f32[8,128]{1,0:T(8,128)S(1)}, u32[]{:S(2)}, u32[]{:S(2)}) %collective-permute-start.10) | collective-permute-done | bytes 4128 | tf_op jit(solution)/shard_map/ppermute | solution.py:691
  33.5 2.7 %collective-permute-done.11.ghi_ref = f32[8,128]{1,0:T(8,128)S(1)} collective-permute-done((f32[8,128]{1,0:T(8,128)S(1)}, f32[8,128]{1,0:T(8,128)S(1)}, u32[]{:S(2)}, u32[]{:S(2)}) %collective-permute-start.11) | collective-permute-done | bytes 4128 | tf_op jit(solution)/shard_map/ppermute | solution.py:691
  36.1 1.6 %final.1 = f32[16,96,256]{2,1,0:T(8,128)} custom-call(f32[16,96,256]{2,1,0:T(8,128)S(1)} %local_x.1.val_ref, f32[2,96,256]{2,1,0:T(8,128)S(1)} %collective-permute-done.8.lo_ref, f32[2,96,256]{2,1,0:T(8,128)S(1)} %collective-permute-done.9.hi_ref, f32[8,128]{1,0:T(8,128)S(1)} %collective-permute-done.10.glo_ref, ...), custom_call_target="tpu_custom_call" | custom-call | tf_op jit(solution)/shard_map/final/pallas_call | solution.py:157
  (61 shorter events, 0.8 us)
Async XLA Ops:
  0.0 3.7 %copy-start.18 = (bf16[768,512]{1,0:T(8,128)(2,1)S(1)}, bf16[768,512]{1,0:T(8,128)(2,1)}, u32[]{:S(2)}) copy-start(bf16[768,512]{1,0:T(8,128)(2,1)} %constant.56.clone.dfz_ref) | copy-start | bytes 2359300
  1.4 6.7 %collective-permute-start = (f32[2,96,256]{2,1,0:T(8,128)S(1)}, f32[2,96,256]{2,1,0:T(8,128)S(1)}, u32[]{:S(2)}, u32[]{:S(2)}) collective-permute-start(f32[2,96,256]{2,1,0:T(8,128)S(1)} %face_hi.1), channel_id=1, source_target_pairs={{0,32},{32,64},{64,96},{96,0},{1,33},{33,65},{65,97},{97,1},{2,34}... | collective-permute-start | bytes 589832 | tf_op jit(solution)/shard_map/ppermute | solution.py:691
  2.0 3.9 %copy-start.4 = (bf16[96,288]{1,0:T(8,128)(2,1)S(1)}, bf16[96,288]{1,0:T(8,128)(2,1)}, u32[]{:S(2)}) copy-start(bf16[96,288]{1,0:T(8,128)(2,1)} %constant.47.clone.dy_ref) | copy-start | bytes 165892
  2.0 3.9 %copy-start.5 = (bf16[96,192]{1,0:T(8,128)(2,1)S(1)}, bf16[96,192]{1,0:T(8,128)(2,1)}, u32[]{:S(2)}) copy-start(bf16[96,192]{1,0:T(8,128)(2,1)} %constant.46.clone.avg_ref) | copy-start | bytes 110596
  2.0 7.8 %collective-permute-start.1 = (f32[2,96,256]{2,1,0:T(8,128)S(1)}, f32[2,96,256]{2,1,0:T(8,128)S(1)}, u32[]{:S(2)}, u32[]{:S(2)}) collective-permute-start(f32[2,96,256]{2,1,0:T(8,128)S(1)} %face_lo.1), channel_id=1, source_target_pairs={{0,96},{32,0},{64,32},{96,64},{1,97},{33,1},{65,33},{97,65},{2,98}... | collective-permute-start | bytes 589832 | tf_op jit(solution)/shard_map/ppermute | solution.py:691
  5.9 3.9 %copy-start.7 = (bf16[768,256]{1,0:T(8,128)(2,1)S(1)}, bf16[768,256]{1,0:T(8,128)(2,1)}, u32[]{:S(2)}) copy-start(bf16[768,256]{1,0:T(8,128)(2,1)} %constant.45.clone.dz_ref) | copy-start | bytes 1179652
  5.9 8.5 %copy-start.2 = (bf16[768,256]{1,0:T(8,128)(2,1)S(1)}, bf16[768,256]{1,0:T(8,128)(2,1)}, u32[]{:S(2)}) copy-start(bf16[768,256]{1,0:T(8,128)(2,1)} %constant.50.clone.rz_ref) | copy-start | bytes 1179652
  5.9 8.5 %copy-start.8 = (bf16[96,288]{1,0:T(8,128)(2,1)S(1)}, bf16[96,288]{1,0:T(8,128)(2,1)}, u32[]{:S(2)}) copy-start(bf16[96,288]{1,0:T(8,128)(2,1)} %constant.49.clone.ry_ref) | copy-start | bytes 165892
  10.2 6.3 %collective-permute-start.2 = (f32[96,128]{1,0:T(8,128)S(1)}, f32[96,128]{1,0:T(8,128)S(1)}, u32[]{:S(2)}, u32[]{:S(2)}) collective-permute-start(f32[96,128]{1,0:T(8,128)S(1)} %get-tuple-element.53.cols), channel_id=1, source_target_pairs={{0,1},{2,3},{4,5},{6,7},{1,0},{3,2},{5,4},{7,6},{8,9},{10,11},{12,... | collective-permute-start | bytes 147464 | tf_op jit(solution)/shard_map/ppermute | solution.py:701
  10.3 6.2 %collective-permute-start.3 = (f32[96,128]{1,0:T(8,128)S(1)}, f32[96,128]{1,0:T(8,128)S(1)}, u32[]{:S(2)}, u32[]{:S(2)}) collective-permute-start(f32[96,128]{1,0:T(8,128)S(1)} %get-tuple-element.53.cols), channel_id=1, source_target_pairs={{1,2},{3,4},{5,6},{7,0},{2,1},{4,3},{6,5},{0,7},{9,10},{11,12},{13... | collective-permute-start | bytes 147464 | tf_op jit(solution)/shard_map/ppermute | solution.py:701
  14.5 6.3 %copy-start.19 = (bf16[768,384]{1,0:T(8,128)(2,1)S(1)}, bf16[768,384]{1,0:T(8,128)(2,1)}, u32[]{:S(2)}) copy-start(bf16[768,384]{1,0:T(8,128)(2,1)} %constant.60.clone.tp_ref) | copy-start | bytes 1769476
  14.5 6.3 %copy-start.21 = (bf16[384,128]{1,0:T(8,128)(2,1)S(1)}, bf16[384,128]{1,0:T(8,128)(2,1)}, u32[]{:S(2)}) copy-start(bf16[384,128]{1,0:T(8,128)(2,1)} %constant.61.clone.zc_ref) | copy-start | bytes 294916
  14.5 6.3 %copy-start.22 = (bf16[96,288]{1,0:T(8,128)(2,1)S(1)}, bf16[96,288]{1,0:T(8,128)(2,1)}, u32[]{:S(2)}) copy-start(bf16[96,288]{1,0:T(8,128)(2,1)} %constant.48.clone.fy_ref) | copy-start | bytes 165892
  14.5 6.2 %copy-start.23 = (bf16[96,288]{1,0:T(8,128)(2,1)S(1)}, bf16[96,288]{1,0:T(8,128)(2,1)}, u32[]{:S(2)}) copy-start(bf16[96,288]{1,0:T(8,128)(2,1)} %constant.54.clone.ty_ref) | copy-start | bytes 165892
  17.4 6.2 %collective-permute-start.4 = (f32[6,16,256]{2,1,0:T(8,128)S(1)}, f32[6,16,256]{2,1,0:T(8,128)S(1)}, u32[]{:S(2)}, u32[]{:S(2)}) collective-permute-start(f32[6,16,256]{2,1,0:T(8,128)S(1)} %get-tuple-element.62.own_hi), channel_id=1, source_target_pairs={{0,8},{8,16},{16,24},{24,0},{1,9},{9,17},{17,25},{25,1},{2,10},{10... | collective-permute-start | bytes 294920 | tf_op jit(solution)/shard_map/ppermute | solution.py:691
  19.1 4.6 %collective-permute-start.5 = (f32[6,16,256]{2,1,0:T(8,128)S(1)}, f32[6,16,256]{2,1,0:T(8,128)S(1)}, u32[]{:S(2)}, u32[]{:S(2)}) collective-permute-start(f32[6,16,256]{2,1,0:T(8,128)S(1)} %get-tuple-element.61.own_lo), channel_id=1, source_target_pairs={{0,24},{8,0},{16,8},{24,16},{1,25},{9,1},{17,9},{25,17},{2,26},{10... | collective-permute-start | bytes 294920 | tf_op jit(solution)/shard_map/ppermute | solution.py:691
  24.2 5.3 %collective-permute-start.6 = (f32[96,128]{1,0:T(8,128)S(1)}, f32[96,128]{1,0:T(8,128)S(1)}, u32[]{:S(2)}, u32[]{:S(2)}) collective-permute-start(f32[96,128]{1,0:T(8,128)S(1)} %get-tuple-element.67), channel_id=1, source_target_pairs={{0,1},{2,3},{4,5},{6,7},{1,0},{3,2},{5,4},{7,6},{8,9},{10,11},{12,... | collective-permute-start | bytes 147464 | tf_op jit(solution)/shard_map/ppermute | solution.py:701
  24.3 5.3 %collective-permute-start.7 = (f32[96,128]{1,0:T(8,128)S(1)}, f32[96,128]{1,0:T(8,128)S(1)}, u32[]{:S(2)}, u32[]{:S(2)}) collective-permute-start(f32[96,128]{1,0:T(8,128)S(1)} %get-tuple-element.67), channel_id=1, source_target_pairs={{1,2},{3,4},{5,6},{7,0},{2,1},{4,3},{6,5},{0,7},{9,10},{11,12},{13... | collective-permute-start | bytes 147464 | tf_op jit(solution)/shard_map/ppermute | solution.py:701
  26.7 5.2 %copy-start.20 = (bf16[384,256]{1,0:T(8,128)(2,1)S(1)}, bf16[384,256]{1,0:T(8,128)(2,1)}, u32[]{:S(2)}) copy-start(bf16[384,256]{1,0:T(8,128)(2,1)} %constant.64.clone.add_ref) | copy-start | bytes 589828
  27.4 8.7 %collective-permute-start.8 = (f32[2,96,256]{2,1,0:T(8,128)S(1)}, f32[2,96,256]{2,1,0:T(8,128)S(1)}, u32[]{:S(2)}, u32[]{:S(2)}) collective-permute-start(f32[2,96,256]{2,1,0:T(8,128)S(1)} %get-tuple-element.69), channel_id=1, source_target_pairs={{0,32},{32,64},{64,96},{96,0},{1,33},{33,65},{65,97},{97,1},{2,34}... | collective-permute-start | bytes 589832 | tf_op jit(solution)/shard_map/ppermute | solution.py:691
  27.7 8.4 %collective-permute-start.9 = (f32[2,96,256]{2,1,0:T(8,128)S(1)}, f32[2,96,256]{2,1,0:T(8,128)S(1)}, u32[]{:S(2)}, u32[]{:S(2)}) collective-permute-start(f32[2,96,256]{2,1,0:T(8,128)S(1)} %get-tuple-element.70), channel_id=1, source_target_pairs={{0,96},{32,0},{64,32},{96,64},{1,97},{33,1},{65,33},{97,65},{2,98}... | collective-permute-start | bytes 589832 | tf_op jit(solution)/shard_map/ppermute | solution.py:691
  29.8 3.7 %collective-permute-start.10 = (f32[8,128]{1,0:T(8,128)S(1)}, f32[8,128]{1,0:T(8,128)S(1)}, u32[]{:S(2)}, u32[]{:S(2)}) collective-permute-start(f32[8,128]{1,0:T(8,128)S(1)} %get-tuple-element.71), channel_id=1, source_target_pairs={{0,32},{32,64},{64,96},{96,0},{1,33},{33,65},{65,97},{97,1},{2,34}... | collective-permute-start | bytes 12296 | tf_op jit(solution)/shard_map/ppermute | solution.py:691
  31.3 4.8 %collective-permute-start.11 = (f32[8,128]{1,0:T(8,128)S(1)}, f32[8,128]{1,0:T(8,128)S(1)}, u32[]{:S(2)}, u32[]{:S(2)}) collective-permute-start(f32[8,128]{1,0:T(8,128)S(1)} %get-tuple-element.72), channel_id=1, source_target_pairs={{0,96},{32,0},{64,32},{96,64},{1,97},{33,1},{65,33},{97,65},{2,98}... | collective-permute-start | bytes 12296 | tf_op jit(solution)/shard_map/ppermute | solution.py:691
  31.9 4.2 %copy-start.10 = (bf16[128,1024]{1,0:T(8,128)(2,1)S(1)}, bf16[128,1024]{1,0:T(8,128)(2,1)}, u32[]{:S(2)}) copy-start(bf16[128,1024]{1,0:T(8,128)(2,1)} %constant.65.clone.mat_ref) | copy-start | bytes 786436
  (12 other events, 32.0 us)

commit v6 on v5

--- a/solution.py
+++ b/solution.py
@@ -177,13 +177,12 @@
 
 def face_hi_kernel(u_hbm, hi_ref, u_ref, sems):
     copies = []
-    for c in range(4):
-        rows = slice(c * 24, c * 24 + 24)
-        copies.append(pltpu.make_async_copy(u_hbm.at[8:16, rows, :], u_ref.at[:, rows, :], sems.at[c]))
+    for c in range(8):
+        copies.append(pltpu.make_async_copy(u_hbm.at[8 + c], u_ref.at[c], sems.at[c]))
         copies[-1].start()
+    for copy in copies:
+        copy.wait()
     for t in range(TILES):
-        if t % 3 == 0:
-            copies[t // 3].wait()
         rows = slice(t * 8, t * 8 + 8)
         hi_ref[0, rows, :] = 0.5 * u_ref[7, rows, :]
         hi_ref[1, rows, :] = sum(float(0.5 * D[7, j]) * u_ref[j, rows, :] for j in range(8))
@@ -720,7 +719,7 @@
 
     hi = call(
         face_hi_kernel, face_x, pltpu.with_memory_space_constraint(u, pltpu.HBM), hbm=(0,),
-        scratch=[pltpu.VMEM((8, NYL, NZL), F32), pltpu.SemaphoreType.DMA((4,))], name="face_hi",
+        scratch=[pltpu.VMEM((8, NYL, NZL), F32), pltpu.SemaphoreType.DMA((8,))], name="face_hi",
     )
     xlo = shift(hi, "gx", 1)
     lo = call(face_lo_kernel, face_x, u, name="face_lo")

time: 37.9 us -> 38 us (level)
  no operation moved by 1% of the time
where the time goes in v6:
time: 38 us; the launch traced here: 37.9 us
  starting transfers between devices  16.4 us (43%)
  Pallas kernels  16.1 us (42%)
  waiting for transfers between devices  4.86 us (13%)
  between operations  0.47 us (1%)
    pallas_call x13, Pallas kernels, call(): pl.pallas_call(kernel, out_shape=shapes, in_specs=[kinds.get(i, VM) for i...  16.1 us
    ppermute x8, starting transfers between devices, shift(): lax.ppermute(val, axis, [(i, (i + step) % count) for i in range(count)])  9.65 us
    ppermute x4, starting transfers between devices, swap(): return lax.ppermute(val, axis, pairs + [(b, a) for a, b in pairs])  6.71 us
    ppermute x8, waiting for transfers between devices, shift(): lax.ppermute(val, axis, [(i, (i + step) % count) for i in range(count)])  4.85 us
  transfers between devices with their start and end apart: 12, of which 5 were waited for; matrix products, arithmetic and copies ran while one was open for 0% of the time, Pallas kernels for 30%

profile of v6, /device:TPU:6, one launch (start us, length us, event | category | flops | bytes accessed | tf_op | source)
XLA Modules:
  0.0 37.9 jit_solution(17953096538571668641)
XLA Ops:
  0.0 1.5 %face_hi.1 = f32[2,96,256]{2,1,0:T(8,128)S(1)} custom-call(f32[16,96,256]{2,1,0:T(8,128)} %u_ref.7), custom_call_target="tpu_custom_call" | custom-call | tf_op jit(solution)/shard_map/face_hi/pallas_call | solution.py:157
  1.5 0.5 %collective-permute-start = (f32[2,96,256]{2,1,0:T(8,128)S(1)}, f32[2,96,256]{2,1,0:T(8,128)S(1)}, u32[]{:S(2)}, u32[]{:S(2)}) collective-permute-start(f32[2,96,256]{2,1,0:T(8,128)S(1)} %face_hi.1), channel_id=1, source_target_pairs={{0,32},{32,64},{64,96},{96,0},{1,33},{33,65},{65,97},{97,1},{2,34}... | collective-permute-start | bytes 589832 | tf_op jit(solution)/shard_map/ppermute | solution.py:690
  2.1 1.7 %collective-permute-start.1 = (f32[2,96,256]{2,1,0:T(8,128)S(1)}, f32[2,96,256]{2,1,0:T(8,128)S(1)}, u32[]{:S(2)}, u32[]{:S(2)}) collective-permute-start(f32[2,96,256]{2,1,0:T(8,128)S(1)} %face_lo.1), channel_id=1, source_target_pairs={{0,96},{32,0},{64,32},{96,64},{1,97},{33,1},{65,33},{97,65},{2,98}... | collective-permute-start | bytes 589832 | tf_op jit(solution)/shard_map/ppermute | solution.py:690
  3.8 2.2 %local_z.1 = (f32[16,96,256]{2,1,0:T(8,128)S(1)}, f32[16,96,256]{2,1,0:T(8,128)S(1)}, f32[16,96,256]{2,1,0:T(8,128)S(1)}, f32[16,96,256]{2,1,0:T(8,128)S(1)}, f32[96,128]{1,0:T(8,128)S(1)}) custom-call(f32[16,96,256]{2,1,0:T(8,128)S(1)} %copy-done, bf16[512,256]{1,0:T(8,128)(2,1)S(1)} %copy-done.9, bf16[768,512]{1,0:T(8,128)(2,1)S(1)} %copy-done.18), custom_call_target="tpu_custom_call" | custom-call | flops 3000000000 | bytes 8000000 | tf_op jit(solution)/shard_map/local_z/pallas_call | solution.py:157
  6.0 2.1 %flux.1 = (f32[14,96,256]{2,1,0:T(8,128)S(1)}, bf16[14,96,256]{2,1,0:T(8,128)(2,1)S(1)}, bf16[14,96,256]{2,1,0:T(8,128)(2,1)S(1)}, bf16[14,96,256]{2,1,0:T(8,128...) custom-call(f32[16,96,256]{2,1,0:T(8,128)S(1)} %get-tuple-element.39.z1, ...), custom_call_target="tpu_custom_call" | custom-call | flops 1000000000 | bytes 12000000 | tf_op jit(solution)/shard_map/flux/pallas_call | solution.py:157
  8.2 1.5 %collective-permute-done.1.hi_ref = f32[2,96,256]{2,1,0:T(8,128)S(1)} collective-permute-done((f32[2,96,256]{2,1,0:T(8,128)S(1)}, f32[2,96,256]{2,1,0:T(8,128)S(1)}, u32[]{:S(2)}, u32[]{:S(2)}) %collective-permute-start.1) | collective-permute-done | bytes 196640 | tf_op jit(solution)/shard_map/ppermute | solution.py:690
  9.8 0.4 %face_z.1 = (f32[2,3,96,256]{3,2,1,0:T(8,128)S(1)}, f32[96,128]{1,0:T(8,128)S(1)}) custom-call(f32[2,96,256]{2,1,0:T(8,128)S(1)} %collective-permute-done.lo_ref, f32[2,96,256]{2,1,0:T(8,128)S(1)} %collective-permute-done.1.hi_ref, f32[96,128]{1,0:T(8,128)S(1)} %get-tuple-element.50.cols_ref, bf16[512,256]{1,0:T(8,128)(2,1)S(1)} %copy-done.9, ...), custom_call_target="tpu_custom_call" | custom-call | tf_op jit(solution)/shard_map/face_z/pallas_call | solution.py:157
  10.3 4.2 %collective-permute-start.3 = (f32[96,128]{1,0:T(8,128)S(1)}, f32[96,128]{1,0:T(8,128)S(1)}, u32[]{:S(2)}, u32[]{:S(2)}) collective-permute-start(f32[96,128]{1,0:T(8,128)S(1)} %get-tuple-element.53.cols), channel_id=1, source_target_pairs={{1,2},{3,4},{5,6},{7,0},{2,1},{4,3},{6,5},{0,7},{9,10},{11,12},{13... | collective-permute-start | bytes 147464 | tf_op jit(solution)/shard_map/ppermute | solution.py:700
  14.5 2.0 %residue.1 = (f32[16,96,256]{2,1,0:T(8,128)S(1)}, f32[6,16,256]{2,1,0:T(8,128)S(1)}, f32[6,16,256]{2,1,0:T(8,128)S(1)}) custom-call(f32[14,96,256]{2,1,0:T(8,128)S(1)} %get-tuple-element.42.fx, bf16[14,96,256]{2,1,0:T(8,128)(2,1)S(1)} %get-tuple-element.43.fyh, bf16[14,96,256]{2,1,0:T(8,128)(2,1)S(1)} %get-tuple-element.44.fyl, ...), custom_call_target="tpu_custom_call" | custom-call | flops 3000000000 | bytes 12000000 | tf_op jit(solution)/shard_map/residue/pallas_call | solution.py:157
  16.6 0.9 %face_y.1 = (f32[6,16,256]{2,1,0:T(8,128)S(1)}, f32[6,16,256]{2,1,0:T(8,128)S(1)}, f32[96,128]{1,0:T(8,128)S(1)}, f32[96,128]{1,0:T(8,128)S(1)}) custom-call(f32[96,128]{1,0:T(8,128)S(1)} %collective-permute-done.2.near, f32[96,128]{1,0:T(8,128)S(1)} %collective-permute-done.3.far, f32[96,128]{1,0:T(8,128)S(1)} %get-tuple-element.53.cols, ...), custom_call_target="tpu_custom_call" | custom-call | tf_op jit(solution)/shard_map/face_y/pallas_call | solution.py:157
  17.4 1.6 %collective-permute-start.4 = (f32[6,16,256]{2,1,0:T(8,128)S(1)}, f32[6,16,256]{2,1,0:T(8,128)S(1)}, u32[]{:S(2)}, u32[]{:S(2)}) collective-permute-start(f32[6,16,256]{2,1,0:T(8,128)S(1)} %get-tuple-element.62.own_hi), channel_id=1, source_target_pairs={{0,8},{8,16},{16,24},{24,0},{1,9},{9,17},{17,25},{25,1},{2,10},{10... | collective-permute-start | bytes 294920 | tf_op jit(solution)/shard_map/ppermute | solution.py:690
  19.1 1.7 %collective-permute-start.5 = (f32[6,16,256]{2,1,0:T(8,128)S(1)}, f32[6,16,256]{2,1,0:T(8,128)S(1)}, u32[]{:S(2)}, u32[]{:S(2)}) collective-permute-start(f32[6,16,256]{2,1,0:T(8,128)S(1)} %get-tuple-element.61.own_lo), channel_id=1, source_target_pairs={{0,24},{8,0},{16,8},{24,16},{1,25},{9,1},{17,9},{25,17},{2,26},{10... | collective-permute-start | bytes 294920 | tf_op jit(solution)/shard_map/ppermute | solution.py:690
  20.8 2.8 %filter.1 = (f32[16,96,256]{2,1,0:T(8,128)S(1)}, f32[16,96,256]{2,1,0:T(8,128)S(1)}, f32[96,128]{1,0:T(8,128)S(1)}, f32[96,128]{1,0:T(8,128)S(1)}) custom-call(f32[16,96,256]{2,1,0:T(8,128)S(1)} %get-tuple-element.52.r_ref, f32[96,128]{1,0:T(8,128)S(1)} %get-tuple-element.56.cval, f32[16,96,256]{2,1,0:T(8,128)S(1)} %get-tuple-element.49.z4, ...), custom_call_target="tpu_custom_call" | custom-call | flops 3000000000 | bytes 9000000 | tf_op jit(solution)/shard_map/filter/pallas_call | solution.py:157
  23.7 0.5 %face_z2.1 = (f32[96,128]{1,0:T(8,128)S(1)}, f32[8,16,256]{2,1,0:T(8,128)S(1)}) custom-call(f32[96,128]{1,0:T(8,128)S(1)} %get-tuple-element.60.cols_ref, f32[16,96,256]{2,1,0:T(8,128)S(1)} %get-tuple-element.58.after_ref.r2, f32[6,16,256]{2,1,0:T(8,128)S(1)} %get-tuple-element.61.own_lo, f32[6,16,256]{2,1,0:T(8,128)S(1)} %get-tuple-element.62.own_hi, ...), custom_call_target="tpu_custom_call" | custom-call | tf_op jit(solution)/shard_map/face_z2/pallas_call | solution.py:157
  24.3 2.4 %collective-permute-start.7 = (f32[96,128]{1,0:T(8,128)S(1)}, f32[96,128]{1,0:T(8,128)S(1)}, u32[]{:S(2)}, u32[]{:S(2)}) collective-permute-start(f32[96,128]{1,0:T(8,128)S(1)} %get-tuple-element.67), channel_id=1, source_target_pairs={{1,2},{3,4},{5,6},{7,0},{2,1},{4,3},{6,5},{0,7},{9,10},{11,12},{13... | collective-permute-start | bytes 147464 | tf_op jit(solution)/shard_map/ppermute | solution.py:700
  26.7 0.8 %spread.1 = (f32[16,96,256]{2,1,0:T(8,128)S(1)}, f32[16,96,256]{2,1,0:T(8,128)S(1)}, f32[2,96,256]{2,1,0:T(8,128)S(1)}, f32[2,96,256]{2,1,0:T(8,128)S(1)}) custom-call(f32[16,96,256]{2,1,0:T(8,128)S(1)} %get-tuple-element.58.after_ref.r2, f32[16,96,256]{2,1,0:T(8,128)S(1)} %get-tuple-element.59.vu, f32[8,16,256]{2,1,0:T(8,128)S(1)} %get-tuple-element.63.rows_ref, ...), custom_call_target="tpu_custom_call" | custom-call | flops 1000000000 | bytes 9000000 | tf_op jit(solution)/shard_map/spread/pallas_call | solution.py:157
  27.4 0.4 collective-permute-start.8
  27.8 1.7 %collective-permute-start.9 = (f32[2,96,256]{2,1,0:T(8,128)S(1)}, f32[2,96,256]{2,1,0:T(8,128)S(1)}, u32[]{:S(2)}, u32[]{:S(2)}) collective-permute-start(f32[2,96,256]{2,1,0:T(8,128)S(1)} %get-tuple-element.70), channel_id=1, source_target_pairs={{0,96},{32,0},{64,32},{96,64},{1,97},{33,1},{65,33},{97,65},{2,98}... | collective-permute-start | bytes 589832 | tf_op jit(solution)/shard_map/ppermute | solution.py:690
  29.8 1.6 %collective-permute-start.10 = (f32[8,128]{1,0:T(8,128)S(1)}, f32[8,128]{1,0:T(8,128)S(1)}, u32[]{:S(2)}, u32[]{:S(2)}) collective-permute-start(f32[8,128]{1,0:T(8,128)S(1)} %get-tuple-element.71), channel_id=1, source_target_pairs={{0,32},{32,64},{64,96},{96,0},{1,33},{33,65},{65,97},{97,1},{2,34}... | collective-permute-start | bytes 12296 | tf_op jit(solution)/shard_map/ppermute | solution.py:690
  31.4 0.5 %collective-permute-start.11 = (f32[8,128]{1,0:T(8,128)S(1)}, f32[8,128]{1,0:T(8,128)S(1)}, u32[]{:S(2)}, u32[]{:S(2)}) collective-permute-start(f32[8,128]{1,0:T(8,128)S(1)} %get-tuple-element.72), channel_id=1, source_target_pairs={{0,96},{32,0},{64,32},{96,64},{1,97},{33,1},{65,33},{97,65},{2,98}... | collective-permute-start | bytes 12296 | tf_op jit(solution)/shard_map/ppermute | solution.py:690
  31.9 1.2 %local_x.1.val_ref = f32[16,96,256]{2,1,0:T(8,128)S(1)} custom-call(f32[16,96,256]{2,1,0:T(8,128)S(1)} %get-tuple-element.65.r2, f32[16,96,256]{2,1,0:T(8,128)S(1)} %get-tuple-element.66.vu, f32[96,128]{1,0:T(8,128)S(1)} %get-tuple-element.68.hs, bf16[384,256]{1,0:T(8,128)(2,1)S(1)} %copy-done.20), custom_call_target="tpu_custom_call" | custom-call | flops 99999997952 | bytes 100000000 | tf_op jit(solution)/shard_map/local_x/pallas_call | solution.py:157
  33.1 0.4 %collective-permute-done.10.glo_ref = f32[8,128]{1,0:T(8,128)S(1)} collective-permute-done((f32[8,128]{1,0:T(8,128)S(1)}, f32[8,128]{1,0:T(8,128)S(1)}, u32[]{:S(2)}, u32[]{:S(2)}) %collective-permute-start.10) | collective-permute-done | bytes 4128 | tf_op jit(solution)/shard_map/ppermute | solution.py:690
  33.5 2.7 %collective-permute-done.11.ghi_ref = f32[8,128]{1,0:T(8,128)S(1)} collective-permute-done((f32[8,128]{1,0:T(8,128)S(1)}, f32[8,128]{1,0:T(8,128)S(1)}, u32[]{:S(2)}, u32[]{:S(2)}) %collective-permute-start.11) | collective-permute-done | bytes 4128 | tf_op jit(solution)/shard_map/ppermute | solution.py:690
  36.2 1.6 %final.1 = f32[16,96,256]{2,1,0:T(8,128)} custom-call(f32[16,96,256]{2,1,0:T(8,128)S(1)} %local_x.1.val_ref, f32[2,96,256]{2,1,0:T(8,128)S(1)} %collective-permute-done.8.lo_ref, f32[2,96,256]{2,1,0:T(8,128)S(1)} %collective-permute-done.9.hi_ref, f32[8,128]{1,0:T(8,128)S(1)} %collective-permute-done.10.glo_ref, ...), custom_call_target="tpu_custom_call" | custom-call | tf_op jit(solution)/shard_map/final/pallas_call | solution.py:157
  (61 shorter events, 0.8 us)
Async XLA Ops:
  0.0 3.8 %copy-start.18 = (bf16[768,512]{1,0:T(8,128)(2,1)S(1)}, bf16[768,512]{1,0:T(8,128)(2,1)}, u32[]{:S(2)}) copy-start(bf16[768,512]{1,0:T(8,128)(2,1)} %constant.56.clone.dfz_ref) | copy-start | bytes 2359300
  1.5 6.7 %collective-permute-start = (f32[2,96,256]{2,1,0:T(8,128)S(1)}, f32[2,96,256]{2,1,0:T(8,128)S(1)}, u32[]{:S(2)}, u32[]{:S(2)}) collective-permute-start(f32[2,96,256]{2,1,0:T(8,128)S(1)} %face_hi.1), channel_id=1, source_target_pairs={{0,32},{32,64},{64,96},{96,0},{1,33},{33,65},{65,97},{97,1},{2,34}... | collective-permute-start | bytes 589832 | tf_op jit(solution)/shard_map/ppermute | solution.py:690
  2.0 3.9 %copy-start.4 = (bf16[96,288]{1,0:T(8,128)(2,1)S(1)}, bf16[96,288]{1,0:T(8,128)(2,1)}, u32[]{:S(2)}) copy-start(bf16[96,288]{1,0:T(8,128)(2,1)} %constant.47.clone.dy_ref) | copy-start | bytes 165892
  2.0 3.9 %copy-start.5 = (bf16[96,192]{1,0:T(8,128)(2,1)S(1)}, bf16[96,192]{1,0:T(8,128)(2,1)}, u32[]{:S(2)}) copy-start(bf16[96,192]{1,0:T(8,128)(2,1)} %constant.46.clone.avg_ref) | copy-start | bytes 110596
  2.1 7.7 %collective-permute-start.1 = (f32[2,96,256]{2,1,0:T(8,128)S(1)}, f32[2,96,256]{2,1,0:T(8,128)S(1)}, u32[]{:S(2)}, u32[]{:S(2)}) collective-permute-start(f32[2,96,256]{2,1,0:T(8,128)S(1)} %face_lo.1), channel_id=1, source_target_pairs={{0,96},{32,0},{64,32},{96,64},{1,97},{33,1},{65,33},{97,65},{2,98}... | collective-permute-start | bytes 589832 | tf_op jit(solution)/shard_map/ppermute | solution.py:690
  6.0 3.8 %copy-start.7 = (bf16[768,256]{1,0:T(8,128)(2,1)S(1)}, bf16[768,256]{1,0:T(8,128)(2,1)}, u32[]{:S(2)}) copy-start(bf16[768,256]{1,0:T(8,128)(2,1)} %constant.45.clone.dz_ref) | copy-start | bytes 1179652
  6.0 8.5 %copy-start.2 = (bf16[768,256]{1,0:T(8,128)(2,1)S(1)}, bf16[768,256]{1,0:T(8,128)(2,1)}, u32[]{:S(2)}) copy-start(bf16[768,256]{1,0:T(8,128)(2,1)} %constant.50.clone.rz_ref) | copy-start | bytes 1179652
  6.0 8.5 %copy-start.8 = (bf16[96,288]{1,0:T(8,128)(2,1)S(1)}, bf16[96,288]{1,0:T(8,128)(2,1)}, u32[]{:S(2)}) copy-start(bf16[96,288]{1,0:T(8,128)(2,1)} %constant.49.clone.ry_ref) | copy-start | bytes 165892
  10.2 6.3 %collective-permute-start.2 = (f32[96,128]{1,0:T(8,128)S(1)}, f32[96,128]{1,0:T(8,128)S(1)}, u32[]{:S(2)}, u32[]{:S(2)}) collective-permute-start(f32[96,128]{1,0:T(8,128)S(1)} %get-tuple-element.53.cols), channel_id=1, source_target_pairs={{0,1},{2,3},{4,5},{6,7},{1,0},{3,2},{5,4},{7,6},{8,9},{10,11},{12,... | collective-permute-start | bytes 147464 | tf_op jit(solution)/shard_map/ppermute | solution.py:700
  10.3 6.3 %collective-permute-start.3 = (f32[96,128]{1,0:T(8,128)S(1)}, f32[96,128]{1,0:T(8,128)S(1)}, u32[]{:S(2)}, u32[]{:S(2)}) collective-permute-start(f32[96,128]{1,0:T(8,128)S(1)} %get-tuple-element.53.cols), channel_id=1, source_target_pairs={{1,2},{3,4},{5,6},{7,0},{2,1},{4,3},{6,5},{0,7},{9,10},{11,12},{13... | collective-permute-start | bytes 147464 | tf_op jit(solution)/shard_map/ppermute | solution.py:700
  14.5 6.3 %copy-start.19 = (bf16[768,384]{1,0:T(8,128)(2,1)S(1)}, bf16[768,384]{1,0:T(8,128)(2,1)}, u32[]{:S(2)}) copy-start(bf16[768,384]{1,0:T(8,128)(2,1)} %constant.60.clone.tp_ref) | copy-start | bytes 1769476
  14.5 6.3 %copy-start.21 = (bf16[384,128]{1,0:T(8,128)(2,1)S(1)}, bf16[384,128]{1,0:T(8,128)(2,1)}, u32[]{:S(2)}) copy-start(bf16[384,128]{1,0:T(8,128)(2,1)} %constant.61.clone.zc_ref) | copy-start | bytes 294916
  14.5 6.3 %copy-start.22 = (bf16[96,288]{1,0:T(8,128)(2,1)S(1)}, bf16[96,288]{1,0:T(8,128)(2,1)}, u32[]{:S(2)}) copy-start(bf16[96,288]{1,0:T(8,128)(2,1)} %constant.48.clone.fy_ref) | copy-start | bytes 165892
  14.5 6.2 %copy-start.23 = (bf16[96,288]{1,0:T(8,128)(2,1)S(1)}, bf16[96,288]{1,0:T(8,128)(2,1)}, u32[]{:S(2)}) copy-start(bf16[96,288]{1,0:T(8,128)(2,1)} %constant.54.clone.ty_ref) | copy-start | bytes 165892
  17.4 6.2 %collective-permute-start.4 = (f32[6,16,256]{2,1,0:T(8,128)S(1)}, f32[6,16,256]{2,1,0:T(8,128)S(1)}, u32[]{:S(2)}, u32[]{:S(2)}) collective-permute-start(f32[6,16,256]{2,1,0:T(8,128)S(1)} %get-tuple-element.62.own_hi), channel_id=1, source_target_pairs={{0,8},{8,16},{16,24},{24,0},{1,9},{9,17},{17,25},{25,1},{2,10},{10... | collective-permute-start | bytes 294920 | tf_op jit(solution)/shard_map/ppermute | solution.py:690
  19.1 4.6 %collective-permute-start.5 = (f32[6,16,256]{2,1,0:T(8,128)S(1)}, f32[6,16,256]{2,1,0:T(8,128)S(1)}, u32[]{:S(2)}, u32[]{:S(2)}) collective-permute-start(f32[6,16,256]{2,1,0:T(8,128)S(1)} %get-tuple-element.61.own_lo), channel_id=1, source_target_pairs={{0,24},{8,0},{16,8},{24,16},{1,25},{9,1},{17,9},{25,17},{2,26},{10... | collective-permute-start | bytes 294920 | tf_op jit(solution)/shard_map/ppermute | solution.py:690
  24.2 5.3 %collective-permute-start.6 = (f32[96,128]{1,0:T(8,128)S(1)}, f32[96,128]{1,0:T(8,128)S(1)}, u32[]{:S(2)}, u32[]{:S(2)}) collective-permute-start(f32[96,128]{1,0:T(8,128)S(1)} %get-tuple-element.67), channel_id=1, source_target_pairs={{0,1},{2,3},{4,5},{6,7},{1,0},{3,2},{5,4},{7,6},{8,9},{10,11},{12,... | collective-permute-start | bytes 147464 | tf_op jit(solution)/shard_map/ppermute | solution.py:700
  24.3 5.3 %collective-permute-start.7 = (f32[96,128]{1,0:T(8,128)S(1)}, f32[96,128]{1,0:T(8,128)S(1)}, u32[]{:S(2)}, u32[]{:S(2)}) collective-permute-start(f32[96,128]{1,0:T(8,128)S(1)} %get-tuple-element.67), channel_id=1, source_target_pairs={{1,2},{3,4},{5,6},{7,0},{2,1},{4,3},{6,5},{0,7},{9,10},{11,12},{13... | collective-permute-start | bytes 147464 | tf_op jit(solution)/shard_map/ppermute | solution.py:700
  26.7 5.2 %copy-start.20 = (bf16[384,256]{1,0:T(8,128)(2,1)S(1)}, bf16[384,256]{1,0:T(8,128)(2,1)}, u32[]{:S(2)}) copy-start(bf16[384,256]{1,0:T(8,128)(2,1)} %constant.64.clone.add_ref) | copy-start | bytes 589828
  27.4 8.7 %collective-permute-start.8 = (f32[2,96,256]{2,1,0:T(8,128)S(1)}, f32[2,96,256]{2,1,0:T(8,128)S(1)}, u32[]{:S(2)}, u32[]{:S(2)}) collective-permute-start(f32[2,96,256]{2,1,0:T(8,128)S(1)} %get-tuple-element.69), channel_id=1, source_target_pairs={{0,32},{32,64},{64,96},{96,0},{1,33},{33,65},{65,97},{97,1},{2,34}... | collective-permute-start | bytes 589832 | tf_op jit(solution)/shard_map/ppermute | solution.py:690
  27.8 8.4 %collective-permute-start.9 = (f32[2,96,256]{2,1,0:T(8,128)S(1)}, f32[2,96,256]{2,1,0:T(8,128)S(1)}, u32[]{:S(2)}, u32[]{:S(2)}) collective-permute-start(f32[2,96,256]{2,1,0:T(8,128)S(1)} %get-tuple-element.70), channel_id=1, source_target_pairs={{0,96},{32,0},{64,32},{96,64},{1,97},{33,1},{65,33},{97,65},{2,98}... | collective-permute-start | bytes 589832 | tf_op jit(solution)/shard_map/ppermute | solution.py:690
  29.8 3.7 %collective-permute-start.10 = (f32[8,128]{1,0:T(8,128)S(1)}, f32[8,128]{1,0:T(8,128)S(1)}, u32[]{:S(2)}, u32[]{:S(2)}) collective-permute-start(f32[8,128]{1,0:T(8,128)S(1)} %get-tuple-element.71), channel_id=1, source_target_pairs={{0,32},{32,64},{64,96},{96,0},{1,33},{33,65},{65,97},{97,1},{2,34}... | collective-permute-start | bytes 12296 | tf_op jit(solution)/shard_map/ppermute | solution.py:690
  31.4 4.8 %collective-permute-start.11 = (f32[8,128]{1,0:T(8,128)S(1)}, f32[8,128]{1,0:T(8,128)S(1)}, u32[]{:S(2)}, u32[]{:S(2)}) collective-permute-start(f32[8,128]{1,0:T(8,128)S(1)} %get-tuple-element.72), channel_id=1, source_target_pairs={{0,96},{32,0},{64,32},{96,64},{1,97},{33,1},{65,33},{97,65},{2,98}... | collective-permute-start | bytes 12296 | tf_op jit(solution)/shard_map/ppermute | solution.py:690
  31.9 4.3 %copy-start.10 = (bf16[128,1024]{1,0:T(8,128)(2,1)S(1)}, bf16[128,1024]{1,0:T(8,128)(2,1)}, u32[]{:S(2)}) copy-start(bf16[128,1024]{1,0:T(8,128)(2,1)} %constant.65.clone.mat_ref) | copy-start | bytes 786436
  (12 other events, 32.1 us)
